TPU v7x, 512 devices: a whole 4x4x16 slice. The times are simulated.
512 devices in a mesh: rve: 32 (over z, core), slab: 16 (over y, x).
Axes of the slice: x: 4, y: 4, z: 16, core: 2. Of those that a mesh axis runs over, the one named last changes fastest.
Arguments:
- phase_ids: int32 [64, 4096], P('slab'), may hold values from 0 to 1, as said below
- yield_flags: int32 [32, 3, 64, 4096], P('rve', None, 'slab'), may hold values from 0 to 1
- plastic_strain: float32 [32, 6, 64, 4096], P('rve', None, 'slab'), may hold values from -0.03 to 0.03
- displacements: float32 [20, 3], replicated, may hold values from -0.06 to 0.06
- connectivity: int32 [4, 8], replicated, may hold values from 0 to 19, as said below
Outputs:
- gauss_stress: float32 [32, 6], P('rve')
- gauss_tangent: float32 [32, 6, 6], P('rve')
- nodal_forces: float32 [20, 3], replicated
- stiffness: float32 [60, 60], replicated
Inputs may be any that keep to these rules, and one draw needn't show every extreme that they name: `phase_ids`: 0 marks ferrite, 1 martensite. `connectivity`: element e is the cube [e, e+1] x [0,1] x [0,1]; entry c of its row is the id of its corner (e + c % 2, c // 2 % 2, c // 4); each point of the mesh has one id, distinct points distinct ids.
All inputs are finite; a program needn't handle non-finite values.
Results may differ from a plain program's by a relative error of at most 0.0001.
Values sent between devices are 32-bit elements; how exact they have to be, the bound alone decides.
No kernel may reach another device: no remote copies, remote signals or barrier semaphores. Data moves between devices by JAX's collectives and lax.ppermute only.
A program may use at most 64 MiB of HBM per device.

v0:
```python
import functools
import math

import jax
import jax.numpy as jnp
import ml_dtypes
import numpy as np
from jax import lax
from jax.experimental import pallas as pl
from jax.experimental.pallas import tpu as pltpu
from jax.sharding import PartitionSpec as P

GRID = 64
ITERS = 2
SLABS = 16
PLANES = GRID // SLABS
KEPT = GRID // 2

SHEAR_MODULUS = 80.0
BULK_MODULUS = 160.0
REFERENCE_SHEAR = 80.0
REFERENCE_LAME = 160.0 - 160.0 / 3.0
TANGENT_UNIT = 100.0
QUADRATURE_WEIGHT = 0.125
PAIR_WEIGHTS = (1.0, 1.0, 1.0, 2.0, 2.0, 2.0)
TENSOR_PAIRS = ((0, 0), (1, 1), (2, 2), (1, 2), (0, 2), (0, 1))
TENSOR_ROWS = ((0, 5, 4), (5, 1, 3), (4, 3, 2))
VOXELS = float(GRID**3)
GAUSS_LOW = 0.5 - 0.5 / math.sqrt(3.0)
GAUSS_HIGH = 0.5 + 0.5 / math.sqrt(3.0)
OUTER_AT = 8


def halves(table):
    high = table.astype(np.float32).astype(ml_dtypes.bfloat16)
    low = (table - high.astype(np.float64)).astype(np.float32).astype(ml_dtypes.bfloat16)
    return high, low


def depth_tables():
    z = np.arange(GRID)
    k = np.arange(KEPT)
    theta = 2.0 * np.pi * np.outer(z, k) / GRID
    forward = np.stack([np.cos(theta), -np.sin(theta)], axis=0)
    weight = np.where(k == 0, 1.0, 2.0) / VOXELS
    inverse = forward * weight[None, None, :]
    planes = np.eye(PLANES)
    pair = np.eye(2)
    there = np.einsum("lL,rR,pzk->lrzRpLk", planes, pair, forward)
    back = np.einsum("lL,rR,pzk->RpLklrz", planes, pair, inverse)
    return there.reshape(512, 512), back.reshape(512, 512)


def row_tables():
    y = 2 * np.arange(32)[None, :] + np.arange(2)[:, None]
    ky = 4 * np.arange(16)[:, None] + np.arange(4)[None, :]
    theta = 2.0 * np.pi * np.einsum("de,rm->derm", ky, y) / GRID
    c, s = np.cos(theta), np.sin(theta)
    there = np.zeros((16, 2, 4, 2, 2, 32))
    there[:, 0, :, :, 0, :] = c
    there[:, 0, :, :, 1, :] = s
    there[:, 1, :, :, 0, :] = -s
    there[:, 1, :, :, 1, :] = c
    back = np.zeros((2, 2, 32, 16, 2, 4))
    ct, st = np.einsum("derm->rmde", c), np.einsum("derm->rmde", s)
    back[:, 0, :, :, 0, :] = ct
    back[:, 0, :, :, 1, :] = -st
    back[:, 1, :, :, 0, :] = st
    back[:, 1, :, :, 1, :] = ct
    return there.reshape(128, 128), back.reshape(128, 128)


def column_tables():
    d = np.arange(16)
    theta = 2.0 * np.pi * np.outer(d, d) / 16.0
    c, s = np.cos(theta), np.sin(theta)
    same = np.eye(4)
    there = np.zeros((2, 16, 4, 16, 2, 4))
    there[0, :, :, :, 0, :] = np.einsum("bd,ef->bedf", c, same)
    there[0, :, :, :, 1, :] = np.einsum("bd,ef->bedf", s, same)
    there[1, :, :, :, 0, :] = np.einsum("bd,ef->bedf", -s, same)
    there[1, :, :, :, 1, :] = np.einsum("bd,ef->bedf", c, same)
    there = there.reshape(128, 128)
    phi = 2.0 * np.pi * np.outer(np.arange(16), np.arange(4)) / GRID
    twist = np.stack([np.cos(phi), np.sin(phi)])[:, :, None, :, None]
    twist = np.broadcast_to(twist, (2, 16, 4, 4, KEPT)).reshape(2, 64, 128)
    quarter = 2.0 * np.pi * np.outer(np.arange(4), np.arange(4)) / 4.0
    cq, sq = np.rint(np.cos(quarter)), np.rint(np.sin(quarter))
    kept = np.eye(KEPT)
    four = np.zeros((2, 4, KEPT, 2, 4, KEPT))
    four[0, :, :, 0] = np.einsum("la,kK->lkaK", cq, kept)
    four[1, :, :, 0] = np.einsum("la,kK->lkaK", sq, kept)
    four[0, :, :, 1] = np.einsum("la,kK->lkaK", -sq, kept)
    four[1, :, :, 1] = np.einsum("la,kK->lkaK", cq, kept)
    four = four.reshape(256, 256)
    return there, there.T.copy(), twist.astype(np.float32), four, four.T.copy()


def split(x):
    high = x.astype(jnp.bfloat16)
    low = (x - high.astype(jnp.float32)).astype(jnp.bfloat16)
    return high, low


def mm(a, b):
    return jnp.dot(a, b, preferred_element_type=jnp.float32)


def data_by_table(high, low, table_high, table_low):
    return mm(high, table_high) + (mm(low, table_high) + mm(high, table_low))


def table_by_data(table_high, table_low, high, low):
    return mm(table_high, high) + (mm(table_low, high) + mm(table_high, low))


def slopes_of(bits, low, high):
    at = [jnp.where(bit == 1, high, low) for bit in bits]
    far = [jnp.where(bit == 1, low, high) for bit in bits]

    def slope(corner, axis):
        value = None
        for other in range(3):
            if other != axis:
                factor = at[other] if corner >> other & 1 else far[other]
                value = factor if value is None else value * factor
        return value if corner >> axis & 1 else -value

    return slope


def macro_strain(point, conn_ref, disp_ref):
    low, high = jnp.float32(GAUSS_LOW), jnp.float32(GAUSS_HIGH)
    bits = [lax.bitwise_and(lax.shift_right_logical(point, d), 1) for d in range(3)]
    slope = slopes_of(bits, low, high)
    element = lax.shift_right_logical(point, 3)
    grad = [[jnp.float32(0.0)] * 3 for _ in range(3)]
    for corner in range(8):
        node = conn_ref[element, corner]
        for k in range(3):
            u = disp_ref[node, k]
            for d in range(3):
                grad[k][d] = grad[k][d] + slope(corner, d) * u
    strain = []
    for i, j in TENSOR_PAIRS:
        strain.append(grad[i][i] if i == j else 0.5 * (grad[i][j] + grad[j][i]))
    return strain


def material(elastic, phases, flags):
    hard = phases == 1
    limit = jnp.where(hard, 1.2, 0.3)
    ratio = jnp.where(
        hard,
        3.0 * SHEAR_MODULUS / (3.0 * SHEAR_MODULUS + 10.0),
        3.0 * SHEAR_MODULUS / (3.0 * SHEAR_MODULUS + 2.0),
    )
    active = flags.astype(jnp.float32)
    volume = elastic[0] + elastic[1] + elastic[2]
    third = volume * (1.0 / 3.0)
    trial = [2.0 * SHEAR_MODULUS * (elastic[a] - third) for a in range(3)]
    trial += [2.0 * SHEAR_MODULUS * elastic[a] for a in range(3, 6)]
    normal = trial[0] * trial[0] + trial[1] * trial[1] + trial[2] * trial[2]
    shear = trial[3] * trial[3] + trial[4] * trial[4] + trial[5] * trial[5]
    equivalent = jnp.sqrt(1.5 * (normal + 2.0 * shear))
    bounded = jnp.maximum(equivalent, limit)
    inverse = 1.0 / bounded
    scaled = ratio * active
    softening = 1.0 - scaled * (equivalent - limit) * inverse
    pressure = BULK_MODULUS * volume
    stress = [trial[a] * softening + pressure for a in range(3)]
    stress += [trial[a] * softening for a in range(3, 6)]
    weight = 3.0 * SHEAR_MODULUS * scaled * limit * (inverse * inverse * inverse)
    return stress, trial, softening, weight


def every_fourth(ref, start, plane):
    return ref[pl.ds(start + plane, 32, stride=4), :]


def put_split(high_ref, low_ref, rows, cols, value):
    high, low = split(value)
    high_ref[rows, cols] = high
    low_ref[rows, cols] = low


def forward_planes(xh, xl, bh, bl, wh, wl, th, tl, out_ref):
    turned = data_by_table(xh[...], xl[...], wh[...], wl[...])
    for c in range(6):
        for s in range(4):
            block = turned[c * 32 : (c + 1) * 32, s * 128 : (s + 1) * 128]
            put_split(bh, bl, pl.ds(s * 32, 32), pl.ds(c * 128, 128), block)
    spectrum = table_by_data(th[...], tl[...], bh[...], bl[...])
    for c in range(6):
        out_ref[:, c * 8 : (c + 1) * 8, :] = spectrum[:, c * 128 : (c + 1) * 128].reshape(
            16, 8, 128
        )


def load_columns(in_ref, bh, bl):
    for c in range(6):
        block = in_ref[:, c * 8 : (c + 1) * 8, :].reshape(128, 128)
        put_split(bh, bl, slice(None), pl.ds(c * 128, 128), block)


def backward_planes(in_ref, xh, xl, bh, bl, wh, wl, th, tl):
    load_columns(in_ref, bh, bl)
    rows = table_by_data(th[...], tl[...], bh[...], bl[...])
    for c in range(6):
        for s in range(4):
            block = rows[s * 32 : (s + 1) * 32, c * 128 : (c + 1) * 128]
            put_split(xh, xl, pl.ds(c * 32, 32), pl.ds(s * 128, 128), block)
    return data_by_table(xh[...], xl[...], wh[...], wl[...])


def first_kernel(
    point_ref, conn_ref, disp_ref, phase_ref, flag_ref, plastic_ref,
    wh, wl, th, tl, out_ref, xh, xl, bh, bl,
):
    macro = macro_strain(point_ref[0], conn_ref, disp_ref)
    for plane in range(PLANES):
        elastic = [macro[c] - every_fourth(plastic_ref, c * 128, plane) for c in range(6)]
        phases = every_fourth(phase_ref, 0, plane)
        flags = every_fourth(flag_ref, 0, plane)
        stress = material(elastic, phases, flags)[0]
        for c in range(6):
            put_split(xh, xl, pl.ds(c * 32, 32), pl.ds(plane * 128, 128), stress[c])
    forward_planes(xh, xl, bh, bl, wh, wl, th, tl, out_ref)


def middle_kernel(
    point_ref, conn_ref, disp_ref, phase_ref, flag_ref, plastic_ref, in_ref,
    vh, vl, uh, ul, wh, wl, th, tl, out_ref, elastic_ref, xh, xl, bh, bl,
):
    macro = macro_strain(point_ref[0], conn_ref, disp_ref)
    correction = backward_planes(in_ref, xh, xl, bh, bl, vh, vl, uh, ul)
    for plane in range(PLANES):
        lanes = slice(plane * 128, (plane + 1) * 128)
        elastic = []
        for c in range(6):
            before = macro[c] - every_fourth(plastic_ref, c * 128, plane)
            after = before - correction[c * 32 : (c + 1) * 32, lanes]
            elastic_ref[c * 32 : (c + 1) * 32, lanes] = after
            elastic.append(after)
        phases = every_fourth(phase_ref, 0, plane)
        flags = every_fourth(flag_ref, 0, plane)
        stress = material(elastic, phases, flags)[0]
        for c in range(6):
            put_split(xh, xl, pl.ds(c * 32, 32), pl.ds(plane * 128, 128), stress[c])
    forward_planes(xh, xl, bh, bl, wh, wl, th, tl, out_ref)


def last_kernel(
    phase_ref, flag_ref, elastic_ref, in_ref, vh, vl, uh, ul, out_ref, xh, xl, bh, bl
):
    correction = backward_planes(in_ref, xh, xl, bh, bl, vh, vl, uh, ul)
    sums = [None] * 28

    def collect(at, value):
        part = value.reshape(4, 8, 128)
        part = (part[0] + part[1]) + (part[2] + part[3])
        sums[at] = part if sums[at] is None else sums[at] + part

    for plane in range(PLANES):
        lanes = slice(plane * 128, (plane + 1) * 128)
        elastic = [
            elastic_ref[c * 32 : (c + 1) * 32, lanes] - correction[c * 32 : (c + 1) * 32, lanes]
            for c in range(6)
        ]
        phases = every_fourth(phase_ref, 0, plane)
        flags = every_fourth(flag_ref, 0, plane)
        stress, trial, softening, weight = material(elastic, phases, flags)
        for c in range(6):
            collect(c, stress[c])
        collect(6, softening)
        at = 7
        for a in range(6):
            scaled = weight * trial[a]
            for b in range(a, 6):
                collect(at, scaled * trial[b])
                at += 1
    row = lax.broadcasted_iota(jnp.int32, (128, 128), 0)
    lines = jnp.zeros((128, 128), jnp.float32)

    def place(at, value):
        return jnp.where(row == at, jnp.broadcast_to(value, (128, 128)), lines)

    totals = [jnp.sum(value, axis=0, keepdims=True) for value in sums]
    for c in range(7):
        lines = place(c, totals[c])
    at = 7
    for a in range(6):
        for b in range(a, 6):
            lines = place(OUTER_AT + 6 * a + b, totals[at])
            if a != b:
                lines = place(OUTER_AT + 6 * b + a, totals[at])
            at += 1
    ones = jnp.ones((8, 128), jnp.float32)
    line = lax.dot_general(
        ones, lines, (((1,), (1,)), ((), ())),
        precision=lax.Precision.HIGHEST, preferred_element_type=jnp.float32,
    )
    out_ref[...] = jnp.broadcast_to(line[None], out_ref.shape)


def column_kernel(slab_ref, in_ref, th, tl, bh_table, bl_table, twist_ref, four, fourback, out_ref, bh, bl, yh, yl):
    load_columns(in_ref, bh, bl)
    mixed = table_by_data(th[...], tl[...], bh[...], bl[...])
    cosine, sine = twist_ref[0], twist_ref[1]
    for c in range(6):
        lanes = slice(c * 128, (c + 1) * 128)
        real, imag = mixed[:64, lanes], mixed[64:, lanes]
        rows = pl.ds(c * 64, 64)
        put_split(yh, yl, rows, pl.ds(0, 128), real * cosine + imag * sine)
        put_split(yh, yl, rows, pl.ds(128, 128), imag * cosine - real * sine)
    spectrum = mm(yh[...], four[...]) + mm(yl[...], four[...])
    tau = [spectrum[c * 64 : (c + 1) * 64] for c in range(6)]

    shape = (64, 256)
    row = lax.broadcasted_iota(jnp.int32, shape, 0)
    lane = lax.broadcasted_iota(jnp.int32, shape, 1)
    lane = lax.bitwise_and(lane, 127)
    kx = 16 * lax.shift_right_logical(lane, 5) + lax.shift_right_logical(row, 2)
    ky = 4 * slab_ref[0] + lax.bitwise_and(row, 3)
    kz = lax.bitwise_and(lane, 31)
    half = GRID // 2
    keep = (kx != half) & (ky != half) & (kx + ky + kz > 0)
    xi = [
        jnp.where(kx < half, kx, kx - GRID).astype(jnp.float32),
        jnp.where(ky < half, ky, ky - GRID).astype(jnp.float32),
        kz.astype(jnp.float32),
    ]
    length = xi[0] * xi[0] + xi[1] * xi[1] + xi[2] * xi[2]
    inverse = jnp.where(keep, 1.0 / jnp.maximum(length, 1.0), 0.0)
    coupling = (REFERENCE_LAME + REFERENCE_SHEAR) / (
        REFERENCE_SHEAR * (REFERENCE_LAME + 2.0 * REFERENCE_SHEAR)
    )
    scaled = inverse * (1.0 / (2.0 * REFERENCE_SHEAR))
    traction = [
        tau[r[0]] * xi[0] + tau[r[1]] * xi[1] + tau[r[2]] * xi[2] for r in TENSOR_ROWS
    ]
    load = xi[0] * traction[0] + xi[1] * traction[1] + xi[2] * traction[2]
    load = load * (inverse * (REFERENCE_SHEAR * coupling))
    field = [scaled * (traction[i] - xi[i] * load) for i in range(3)]
    for c, (i, k) in enumerate(TENSOR_PAIRS):
        entry = xi[i] * field[k] + xi[k] * field[i]
        put_split(yh, yl, pl.ds(c * 64, 64), slice(None), entry)
    turned = mm(yh[...], fourback[...]) + mm(yl[...], fourback[...])
    for c in range(6):
        real, imag = turned[c * 64 : (c + 1) * 64, :128], turned[c * 64 : (c + 1) * 64, 128:]
        cols = pl.ds(c * 128, 128)
        put_split(bh, bl, pl.ds(0, 64), cols, real * cosine - imag * sine)
        put_split(bh, bl, pl.ds(64, 64), cols, real * sine + imag * cosine)
    result = table_by_data(bh_table[...], bl_table[...], bh[...], bl[...])
    for c in range(6):
        out_ref[:, c * 8 : (c + 1) * 8, :] = result[:, c * 128 : (c + 1) * 128].reshape(16, 8, 128)


def assembly_kernel(points, conn_ref, in_ref, stiffness_ref, forces_ref):
    sums = in_ref[pl.ds(0, points, stride=8), :] * (1.0 / VOXELS)
    shape = (points, 128)
    lane = lax.broadcasted_iota(jnp.int32, shape, 1)
    point = lax.broadcasted_iota(jnp.int32, shape, 0)
    element = lax.shift_right_logical(point, 3)
    bits = [lax.bitwise_and(lax.shift_right_logical(point, d), 1) for d in range(3)]
    slope = slopes_of(bits, GAUSS_LOW, GAUSS_HIGH)
    node = lane // 3
    part = lane - 3 * node
    elements = conn_ref.shape[0]
    grad = [jnp.zeros(shape, jnp.float32) for _ in range(3)]
    for corner in range(8):
        owner = jnp.full(shape, conn_ref[0, corner], jnp.int32)
        for e in range(1, elements):
            owner = jnp.where(element == e, conn_ref[e, corner], owner)
        here = (owner == node) & (lane < 60)
        for d in range(3):
            grad[d] = grad[d] + jnp.where(here, slope(corner, d), 0.0)
    basis = []
    for i, k in TENSOR_PAIRS:
        if i == k:
            basis.append(jnp.where(part == i, grad[i], 0.0))
        else:
            value = jnp.where(part == i, 0.5 * grad[k], 0.0)
            basis.append(value + jnp.where(part == k, 0.5 * grad[i], 0.0))
    mean_shear = 2.0 * SHEAR_MODULUS * sums[:, 6:7]

    def column(at):
        return jnp.broadcast_to(sums[:, at : at + 1], shape)

    mean_shear = jnp.broadcast_to(mean_shear, shape)
    on_diagonal = BULK_MODULUS + mean_shear * (2.0 / 3.0)
    off_diagonal = BULK_MODULUS - mean_shear * (1.0 / 3.0)
    answers = []
    force = jnp.zeros(shape, jnp.float32)
    scale = QUADRATURE_WEIGHT / TANGENT_UNIT
    for a in range(6):
        total = jnp.zeros(shape, jnp.float32)
        for b in range(6):
            low, high = min(a, b), max(a, b)
            entry = -PAIR_WEIGHTS[b] * column(OUTER_AT + 6 * low + high)
            if a == b:
                entry = entry + (on_diagonal if a < 3 else mean_shear)
            elif a < 3 and b < 3:
                entry = entry + off_diagonal
            total = total + entry * basis[b]
        answers.append(total * (PAIR_WEIGHTS[a] * scale))
        force = force + basis[a] * (column(a) * (PAIR_WEIGHTS[a] * QUADRATURE_WEIGHT))
    left = jnp.concatenate(basis, axis=0)
    right = jnp.concatenate(answers, axis=0)
    whole = lax.dot_general(
        left, right, (((0,), (0,)), ((), ())),
        precision=lax.Precision.HIGHEST, preferred_element_type=jnp.float32,
    )
    stiffness_ref[...] = whole[:60, :60]
    line = jnp.sum(force, axis=0, keepdims=True)
    row24 = lax.broadcasted_iota(jnp.int32, (24, 128), 0)
    lane24 = lax.broadcasted_iota(jnp.int32, (24, 128), 1)
    spread = jnp.where(lane24 // 3 == row24, jnp.broadcast_to(line, (24, 128)), 0.0)
    pick_row = lax.broadcasted_iota(jnp.int32, (128, 128), 0)
    pick_col = lax.broadcasted_iota(jnp.int32, (128, 128), 1)
    pick = (pick_row % 3 == pick_col).astype(jnp.float32)
    forces = jnp.dot(
        spread, pick, precision=lax.Precision.HIGHEST, preferred_element_type=jnp.float32
    )
    forces_ref[...] = forces[:20, :3]


SMEM = pl.BlockSpec(memory_space=pltpu.SMEM)
VMEM = pl.BlockSpec(memory_space=pltpu.VMEM)
BF16 = jnp.bfloat16
F32 = jnp.float32
LIMIT = 16 * 1024 * 1024


def params():
    return pltpu.CompilerParams(vmem_limit_bytes=LIMIT)


def cost(flops, size):
    return pl.CostEstimate(flops=flops, bytes_accessed=size, transcendentals=0)


def plane_scratch():
    return [
        pltpu.VMEM((192, 512), BF16),
        pltpu.VMEM((192, 512), BF16),
        pltpu.VMEM((128, 768), BF16),
        pltpu.VMEM((128, 768), BF16),
    ]


def exchange(array):
    return lax.all_to_all(array, "slab", split_axis=0, concat_axis=0, tiled=True)


def on_device(phase_ids, yield_flags, plastic_strain, displacements, connectivity):
    points = lax.axis_size("rve")
    point = lax.axis_index("rve").astype(jnp.int32).reshape(1)
    slab = lax.axis_index("slab").astype(jnp.int32).reshape(1)

    def rows(array):
        lead = math.prod(array.shape[:-2])
        array = array.reshape(lead, PLANES, 32, 128)
        return jnp.transpose(array, (0, 2, 1, 3)).reshape(lead * 128, 128)

    phases = rows(phase_ids)
    flags = rows(yield_flags)
    plastic = rows(plastic_strain)

    there, back = depth_tables()
    wh, wl = (jnp.asarray(t) for t in halves(there))
    vh, vl = (jnp.asarray(t) for t in halves(back))
    there, back = row_tables()
    th, tl = (jnp.asarray(t) for t in halves(there))
    uh, ul = (jnp.asarray(t) for t in halves(back))
    there, back, twist, four, fourback = column_tables()
    ch, cl = (jnp.asarray(t) for t in halves(there))
    dh, dl = (jnp.asarray(t) for t in halves(back))
    twist = jnp.asarray(twist)
    four = jnp.asarray(four.astype(ml_dtypes.bfloat16))
    fourback = jnp.asarray(fourback.astype(ml_dtypes.bfloat16))

    block = jax.ShapeDtypeStruct((16, 48, 128), F32)

    def flag_block(evaluation):
        return flags[evaluation * 128 : (evaluation + 1) * 128]

    first = pl.pallas_call(
        first_kernel, out_shape=block,
        in_specs=[SMEM] * 3 + [VMEM] * 7, out_specs=VMEM,
        scratch_shapes=plane_scratch(), compiler_params=params(),
        cost_estimate=cost(400_000_000, 2_000_000), name="first",
    )
    columns = pl.pallas_call(
        column_kernel, out_shape=block,
        in_specs=[SMEM] + [VMEM] * 8, out_specs=VMEM,
        scratch_shapes=[
            pltpu.VMEM((128, 768), BF16), pltpu.VMEM((128, 768), BF16),
            pltpu.VMEM((384, 256), BF16), pltpu.VMEM((384, 256), BF16),
        ],
        compiler_params=params(), cost_estimate=cost(400_000_000, 2_000_000), name="columns",
    )
    middle = pl.pallas_call(
        middle_kernel, out_shape=(block, jax.ShapeDtypeStruct((192, 512), F32)),
        in_specs=[SMEM] * 3 + [VMEM] * 12, out_specs=(VMEM, VMEM),
        scratch_shapes=plane_scratch(), compiler_params=params(),
        cost_estimate=cost(800_000_000, 4_000_000), name="middle",
    )
    last = pl.pallas_call(
        last_kernel, out_shape=jax.ShapeDtypeStruct((16, 8, 128), F32),
        in_specs=[VMEM] * 8, out_specs=VMEM,
        scratch_shapes=plane_scratch(), compiler_params=params(),
        cost_estimate=cost(400_000_000, 2_000_000), name="last",
    )
    assembly = pl.pallas_call(
        functools.partial(assembly_kernel, points),
        out_shape=(jax.ShapeDtypeStruct((60, 60), F32), jax.ShapeDtypeStruct((20, 3), F32)),
        in_specs=[SMEM, VMEM], out_specs=(VMEM, VMEM), compiler_params=params(),
        cost_estimate=cost(10_000_000, 200_000), name="assembly",
    )

    def apply_columns(array):
        received = exchange(array)
        return exchange(columns(slab, received, ch, cl, dh, dl, twist, four, fourback))

    spectrum = first(
        point, connectivity, displacements, phases, flag_block(0), plastic, wh, wl, th, tl
    )
    planes = apply_columns(spectrum)
    spectrum, elastic = middle(
        point, connectivity, displacements, phases, flag_block(1), plastic, planes,
        vh, vl, uh, ul, wh, wl, th, tl,
    )
    planes = apply_columns(spectrum)
    partial = last(phases, flag_block(2), elastic, planes, vh, vl, uh, ul)
    sums = jnp.sum(exchange(partial), axis=0)
    everyone = lax.all_to_all(
        jnp.broadcast_to(sums[None], (points, 8, 128)), "rve", 0, 0, tiled=True
    )
    stiffness, forces = assembly(connectivity, everyone.reshape(points * 8, 128))

    own = sums[0] * (1.0 / VOXELS)
    mean_stress = own[:6].reshape(1, 6)
    outer = own[OUTER_AT : OUTER_AT + 36].reshape(6, 6)
    diagonal = np.array([1.0, 1.0, 1.0, 0.0, 0.0, 0.0])
    volumetric = diagonal[:, None] * diagonal[None, :]
    fixed = jnp.asarray(BULK_MODULUS * volumetric / TANGENT_UNIT, F32)
    turning = (np.eye(6) - volumetric / 3.0) * (2.0 * SHEAR_MODULUS / TANGENT_UNIT)
    weights = np.asarray(PAIR_WEIGHTS)[None, :] / TANGENT_UNIT
    tangent = (
        fixed + own[6] * jnp.asarray(turning, F32) - outer * jnp.asarray(weights, F32)
    )
    return (mean_stress, tangent[None], forces, stiffness)


def solution(mesh):
    return jax.shard_map(
        on_device,
        mesh=mesh,
        in_specs=(
            P("slab", None),
            P("rve", None, "slab", None),
            P("rve", None, "slab", None),
            P(),
            P(),
        ),
        out_specs=(P("rve", None), P("rve", None, None), P(), P()),
        check_vma=False,
    )
```

profile of v0, /device:TPU:1, one launch (start us, length us, event | category | flops | bytes accessed | tf_op | source)
XLA Modules:
  0.0 116.8 jit_solution(16642843945415901614)
XLA Ops:
  0.6 0.0 copy-start.12
  0.7 0.8 copy.31.disp_ref
  1.5 0.9 fusion.1
  2.4 0.0 copy-start.2
  2.5 1.0 copy-done.2
  3.5 1.0 copy-done.4
  4.5 0.8 copy-done.7
  5.4 0.7 copy-done.13
  6.0 2.5 %first.1 = f32[16,48,128]{2,1,0:T(8,128)} custom-call(s32[1]{0:T(128)} %bitcast.6.point_ref, s32[4,8]{1,0:T(4,128)S(1)} %copy-done.13, f32[20,3]{1,0:T(8,128)S(1)} %copy.31.disp_ref, s32[128,128]{1,0:T(8,128)S(1)} %bitcast.25, s32[128,128]{1,0:T(8,128)S(1)} %bitcast.31, f32[768,128]{1,0:T(8,128)S(1)} %bitcast.23, bf16[512,512]{1,0:T(8,128)(2,1)S(1)} %copy-done.4, ...), custom_call_target="tpu_custom_call" | custom-call | flops 400000000 | bytes 2000000 | tf_op jit(solution)/shard_map/first/pallas_call | solution.py:526
  8.6 0.0 copy-start.19
  8.6 0.0 copy-start.20
  8.6 0.0 copy-start.21
  8.6 7.7 %all-to-all-start = ((f32[16,48,128]{2,1,0:T(8,128)}), f32[16,48,128]{2,1,0:T(8,128)S(1)}, u32[]{:S(2)}, u32[]{:S(2)}) async-start(f32[16,48,128]{2,1,0:T(8,128)} %first.1), calls=%async_computation | async-start | bytes 786432 | tf_op jit(solution)/shard_map/all_to_all | solution.py:453
  16.4 8.2 %all-to-all-done.in_ref = f32[16,48,128]{2,1,0:T(8,128)S(1)} async-done(((f32[16,48,128]{2,1,0:T(8,128)}), f32[16,48,128]{2,1,0:T(8,128)S(1)}, u32[]{:S(2)}, u32[]{:S(2)}) %all-to-all-start) | async-done | bytes 393248 | tf_op jit(solution)/shard_map/all_to_all | solution.py:453
  24.6 0.0 copy-done.18
  24.6 0.0 copy-done.19
  24.6 0.0 copy-done.20
  24.7 0.0 copy-done.21
  24.7 0.0 copy-start.1
  24.7 0.0 copy-start.3
  24.7 0.0 copy-start.5
  24.7 1.4 %columns.2 = f32[16,48,128]{2,1,0:T(8,128)S(1)} custom-call(s32[1]{0:T(128)} %bitcast.14.slab_ref, f32[16,48,128]{2,1,0:T(8,128)S(1)} %all-to-all-done.in_ref, bf16[128,128]{1,0:T(8,128)(2,1)S(1)} %copy-done.21, bf16[128,128]{1,0:T(8,128)(2,1)S(1)} %copy-done.20, bf16[128,128]{1,0:T(8,128)(2,1)S(1)} %copy-done.19, bf16[128,128]{1,0:T(8,128)(2,1)S(1)} %copy-done.18, ...), custom_call_target="tpu_custom_call" | custom-call | flops 400000000 | bytes 2000000 | tf_op jit(solution)/shard_map/columns/pallas_call | solution.py:524
  26.1 0.0 copy-start
  26.1 0.0 copy-start.8
  26.1 0.0 copy-start.9
  26.2 0.0 copy-start.10
  26.2 11.1 %all_to_all.30.in_ref = f32[16,48,128]{2,1,0:T(8,128)S(1)} all-to-all(f32[16,48,128]{2,1,0:T(8,128)S(1)} %columns.2), channel_id=1, replica_groups=mesh['rve'=32,'slab'=16] {'slab'}, dimensions={0} | all-to-all | bytes 786432 | tf_op jit(solution)/shard_map/all_to_all | solution.py:453
  37.3 0.6 copy-done.14
  38.0 2.6 %middle.1 = (f32[16,48,128]{2,1,0:T(8,128)S(1)}, f32[192,512]{1,0:T(8,128)S(1)}) custom-call(s32[1]{0:T(128)} %bitcast.6.point_ref, s32[4,8]{1,0:T(4,128)S(1)} %copy-done.14, f32[20,3]{1,0:T(8,128)S(1)} %copy.31.disp_ref, s32[128,128]{1,0:T(8,128)S(1)} %bitcast.26, s32[128,128]{1,0:T(8,128)S(1)} %bitcast.30, f32[768,128]{1,0:T(8,128)S(1)} %bitcast.24, ...), custom_call_target="tpu_custom_call" | custom-call | flops 800000000 | bytes 4000000 | tf_op jit(solution)/shard_map/middle/pallas_call | solution.py:530
  40.5 10.9 %all_to_all.31.in_ref = f32[16,48,128]{2,1,0:T(8,128)S(1)} all-to-all(f32[16,48,128]{2,1,0:T(8,128)S(1)} %get-tuple-element.9), channel_id=1, replica_groups=mesh['rve'=32,'slab'=16] {'slab'}, dimensions={0} | all-to-all | bytes 786432 | tf_op jit(solution)/shard_map/all_to_all | solution.py:453
  51.4 1.4 %columns.3 = f32[16,48,128]{2,1,0:T(8,128)S(1)} custom-call(s32[1]{0:T(128)} %bitcast.14.slab_ref, f32[16,48,128]{2,1,0:T(8,128)S(1)} %all_to_all.31.in_ref, bf16[128,128]{1,0:T(8,128)(2,1)S(1)} %copy-done.21, bf16[128,128]{1,0:T(8,128)(2,1)S(1)} %copy-done.20, bf16[128,128]{1,0:T(8,128)(2,1)S(1)} %copy-done.19, bf16[128,128]{1,0:T(8,128)(2,1)S(1)} %copy-done.18, ...), custom_call_target="tpu_custom_call" | custom-call | flops 400000000 | bytes 2000000 | tf_op jit(solution)/shard_map/columns/pallas_call | solution.py:524
  52.8 10.9 %all_to_all.32.in_ref = f32[16,48,128]{2,1,0:T(8,128)S(1)} all-to-all(f32[16,48,128]{2,1,0:T(8,128)S(1)} %columns.3), channel_id=1, replica_groups=mesh['rve'=32,'slab'=16] {'slab'}, dimensions={0} | all-to-all | bytes 786432 | tf_op jit(solution)/shard_map/all_to_all | solution.py:453
  63.7 1.3 %last.1 = f32[16,8,128]{2,1,0:T(8,128)S(1)} custom-call(s32[128,128]{1,0:T(8,128)S(1)} %bitcast.27, s32[128,128]{1,0:T(8,128)S(1)} %bitcast.29, f32[192,512]{1,0:T(8,128)S(1)} %get-tuple-element.8.elastic_ref, f32[16,48,128]{2,1,0:T(8,128)S(1)} %all_to_all.32.in_ref, bf16[512,512]{1,0:T(8,128)(2,1)S(1)} %copy-done.1, bf16[512,512]{1,0:T(8,128)(2,1)S(1)} %copy-done, ...), custom_call_target="tpu_custom_call" | custom-call | flops 400000000 | bytes 2000000 | tf_op jit(solution)/shard_map/last/pallas_call | solution.py:535
  65.0 9.1 %all_to_all.33 = f32[16,8,128]{2,1,0:T(8,128)S(1)} all-to-all(f32[16,8,128]{2,1,0:T(8,128)S(1)} %last.1), channel_id=1, replica_groups=mesh['rve'=32,'slab'=16] {'slab'}, dimensions={0} | all-to-all | bytes 131072 | tf_op jit(solution)/shard_map/all_to_all | solution.py:453
  74.1 0.7 broadcast_in_dim.10
  74.8 23.8 %all-to-all-start.5 = ((f32[32,8,128]{2,1,0:T(8,128)}), f32[32,8,128]{2,1,0:T(8,128)S(1)}, u32[]{:S(2)}, u32[]{:S(2)}) async-start(f32[32,8,128]{2,1,0:T(8,128)} %broadcast_in_dim.10), calls=%async_computation.5 | async-start | bytes 262144 | tf_op jit(solution)/shard_map/all_to_all | solution.py:537
  98.6 0.0 copy-start.25
  98.6 0.6 slice.41
  99.2 0.0 copy-done.25
  99.2 0.1 slice_reduce_fusion
  99.3 0.1 reshape.56
  99.4 0.5 copy-done.22
  99.9 0.0 copy-done.23
  99.9 0.6 fusion
  100.6 0.6 copy.32
  101.1 13.3 %all-to-all-done.5 = f32[32,8,128]{2,1,0:T(8,128)S(1)} async-done(((f32[32,8,128]{2,1,0:T(8,128)}), f32[32,8,128]{2,1,0:T(8,128)S(1)}, u32[]{:S(2)}, u32[]{:S(2)}) %all-to-all-start.5) | async-done | bytes 131104 | tf_op jit(solution)/shard_map/all_to_all | solution.py:537
  114.4 1.7 %assembly.1 = (f32[60,60]{1,0:T(8,128)}, f32[20,3]{1,0:T(8,128)S(1)}) custom-call(s32[4,8]{1,0:T(4,128)S(1)} %copy-done.14, f32[256,128]{1,0:T(8,128)S(1)} %bitcast.28), custom_call_target="tpu_custom_call" | custom-call | flops 10000000 | bytes 200000 | tf_op jit(solution)/shard_map/assembly/pallas_call | solution.py:540
  116.2 0.7 copy.33
  (29 shorter events, 0.1 us)
Async XLA Ops:
  0.6 1.8 %copy-start.12 = (bf16[128,128]{1,0:T(8,128)(2,1)S(1)}, bf16[128,128]{1,0:T(8,128)(2,1)}, u32[]{:S(2)}) copy-start(bf16[128,128]{1,0:T(8,128)(2,1)} %constant.53.clone.th) | copy-start | bytes 98308
  0.6 1.8 %copy-start.6 = (f32[1,6,4,4096]{3,2,1,0:T(4,128)S(1)}, f32[1,6,4,4096]{3,2,1,0:T(4,128)}, u32[]{:S(2)}) copy-start(f32[1,6,4,4096]{3,2,1,0:T(4,128)} %param.25) | copy-start | bytes 1179652
  1.5 0.9 copy-start.11
  2.4 1.0 copy-start.2
  3.5 1.0 copy-start.4
  4.5 0.8 copy-start.7
  5.4 0.7 copy-start.13
  8.6 16.0 %copy-start.15 = (bf16[256,256]{1,0:T(8,128)(2,1)S(1)}, bf16[256,256]{1,0:T(8,128)(2,1)}, u32[]{:S(2)}) copy-start(bf16[256,256]{1,0:T(8,128)(2,1)} %constant.63.clone.fourback) | copy-start | bytes 393220
  8.6 16.0 %copy-start.16 = (bf16[256,256]{1,0:T(8,128)(2,1)S(1)}, bf16[256,256]{1,0:T(8,128)(2,1)}, u32[]{:S(2)}) copy-start(bf16[256,256]{1,0:T(8,128)(2,1)} %constant.62.clone.four) | copy-start | bytes 393220
  8.6 16.0 %copy-start.17 = (f32[2,64,128]{2,1,0:T(8,128)S(1)}, f32[2,64,128]{2,1,0:T(8,128)}, u32[]{:S(2)}) copy-start(f32[2,64,128]{2,1,0:T(8,128)} %constant.61.clone.twist_ref) | copy-start | bytes 196612
  8.6 16.0 %copy-start.18 = (bf16[128,128]{1,0:T(8,128)(2,1)S(1)}, bf16[128,128]{1,0:T(8,128)(2,1)}, u32[]{:S(2)}) copy-start(bf16[128,128]{1,0:T(8,128)(2,1)} %constant.60.clone.bl_table) | copy-start | bytes 98308
  8.6 16.0 %copy-start.19 = (bf16[128,128]{1,0:T(8,128)(2,1)S(1)}, bf16[128,128]{1,0:T(8,128)(2,1)}, u32[]{:S(2)}) copy-start(bf16[128,128]{1,0:T(8,128)(2,1)} %constant.59.clone.bh_table) | copy-start | bytes 98308
  8.6 16.0 %copy-start.20 = (bf16[128,128]{1,0:T(8,128)(2,1)S(1)}, bf16[128,128]{1,0:T(8,128)(2,1)}, u32[]{:S(2)}) copy-start(bf16[128,128]{1,0:T(8,128)(2,1)} %constant.58.clone.tl) | copy-start | bytes 98308
  8.6 16.0 %copy-start.21 = (bf16[128,128]{1,0:T(8,128)(2,1)S(1)}, bf16[128,128]{1,0:T(8,128)(2,1)}, u32[]{:S(2)}) copy-start(bf16[128,128]{1,0:T(8,128)(2,1)} %constant.57.clone.th) | copy-start | bytes 98308
  8.6 16.0 %all-to-all-start = ((f32[16,48,128]{2,1,0:T(8,128)}), f32[16,48,128]{2,1,0:T(8,128)S(1)}, u32[]{:S(2)}, u32[]{:S(2)}) async-start(f32[16,48,128]{2,1,0:T(8,128)} %first.1), calls=%async_computation | async-start | bytes 786432 | tf_op jit(solution)/shard_map/all_to_all | solution.py:453
  24.7 12.6 %copy-start.1 = (bf16[512,512]{1,0:T(8,128)(2,1)S(1)}, bf16[512,512]{1,0:T(8,128)(2,1)}, u32[]{:S(2)}) copy-start(bf16[512,512]{1,0:T(8,128)(2,1)} %constant.51.clone.vh) | copy-start | bytes 1572868
  24.7 12.6 %copy-start.3 = (bf16[512,512]{1,0:T(8,128)(2,1)S(1)}, bf16[512,512]{1,0:T(8,128)(2,1)}, u32[]{:S(2)}) copy-start(bf16[512,512]{1,0:T(8,128)(2,1)} %constant.50.clone.wl) | copy-start | bytes 1572868
  24.7 12.6 %copy-start.5 = (bf16[512,512]{1,0:T(8,128)(2,1)S(1)}, bf16[512,512]{1,0:T(8,128)(2,1)}, u32[]{:S(2)}) copy-start(bf16[512,512]{1,0:T(8,128)(2,1)} %constant.49.clone.wh) | copy-start | bytes 1572868
  26.1 11.2 %copy-start = (bf16[512,512]{1,0:T(8,128)(2,1)S(1)}, bf16[512,512]{1,0:T(8,128)(2,1)}, u32[]{:S(2)}) copy-start(bf16[512,512]{1,0:T(8,128)(2,1)} %constant.52.clone.vl) | copy-start | bytes 1572868
  26.1 11.2 %copy-start.8 = (s32[4,4096]{1,0:T(4,128)S(1)}, s32[4,4096]{1,0:T(4,128)}, u32[]{:S(2)}) copy-start(s32[4,4096]{1,0:T(4,128)} %param.23) | copy-start | bytes 196612
  26.1 11.2 %copy-start.9 = (bf16[128,128]{1,0:T(8,128)(2,1)S(1)}, bf16[128,128]{1,0:T(8,128)(2,1)}, u32[]{:S(2)}) copy-start(bf16[128,128]{1,0:T(8,128)(2,1)} %constant.56.clone.ul) | copy-start | bytes 98308
  26.2 11.2 %copy-start.10 = (bf16[128,128]{1,0:T(8,128)(2,1)S(1)}, bf16[128,128]{1,0:T(8,128)(2,1)}, u32[]{:S(2)}) copy-start(bf16[128,128]{1,0:T(8,128)(2,1)} %constant.55.clone.uh) | copy-start | bytes 98308
  37.3 0.7 copy-start.14
  74.8 24.6 %copy-start.24 = (f32[6]{0:T(128)S(1)}, f32[6]{0:T(128)}, u32[]{:S(2)}) copy-start(f32[6]{0:T(128)} %constant.70) | copy-start | bytes 76
  74.8 39.6 %all-to-all-start.5 = ((f32[32,8,128]{2,1,0:T(8,128)}), f32[32,8,128]{2,1,0:T(8,128)S(1)}, u32[]{:S(2)}, u32[]{:S(2)}) async-start(f32[32,8,128]{2,1,0:T(8,128)} %broadcast_in_dim.10), calls=%async_computation.5 | async-start | bytes 262144 | tf_op jit(solution)/shard_map/all_to_all | solution.py:537
  98.6 0.6 copy-start.25
  99.2 0.7 copy-start.22
  99.2 0.7 copy-start.23
where the time goes:
time: 118 us; the launch traced here: 117 us
  blocking collectives  42 us (36%)
  starting transfers between devices  31.5 us (27%)
  waiting for transfers between devices  21.5 us (18%)
  Pallas kernels  10.9 us (9%)
  local copies, waits for them, and re-layouts  9.26 us (8%)
    all_to_all x4, blocking collectives, exchange(): lax.all_to_all(array, 'slab', split_axis=0, concat_axis=0, tiled=True)  42 us
    all_to_all x1, starting transfers between devices, on_device(): lax.all_to_all(jnp.broadcast_to(sums[None], (points, 8, 128)), 'rve', 0,...  23.8 us
    all_to_all x1, waiting for transfers between devices, on_device(): lax.all_to_all(jnp.broadcast_to(sums[None], (points, 8, 128)), 'rve', 0,...  13.3 us
    all_to_all x1, waiting for transfers between devices, exchange(): lax.all_to_all(array, 'slab', split_axis=0, concat_axis=0, tiled=True)  8.24 us
    all_to_all x1, starting transfers between devices, exchange(): lax.all_to_all(array, 'slab', split_axis=0, concat_axis=0, tiled=True)  7.72 us
    unnamed x55, local copies, waits for them, and re-layouts  6.93 us
    pallas_call x2, Pallas kernels, apply_columns(): columns(slab, received, ch, cl, dh, dl, twist, four, fourback)  2.82 us
    pallas_call x1, Pallas kernels, on_device(): middle(point, connectivity, displacements, phases, flag_block(1), plastic...  2.58 us
  transfers between devices with their start and end apart: 2, of which 2 were waited for; matrix products, arithmetic and copies ran while one was open for 2% of the time, Pallas kernels for 0%

commit v1 on v0

--- a/solution.py
+++ b/solution.py
@@ -138,7 +138,7 @@
     for corner in range(8):
         node = conn_ref[element, corner]
         for k in range(3):
-            u = disp_ref[node, k]
+            u = disp_ref[k, node]
             for d in range(3):
                 grad[k][d] = grad[k][d] + slope(corner, d) * u
     strain = []
@@ -214,10 +214,28 @@
 
 
 def first_kernel(
-    point_ref, conn_ref, disp_ref, phase_ref, flag_ref, plastic_ref,
-    wh, wl, th, tl, out_ref, xh, xl, bh, bl,
+    conn_hbm, disp_hbm, phase_hbm, flag_hbm, plastic_hbm, wh_hbm, wl_hbm, th_hbm, tl_hbm,
+    out_ref, macro_ref,
+    conn_ref, disp_ref, phase_ref, flag_ref, plastic_ref, wh, wl, th, tl, sems, xh, xl, bh, bl,
 ):
-    macro = macro_strain(point_ref[0], conn_ref, disp_ref)
+    pairs = (
+        (conn_hbm, conn_ref), (disp_hbm, disp_ref), (plastic_hbm, plastic_ref),
+        (phase_hbm, phase_ref), (flag_hbm.at[pl.ds(0, 128)], flag_ref),
+        (wh_hbm, wh), (wl_hbm, wl), (th_hbm, th), (tl_hbm, tl),
+    )
+    copies = [pltpu.make_async_copy(a, b, sems.at[i]) for i, (a, b) in enumerate(pairs)]
+    for copy in copies:
+        copy.start()
+    for copy in copies[:2]:
+        copy.wait()
+    macro = macro_strain(lax.axis_index("rve"), conn_ref, disp_ref)
+    row = lax.broadcasted_iota(jnp.int32, (8, 128), 0)
+    table = jnp.zeros((8, 128), jnp.float32)
+    for c in range(6):
+        table = jnp.where(row == c, macro[c], table)
+    macro_ref[...] = table
+    for copy in copies[2:5]:
+        copy.wait()
     for plane in range(PLANES):
         elastic = [macro[c] - every_fourth(plastic_ref, c * 128, plane) for c in range(6)]
         phases = every_fourth(phase_ref, 0, plane)
@@ -225,14 +243,16 @@
         stress = material(elastic, phases, flags)[0]
         for c in range(6):
             put_split(xh, xl, pl.ds(c * 32, 32), pl.ds(plane * 128, 128), stress[c])
+    for copy in copies[5:]:
+        copy.wait()
     forward_planes(xh, xl, bh, bl, wh, wl, th, tl, out_ref)
 
 
 def middle_kernel(
-    point_ref, conn_ref, disp_ref, phase_ref, flag_ref, plastic_ref, in_ref,
+    macro_ref, phase_ref, flag_ref, plastic_ref, in_ref,
     vh, vl, uh, ul, wh, wl, th, tl, out_ref, elastic_ref, xh, xl, bh, bl,
 ):
-    macro = macro_strain(point_ref[0], conn_ref, disp_ref)
+    macro = [macro_ref[c : c + 1, :] for c in range(6)]
     correction = backward_planes(in_ref, xh, xl, bh, bl, vh, vl, uh, ul)
     for plane in range(PLANES):
         lanes = slice(plane * 128, (plane + 1) * 128)
@@ -243,7 +263,7 @@
             elastic_ref[c * 32 : (c + 1) * 32, lanes] = after
             elastic.append(after)
         phases = every_fourth(phase_ref, 0, plane)
-        flags = every_fourth(flag_ref, 0, plane)
+        flags = every_fourth(flag_ref, 128, plane)
         stress = material(elastic, phases, flags)[0]
         for c in range(6):
             put_split(xh, xl, pl.ds(c * 32, 32), pl.ds(plane * 128, 128), stress[c])
@@ -268,7 +288,7 @@
             for c in range(6)
         ]
         phases = every_fourth(phase_ref, 0, plane)
-        flags = every_fourth(flag_ref, 0, plane)
+        flags = every_fourth(flag_ref, 256, plane)
         stress, trial, softening, weight = material(elastic, phases, flags)
         for c in range(6):
             collect(c, stress[c])
@@ -295,15 +315,15 @@
             if a != b:
                 lines = place(OUTER_AT + 6 * b + a, totals[at])
             at += 1
-    ones = jnp.ones((8, 128), jnp.float32)
+    ones = jnp.ones((SLABS, 128), jnp.float32)
     line = lax.dot_general(
         ones, lines, (((1,), (1,)), ((), ())),
         precision=lax.Precision.HIGHEST, preferred_element_type=jnp.float32,
     )
-    out_ref[...] = jnp.broadcast_to(line[None], out_ref.shape)
-
-
-def column_kernel(slab_ref, in_ref, th, tl, bh_table, bl_table, twist_ref, four, fourback, out_ref, bh, bl, yh, yl):
+    out_ref[...] = line.reshape(SLABS, 1, 128)
+
+
+def column_kernel(in_ref, th, tl, bh_table, bl_table, twist_ref, four, fourback, out_ref, bh, bl, yh, yl):
     load_columns(in_ref, bh, bl)
     mixed = table_by_data(th[...], tl[...], bh[...], bl[...])
     cosine, sine = twist_ref[0], twist_ref[1]
@@ -321,7 +341,7 @@
     lane = lax.broadcasted_iota(jnp.int32, shape, 1)
     lane = lax.bitwise_and(lane, 127)
     kx = 16 * lax.shift_right_logical(lane, 5) + lax.shift_right_logical(row, 2)
-    ky = 4 * slab_ref[0] + lax.bitwise_and(row, 3)
+    ky = 4 * lax.axis_index("slab") + lax.bitwise_and(row, 3)
     kz = lax.bitwise_and(lane, 31)
     half = GRID // 2
     keep = (kx != half) & (ky != half) & (kx + ky + kz > 0)
@@ -356,8 +376,25 @@
         out_ref[:, c * 8 : (c + 1) * 8, :] = result[:, c * 128 : (c + 1) * 128].reshape(16, 8, 128)
 
 
+def totals_kernel(in_ref, all_ref, stress_ref, tangent_ref):
+    line = jnp.sum(in_ref[...].reshape(SLABS, 128), axis=0, keepdims=True)
+    all_ref[...] = jnp.broadcast_to(line[None], all_ref.shape)
+    line = line * (1.0 / VOXELS)
+    stress_ref[...] = line[:, :6]
+    at = lax.broadcasted_iota(jnp.int32, (1, 128), 1) - OUTER_AT
+    a = at // 6
+    b = at - 6 * a
+    both = (a < 3) & (b < 3)
+    shear = jnp.broadcast_to(line[:, 6:7], (1, 128)) * (2.0 * SHEAR_MODULUS)
+    fixed = jnp.where(both, BULK_MODULUS - shear * (1.0 / 3.0), 0.0)
+    fixed = fixed + jnp.where(a == b, shear, 0.0)
+    whole = (fixed - line * jnp.where(b < 3, 1.0, 2.0)) * (1.0 / TANGENT_UNIT)
+    for i in range(6):
+        tangent_ref[i] = whole[:, OUTER_AT + 6 * i : OUTER_AT + 6 * i + 6]
+
+
 def assembly_kernel(points, conn_ref, in_ref, stiffness_ref, forces_ref):
-    sums = in_ref[pl.ds(0, points, stride=8), :] * (1.0 / VOXELS)
+    sums = in_ref[...].reshape(points, 128) * (1.0 / VOXELS)
     shape = (points, 128)
     lane = lax.broadcasted_iota(jnp.int32, shape, 1)
     point = lax.broadcasted_iota(jnp.int32, shape, 0)
@@ -413,20 +450,21 @@
     )
     stiffness_ref[...] = whole[:60, :60]
     line = jnp.sum(force, axis=0, keepdims=True)
-    row24 = lax.broadcasted_iota(jnp.int32, (24, 128), 0)
-    lane24 = lax.broadcasted_iota(jnp.int32, (24, 128), 1)
-    spread = jnp.where(lane24 // 3 == row24, jnp.broadcast_to(line, (24, 128)), 0.0)
+    part8 = lax.broadcasted_iota(jnp.int32, (8, 128), 0)
+    lane8 = lax.broadcasted_iota(jnp.int32, (8, 128), 1)
+    spread = jnp.where(lane8 % 3 == part8, jnp.broadcast_to(line, (8, 128)), 0.0)
     pick_row = lax.broadcasted_iota(jnp.int32, (128, 128), 0)
     pick_col = lax.broadcasted_iota(jnp.int32, (128, 128), 1)
-    pick = (pick_row % 3 == pick_col).astype(jnp.float32)
+    pick = (pick_row // 3 == pick_col).astype(jnp.float32)
     forces = jnp.dot(
         spread, pick, precision=lax.Precision.HIGHEST, preferred_element_type=jnp.float32
     )
-    forces_ref[...] = forces[:20, :3]
+    forces_ref[...] = forces[:3, :20]
 
 
 SMEM = pl.BlockSpec(memory_space=pltpu.SMEM)
 VMEM = pl.BlockSpec(memory_space=pltpu.VMEM)
+HBM = pl.BlockSpec(memory_space=pltpu.HBM)
 BF16 = jnp.bfloat16
 F32 = jnp.float32
 LIMIT = 16 * 1024 * 1024
@@ -455,8 +493,6 @@
 
 def on_device(phase_ids, yield_flags, plastic_strain, displacements, connectivity):
     points = lax.axis_size("rve")
-    point = lax.axis_index("rve").astype(jnp.int32).reshape(1)
-    slab = lax.axis_index("slab").astype(jnp.int32).reshape(1)
 
     def rows(array):
         lead = math.prod(array.shape[:-2])
@@ -482,18 +518,21 @@
 
     block = jax.ShapeDtypeStruct((16, 48, 128), F32)
 
-    def flag_block(evaluation):
-        return flags[evaluation * 128 : (evaluation + 1) * 128]
-
     first = pl.pallas_call(
-        first_kernel, out_shape=block,
-        in_specs=[SMEM] * 3 + [VMEM] * 7, out_specs=VMEM,
-        scratch_shapes=plane_scratch(), compiler_params=params(),
-        cost_estimate=cost(400_000_000, 2_000_000), name="first",
+        first_kernel, out_shape=(block, jax.ShapeDtypeStruct((8, 128), F32)),
+        in_specs=[HBM] * 9, out_specs=(VMEM, VMEM),
+        scratch_shapes=[
+            pltpu.SMEM(connectivity.shape, jnp.int32), pltpu.SMEM(displacements.shape[::-1], F32),
+            pltpu.VMEM((128, 128), jnp.int32), pltpu.VMEM((128, 128), jnp.int32),
+            pltpu.VMEM((768, 128), F32), pltpu.VMEM((512, 512), BF16), pltpu.VMEM((512, 512), BF16),
+            pltpu.VMEM((128, 128), BF16), pltpu.VMEM((128, 128), BF16),
+            pltpu.SemaphoreType.DMA((9,)), *plane_scratch(),
+        ],
+        compiler_params=params(), cost_estimate=cost(400_000_000, 2_000_000), name="first",
     )
     columns = pl.pallas_call(
         column_kernel, out_shape=block,
-        in_specs=[SMEM] + [VMEM] * 8, out_specs=VMEM,
+        in_specs=[VMEM] * 8, out_specs=VMEM,
         scratch_shapes=[
             pltpu.VMEM((128, 768), BF16), pltpu.VMEM((128, 768), BF16),
             pltpu.VMEM((384, 256), BF16), pltpu.VMEM((384, 256), BF16),
@@ -502,55 +541,50 @@
     )
     middle = pl.pallas_call(
         middle_kernel, out_shape=(block, jax.ShapeDtypeStruct((192, 512), F32)),
-        in_specs=[SMEM] * 3 + [VMEM] * 12, out_specs=(VMEM, VMEM),
+        in_specs=[VMEM] * 13, out_specs=(VMEM, VMEM),
         scratch_shapes=plane_scratch(), compiler_params=params(),
         cost_estimate=cost(800_000_000, 4_000_000), name="middle",
     )
     last = pl.pallas_call(
-        last_kernel, out_shape=jax.ShapeDtypeStruct((16, 8, 128), F32),
+        last_kernel, out_shape=jax.ShapeDtypeStruct((SLABS, 1, 128), F32),
         in_specs=[VMEM] * 8, out_specs=VMEM,
         scratch_shapes=plane_scratch(), compiler_params=params(),
         cost_estimate=cost(400_000_000, 2_000_000), name="last",
     )
+    totals = pl.pallas_call(
+        totals_kernel,
+        out_shape=(
+            jax.ShapeDtypeStruct((points, 1, 128), F32), jax.ShapeDtypeStruct((1, 6), F32),
+            jax.ShapeDtypeStruct((6, 1, 6), F32),
+        ),
+        in_specs=[VMEM], out_specs=(VMEM, VMEM, VMEM), compiler_params=params(),
+        cost_estimate=cost(10_000, 50_000), name="totals",
+    )
     assembly = pl.pallas_call(
         functools.partial(assembly_kernel, points),
-        out_shape=(jax.ShapeDtypeStruct((60, 60), F32), jax.ShapeDtypeStruct((20, 3), F32)),
+        out_shape=(jax.ShapeDtypeStruct((60, 60), F32), jax.ShapeDtypeStruct((3, 20), F32)),
         in_specs=[SMEM, VMEM], out_specs=(VMEM, VMEM), compiler_params=params(),
         cost_estimate=cost(10_000_000, 200_000), name="assembly",
     )
 
     def apply_columns(array):
         received = exchange(array)
-        return exchange(columns(slab, received, ch, cl, dh, dl, twist, four, fourback))
-
-    spectrum = first(
-        point, connectivity, displacements, phases, flag_block(0), plastic, wh, wl, th, tl
+        return exchange(columns(received, ch, cl, dh, dl, twist, four, fourback))
+
+    operands = (connectivity, displacements.T, phases, flags, plastic, wh, wl, th, tl)
+    spectrum, macro = first(
+        *(pltpu.with_memory_space_constraint(operand, pltpu.HBM) for operand in operands)
     )
     planes = apply_columns(spectrum)
     spectrum, elastic = middle(
-        point, connectivity, displacements, phases, flag_block(1), plastic, planes,
-        vh, vl, uh, ul, wh, wl, th, tl,
+        macro, phases, flags, plastic, planes, vh, vl, uh, ul, wh, wl, th, tl
     )
     planes = apply_columns(spectrum)
-    partial = last(phases, flag_block(2), elastic, planes, vh, vl, uh, ul)
-    sums = jnp.sum(exchange(partial), axis=0)
-    everyone = lax.all_to_all(
-        jnp.broadcast_to(sums[None], (points, 8, 128)), "rve", 0, 0, tiled=True
-    )
-    stiffness, forces = assembly(connectivity, everyone.reshape(points * 8, 128))
-
-    own = sums[0] * (1.0 / VOXELS)
-    mean_stress = own[:6].reshape(1, 6)
-    outer = own[OUTER_AT : OUTER_AT + 36].reshape(6, 6)
-    diagonal = np.array([1.0, 1.0, 1.0, 0.0, 0.0, 0.0])
-    volumetric = diagonal[:, None] * diagonal[None, :]
-    fixed = jnp.asarray(BULK_MODULUS * volumetric / TANGENT_UNIT, F32)
-    turning = (np.eye(6) - volumetric / 3.0) * (2.0 * SHEAR_MODULUS / TANGENT_UNIT)
-    weights = np.asarray(PAIR_WEIGHTS)[None, :] / TANGENT_UNIT
-    tangent = (
-        fixed + own[6] * jnp.asarray(turning, F32) - outer * jnp.asarray(weights, F32)
-    )
-    return (mean_stress, tangent[None], forces, stiffness)
+    partial = last(phases, flags, elastic, planes, vh, vl, uh, ul)
+    everyone, stress, tangent = totals(exchange(partial))
+    everyone = lax.all_to_all(everyone, "rve", 0, 0, tiled=True)
+    stiffness, forces = assembly(connectivity, everyone)
+    return (stress, jnp.transpose(tangent, (1, 0, 2)), forces.T, stiffness)
 
 
 def solution(mesh):

time: 118 us -> 106 us (0.90)
  blocking collectives: 42 us -> 93.1 us
  starting transfers between devices: 31.5 us -> 0 us
  waiting for transfers between devices: 21.5 us -> 0 us
  local copies, waits for them, and re-layouts: 9.26 us -> 0.13 us
    all_to_all x0 -> x1, blocking collectives: none -> 35.1 us  [on_device(): everyone = lax.all_to_all(everyone, 'rve', 0, 0, tiled=True)]
    all_to_all x2 -> x0, starting transfers between devices: 31.5 us -> none  [the longest x1 23.8 us: on_device(): lax.all_to_all(jnp.broadcast_to(sums[None], (points, 8, 128)), 'rve', 0,...]
    all_to_all x2 -> x0, waiting for transfers between devices: 21.5 us -> none  [the longest x1 13.3 us: on_device(): lax.all_to_all(jnp.broadcast_to(sums[None], (points, 8, 128)), 'rve', 0,...]
    all_to_all x4 -> x5, blocking collectives: 42 us -> 58 us  [exchange(): lax.all_to_all(array, 'slab', split_axis=0, concat_axis=0, tiled=True)]
    unnamed x55 -> x38, local copies, waits for them, and re-layouts: 6.93 us -> 0.13 us
    slice x3 -> x0, local copies, waits for them, and re-layouts: 1.59 us -> none  [the longest x1 0.92 us: flag_block(): return flags[evaluation * 128:(evaluation + 1) * 128]]
    pallas_call x6 -> x7, Pallas kernels: 10.9 us -> 11.8 us  [the longest x2 2.82 us: apply_columns(): return exchange(columns(received, ch, cl, dh, dl, twist, four, fourback))]
  transfers between devices with their start and end apart: 2 -> 0, of which waited for: 2 -> 0; matrix products, arithmetic and copies ran while one was open for 2% -> 0% of each run, Pallas kernels for 0% -> 0%
where the time goes in v1:
time: 106 us
  blocking collectives  93.1 us (88%)
  Pallas kernels  11.8 us (11%)
    all_to_all x5, blocking collectives, exchange(): lax.all_to_all(array, 'slab', split_axis=0, concat_axis=0, tiled=True)  58 us
    all_to_all x1, blocking collectives, on_device(): everyone = lax.all_to_all(everyone, 'rve', 0, 0, tiled=True)  35.1 us
    pallas_call x2, Pallas kernels, apply_columns(): return exchange(columns(received, ch, cl, dh, dl, twist, four, fourback))  2.82 us
    pallas_call x1, Pallas kernels, on_device(): stiffness, forces = assembly(connectivity, everyone)  2.76 us
    pallas_call x1, Pallas kernels, on_device(): first(*(pltpu.with_memory_space_constraint(operand, pltpu.HBM) for operan...  2.38 us

profile of v1, /device:TPU:1, one launch (start us, length us, event | category | flops | bytes accessed | tf_op | source)
XLA Modules:
  0.0 105.9 jit_solution(16451999086300925795)
XLA Ops:
  0.6 0.0 copy-start.13
  0.6 0.0 copy-start.14
  0.7 0.0 copy-start.16
  0.7 0.0 copy-start.17
  0.7 0.0 copy-start.18
  0.7 2.4 %first.1 = (f32[16,48,128]{2,1,0:T(8,128)S(1)}, f32[8,128]{1,0:T(8,128)S(1)}) custom-call(s32[4,8]{1,0:T(4,128)} %conn_ref.1, f32[3,20]{1,0:T(4,128)} %bitcast.26, s32[128,128]{1,0:T(8,128)} %bitcast.23, s32[384,128]{1,0:T(8,128)} %bitcast.18, f32[768,128]{1,0:T(8,128)} %bitcast.21, bf16[512,512]{1,0:T(8,128)(2,1)} %constant.30.clone.wh_hbm.wh, ...), custom_call_target="tpu_custom_call" | custom-call | flops 400000000 | bytes 2000000 | tf_op jit(solution)/shard_map/first/pallas_call | solution.py:575
  3.1 0.0 copy-start.12
  3.1 0.0 copy-start.15
  3.1 0.0 copy-start.4
  3.1 0.0 copy-start.5
  3.1 0.0 copy-start.10
  3.1 16.0 %all_to_all.30.in_ref = f32[16,48,128]{2,1,0:T(8,128)S(1)} all-to-all(f32[16,48,128]{2,1,0:T(8,128)S(1)} %get-tuple-element.14), channel_id=1, replica_groups=mesh['rve'=32,'slab'=16] {'slab'}, dimensions={0} | all-to-all | bytes 786432 | tf_op jit(solution)/shard_map/all_to_all | solution.py:491
  19.1 0.0 copy-done.13
  19.1 0.0 copy-done.14
  19.1 0.0 copy-done.16
  19.1 0.0 copy-done.17
  19.2 0.0 copy-done.18
  19.2 0.0 copy-done.12
  19.2 0.0 copy-done.15
  19.2 0.0 copy-start.1
  19.2 0.0 copy-start.2
  19.2 0.0 copy-start.3
  19.2 1.4 %columns.2 = f32[16,48,128]{2,1,0:T(8,128)S(1)} custom-call(f32[16,48,128]{2,1,0:T(8,128)S(1)} %all_to_all.30.in_ref, bf16[128,128]{1,0:T(8,128)(2,1)S(1)} %copy-done.18, bf16[128,128]{1,0:T(8,128)(2,1)S(1)} %copy-done.17, bf16[128,128]{1,0:T(8,128)(2,1)S(1)} %copy-done.16, bf16[128,128]{1,0:T(8,128)(2,1)S(1)} %copy-done.15, f32[2,64,128]{2,1,0:T(8,128)S(1)} %copy-done.14, ...), custom_call_target="tpu_custom_call" | custom-call | flops 400000000 | bytes 2000000 | tf_op jit(solution)/shard_map/columns/pallas_call | solution.py:572
  20.6 0.0 copy-start
  20.6 0.0 copy-start.6
  20.7 0.0 copy-start.7
  20.7 0.0 copy-start.8
  20.7 0.0 copy-start.9
  20.7 11.2 %all_to_all.31.in_ref = f32[16,48,128]{2,1,0:T(8,128)S(1)} all-to-all(f32[16,48,128]{2,1,0:T(8,128)S(1)} %columns.2), channel_id=1, replica_groups=mesh['rve'=32,'slab'=16] {'slab'}, dimensions={0} | all-to-all | bytes 786432 | tf_op jit(solution)/shard_map/all_to_all | solution.py:491
  31.9 0.0 copy-done.4
  31.9 0.0 copy-done.1
  31.9 0.0 copy-done.2
  31.9 0.0 copy-done.3
  31.9 0.0 copy-done
  32.0 0.0 copy-done.6
  32.0 0.0 copy-done.7
  32.0 0.0 copy-done.8
  32.0 0.0 copy-done.9
  32.0 1.8 %middle.1 = (f32[16,48,128]{2,1,0:T(8,128)S(1)}, f32[192,512]{1,0:T(8,128)S(1)}) custom-call(f32[8,128]{1,0:T(8,128)S(1)} %get-tuple-element.13.macro_ref, s32[128,128]{1,0:T(8,128)S(1)} %bitcast.24, s32[384,128]{1,0:T(8,128)S(1)} %bitcast.19, f32[768,128]{1,0:T(8,128)S(1)} %bitcast.22, f32[16,48,128]{2,1,0:T(8,128)S(1)} %all_to_all.31.in_ref, ...), custom_call_target="tpu_custom_call" | custom-call | flops 800000000 | bytes 4000000 | tf_op jit(solution)/shard_map/middle/pallas_call | solution.py:579
  33.8 10.9 %all_to_all.32.in_ref = f32[16,48,128]{2,1,0:T(8,128)S(1)} all-to-all(f32[16,48,128]{2,1,0:T(8,128)S(1)} %get-tuple-element.16), channel_id=1, replica_groups=mesh['rve'=32,'slab'=16] {'slab'}, dimensions={0} | all-to-all | bytes 786432 | tf_op jit(solution)/shard_map/all_to_all | solution.py:491
  44.7 1.4 %columns.3 = f32[16,48,128]{2,1,0:T(8,128)S(1)} custom-call(f32[16,48,128]{2,1,0:T(8,128)S(1)} %all_to_all.32.in_ref, bf16[128,128]{1,0:T(8,128)(2,1)S(1)} %copy-done.18, bf16[128,128]{1,0:T(8,128)(2,1)S(1)} %copy-done.17, bf16[128,128]{1,0:T(8,128)(2,1)S(1)} %copy-done.16, bf16[128,128]{1,0:T(8,128)(2,1)S(1)} %copy-done.15, f32[2,64,128]{2,1,0:T(8,128)S(1)} %copy-done.14, ...), custom_call_target="tpu_custom_call" | custom-call | flops 400000000 | bytes 2000000 | tf_op jit(solution)/shard_map/columns/pallas_call | solution.py:572
  46.1 10.9 %all_to_all.33.in_ref = f32[16,48,128]{2,1,0:T(8,128)S(1)} all-to-all(f32[16,48,128]{2,1,0:T(8,128)S(1)} %columns.3), channel_id=1, replica_groups=mesh['rve'=32,'slab'=16] {'slab'}, dimensions={0} | all-to-all | bytes 786432 | tf_op jit(solution)/shard_map/all_to_all | solution.py:491
  56.9 1.2 %last.1 = f32[16,1,128]{2,1,0:T(1,128)S(1)} custom-call(s32[128,128]{1,0:T(8,128)S(1)} %bitcast.25, s32[384,128]{1,0:T(8,128)S(1)} %bitcast.20, f32[192,512]{1,0:T(8,128)S(1)} %get-tuple-element.15.elastic_ref, f32[16,48,128]{2,1,0:T(8,128)S(1)} %all_to_all.33.in_ref, bf16[512,512]{1,0:T(8,128)(2,1)S(1)} %copy-done.3, bf16[512,512]{1,0:T(8,128)(2,1)S(1)} %copy-done.2, ...), custom_call_target="tpu_custom_call" | custom-call | flops 400000000 | bytes 2000000 | tf_op jit(solution)/shard_map/last/pallas_call | solution.py:583
  58.2 9.1 %all_to_all.34.in_ref = f32[16,1,128]{2,1,0:T(1,128)S(1)} all-to-all(f32[16,1,128]{2,1,0:T(1,128)S(1)} %last.1), channel_id=1, replica_groups=mesh['rve'=32,'slab'=16] {'slab'}, dimensions={0} | all-to-all | bytes 16384 | tf_op jit(solution)/shard_map/all_to_all | solution.py:491
  67.3 0.7 totals.1
  68.0 35.1 %all_to_all.35.in_ref = f32[32,1,128]{2,1,0:T(1,128)S(1)} all-to-all(f32[32,1,128]{2,1,0:T(1,128)S(1)} %get-tuple-element.19), channel_id=1, replica_groups=mesh['rve'=32,'slab'=16] {'rve'}, dimensions={0} | all-to-all | bytes 32768 | tf_op jit(solution)/shard_map/all_to_all | solution.py:585
  103.1 0.0 copy-done.11
  103.1 2.8 %assembly.1 = (f32[60,60]{1,0:T(8,128)}, f32[3,20]{1,0:T(4,128)}) custom-call(s32[4,8]{1,0:T(4,128)S(1)} %copy-done.11, f32[32,1,128]{2,1,0:T(1,128)S(1)} %all_to_all.35.in_ref), custom_call_target="tpu_custom_call" | custom-call | flops 10000000 | bytes 200000 | tf_op jit(solution)/shard_map/assembly/pallas_call | solution.py:586
  (3 shorter events, 0.0 us)
Async XLA Ops:
  0.6 18.5 %copy-start.13 = (bf16[256,256]{1,0:T(8,128)(2,1)S(1)}, bf16[256,256]{1,0:T(8,128)(2,1)}, u32[]{:S(2)}) copy-start(bf16[256,256]{1,0:T(8,128)(2,1)} %constant.43.clone.four) | copy-start | bytes 393220
  0.6 18.5 %copy-start.14 = (f32[2,64,128]{2,1,0:T(8,128)S(1)}, f32[2,64,128]{2,1,0:T(8,128)}, u32[]{:S(2)}) copy-start(f32[2,64,128]{2,1,0:T(8,128)} %constant.42.clone.twist_ref) | copy-start | bytes 196612
  0.7 18.5 %copy-start.16 = (bf16[128,128]{1,0:T(8,128)(2,1)S(1)}, bf16[128,128]{1,0:T(8,128)(2,1)}, u32[]{:S(2)}) copy-start(bf16[128,128]{1,0:T(8,128)(2,1)} %constant.40.clone.bh_table) | copy-start | bytes 98308
  0.7 18.5 %copy-start.17 = (bf16[128,128]{1,0:T(8,128)(2,1)S(1)}, bf16[128,128]{1,0:T(8,128)(2,1)}, u32[]{:S(2)}) copy-start(bf16[128,128]{1,0:T(8,128)(2,1)} %constant.39.clone.tl) | copy-start | bytes 98308
  0.7 18.5 %copy-start.18 = (bf16[128,128]{1,0:T(8,128)(2,1)S(1)}, bf16[128,128]{1,0:T(8,128)(2,1)}, u32[]{:S(2)}) copy-start(bf16[128,128]{1,0:T(8,128)(2,1)} %constant.38.clone.th) | copy-start | bytes 98308
  3.1 16.1 %copy-start.12 = (bf16[256,256]{1,0:T(8,128)(2,1)S(1)}, bf16[256,256]{1,0:T(8,128)(2,1)}, u32[]{:S(2)}) copy-start(bf16[256,256]{1,0:T(8,128)(2,1)} %constant.44.clone.fourback) | copy-start | bytes 393220
  3.1 16.1 %copy-start.15 = (bf16[128,128]{1,0:T(8,128)(2,1)S(1)}, bf16[128,128]{1,0:T(8,128)(2,1)}, u32[]{:S(2)}) copy-start(bf16[128,128]{1,0:T(8,128)(2,1)} %constant.41.clone.bl_table) | copy-start | bytes 98308
  3.1 28.8 %copy-start.4 = (s32[1,3,4,4096]{3,2,1,0:T(4,128)S(1)}, s32[1,3,4,4096]{3,2,1,0:T(4,128)}, u32[]{:S(2)}) copy-start(s32[1,3,4,4096]{3,2,1,0:T(4,128)} %param.21) | copy-start | bytes 589828
  3.1 28.8 %copy-start.5 = (f32[1,6,4,4096]{3,2,1,0:T(4,128)S(1)}, f32[1,6,4,4096]{3,2,1,0:T(4,128)}, u32[]{:S(2)}) copy-start(f32[1,6,4,4096]{3,2,1,0:T(4,128)} %param.22) | copy-start | bytes 1179652
  3.1 28.8 %copy-start.10 = (bf16[128,128]{1,0:T(8,128)(2,1)S(1)}, bf16[128,128]{1,0:T(8,128)(2,1)}, u32[]{:S(2)}) copy-start(bf16[128,128]{1,0:T(8,128)(2,1)} %constant.34.clone.th_hbm.th) | copy-start | bytes 98308
  19.2 12.7 %copy-start.1 = (bf16[512,512]{1,0:T(8,128)(2,1)S(1)}, bf16[512,512]{1,0:T(8,128)(2,1)}, u32[]{:S(2)}) copy-start(bf16[512,512]{1,0:T(8,128)(2,1)} %constant.30.clone.wh_hbm.wh) | copy-start | bytes 1572868
  19.2 12.7 %copy-start.2 = (bf16[512,512]{1,0:T(8,128)(2,1)S(1)}, bf16[512,512]{1,0:T(8,128)(2,1)}, u32[]{:S(2)}) copy-start(bf16[512,512]{1,0:T(8,128)(2,1)} %constant.33.clone.vl) | copy-start | bytes 1572868
  19.2 12.7 %copy-start.3 = (bf16[512,512]{1,0:T(8,128)(2,1)S(1)}, bf16[512,512]{1,0:T(8,128)(2,1)}, u32[]{:S(2)}) copy-start(bf16[512,512]{1,0:T(8,128)(2,1)} %constant.32.clone.vh) | copy-start | bytes 1572868
  20.6 11.3 %copy-start = (bf16[512,512]{1,0:T(8,128)(2,1)S(1)}, bf16[512,512]{1,0:T(8,128)(2,1)}, u32[]{:S(2)}) copy-start(bf16[512,512]{1,0:T(8,128)(2,1)} %constant.31.clone.wl_hbm.wl) | copy-start | bytes 1572868
  20.6 11.3 %copy-start.6 = (s32[4,4096]{1,0:T(4,128)S(1)}, s32[4,4096]{1,0:T(4,128)}, u32[]{:S(2)}) copy-start(s32[4,4096]{1,0:T(4,128)} %param.20) | copy-start | bytes 196612
  20.7 11.3 %copy-start.7 = (bf16[128,128]{1,0:T(8,128)(2,1)S(1)}, bf16[128,128]{1,0:T(8,128)(2,1)}, u32[]{:S(2)}) copy-start(bf16[128,128]{1,0:T(8,128)(2,1)} %constant.37.clone.ul) | copy-start | bytes 98308
  20.7 11.3 %copy-start.8 = (bf16[128,128]{1,0:T(8,128)(2,1)S(1)}, bf16[128,128]{1,0:T(8,128)(2,1)}, u32[]{:S(2)}) copy-start(bf16[128,128]{1,0:T(8,128)(2,1)} %constant.36.clone.uh) | copy-start | bytes 98308
  20.7 11.3 %copy-start.9 = (bf16[128,128]{1,0:T(8,128)(2,1)S(1)}, bf16[128,128]{1,0:T(8,128)(2,1)}, u32[]{:S(2)}) copy-start(bf16[128,128]{1,0:T(8,128)(2,1)} %constant.35.clone.tl_hbm.tl) | copy-start | bytes 98308
  68.0 35.1 %copy-start.11 = (s32[4,8]{1,0:T(4,128)S(1)}, s32[4,8]{1,0:T(4,128)}, u32[]{:S(2)}) copy-start(s32[4,8]{1,0:T(4,128)} %conn_ref.1) | copy-start | bytes 388

commit v2 on v1

--- a/solution.py
+++ b/solution.py
@@ -394,7 +394,9 @@
 
 
 def assembly_kernel(points, conn_ref, in_ref, stiffness_ref, forces_ref):
+    half = points // 2
     sums = in_ref[...].reshape(points, 128) * (1.0 / VOXELS)
+    sums = jnp.concatenate([sums[half:], sums[:half]], axis=0)
     shape = (points, 128)
     lane = lax.broadcasted_iota(jnp.int32, shape, 1)
     point = lax.broadcasted_iota(jnp.int32, shape, 0)
@@ -582,7 +584,11 @@
     planes = apply_columns(spectrum)
     partial = last(phases, flags, elastic, planes, vh, vl, uh, ul)
     everyone, stress, tangent = totals(exchange(partial))
-    everyone = lax.all_to_all(everyone, "rve", 0, 0, tiled=True)
+    half = points // 2
+    turned = [*range(half, points), *range(half)]
+    everyone = lax.all_to_all(
+        everyone, "rve", 0, 0, tiled=True, axis_index_groups=[turned]
+    )
     stiffness, forces = assembly(connectivity, everyone)
     return (stress, jnp.transpose(tangent, (1, 0, 2)), forces.T, stiffness)
 

time: 106 us -> 99 us (0.934)
  blocking collectives: 93.1 us -> 86.8 us
  Pallas kernels: 11.8 us -> 10.7 us
    all_to_all x1, blocking collectives: 35.1 us -> 28.9 us  [on_device(): lax.all_to_all(everyone, 'rve', 0, 0, tiled=True, axis_index_groups=[turn...]
where the time goes in v2:
time: 99 us; the launch traced here: 98.6 us
  blocking collectives  86.8 us (88%)
  Pallas kernels  10.7 us (11%)
    all_to_all x5, blocking collectives, exchange(): lax.all_to_all(array, 'slab', split_axis=0, concat_axis=0, tiled=True)  58 us
    all_to_all x1, blocking collectives, on_device(): lax.all_to_all(everyone, 'rve', 0, 0, tiled=True, axis_index_groups=[turn...  28.9 us
    pallas_call x2, Pallas kernels, apply_columns(): return exchange(columns(received, ch, cl, dh, dl, twist, four, fourback))  2.82 us
    pallas_call x1, Pallas kernels, on_device(): first(*(pltpu.with_memory_space_constraint(operand, pltpu.HBM) for operan...  2.38 us

profile of v2, /device:TPU:1, one launch (start us, length us, event | category | flops | bytes accessed | tf_op | source)
XLA Modules:
  0.0 98.6 jit_solution(15994626832479734515)
XLA Ops:
  0.6 0.0 copy-start.13
  0.6 0.0 copy-start.14
  0.7 0.0 copy-start.16
  0.7 0.0 copy-start.17
  0.7 0.0 copy-start.18
  0.7 2.4 %first.1 = (f32[16,48,128]{2,1,0:T(8,128)S(1)}, f32[8,128]{1,0:T(8,128)S(1)}) custom-call(s32[4,8]{1,0:T(4,128)} %conn_ref.1, f32[3,20]{1,0:T(4,128)} %bitcast.26, s32[128,128]{1,0:T(8,128)} %bitcast.23, s32[384,128]{1,0:T(8,128)} %bitcast.18, f32[768,128]{1,0:T(8,128)} %bitcast.21, bf16[512,512]{1,0:T(8,128)(2,1)} %constant.30.clone.wh_hbm.wh, ...), custom_call_target="tpu_custom_call" | custom-call | flops 400000000 | bytes 2000000 | tf_op jit(solution)/shard_map/first/pallas_call | solution.py:577
  3.1 0.0 copy-start.12
  3.1 0.0 copy-start.15
  3.1 0.0 copy-start.4
  3.1 0.0 copy-start.5
  3.1 0.0 copy-start.10
  3.1 16.0 %all_to_all.30.in_ref = f32[16,48,128]{2,1,0:T(8,128)S(1)} all-to-all(f32[16,48,128]{2,1,0:T(8,128)S(1)} %get-tuple-element.14), channel_id=1, replica_groups=mesh['rve'=32,'slab'=16] {'slab'}, dimensions={0} | all-to-all | bytes 786432 | tf_op jit(solution)/shard_map/all_to_all | solution.py:493
  19.1 0.0 copy-done.13
  19.1 0.0 copy-done.14
  19.1 0.0 copy-done.16
  19.1 0.0 copy-done.17
  19.2 0.0 copy-done.18
  19.2 0.0 copy-done.12
  19.2 0.0 copy-done.15
  19.2 0.0 copy-start.1
  19.2 0.0 copy-start.2
  19.2 0.0 copy-start.3
  19.2 1.4 %columns.2 = f32[16,48,128]{2,1,0:T(8,128)S(1)} custom-call(f32[16,48,128]{2,1,0:T(8,128)S(1)} %all_to_all.30.in_ref, bf16[128,128]{1,0:T(8,128)(2,1)S(1)} %copy-done.18, bf16[128,128]{1,0:T(8,128)(2,1)S(1)} %copy-done.17, bf16[128,128]{1,0:T(8,128)(2,1)S(1)} %copy-done.16, bf16[128,128]{1,0:T(8,128)(2,1)S(1)} %copy-done.15, f32[2,64,128]{2,1,0:T(8,128)S(1)} %copy-done.14, ...), custom_call_target="tpu_custom_call" | custom-call | flops 400000000 | bytes 2000000 | tf_op jit(solution)/shard_map/columns/pallas_call | solution.py:574
  20.6 0.0 copy-start
  20.6 0.0 copy-start.6
  20.7 0.0 copy-start.7
  20.7 0.0 copy-start.8
  20.7 0.0 copy-start.9
  20.7 11.2 %all_to_all.31.in_ref = f32[16,48,128]{2,1,0:T(8,128)S(1)} all-to-all(f32[16,48,128]{2,1,0:T(8,128)S(1)} %columns.2), channel_id=1, replica_groups=mesh['rve'=32,'slab'=16] {'slab'}, dimensions={0} | all-to-all | bytes 786432 | tf_op jit(solution)/shard_map/all_to_all | solution.py:493
  31.9 0.0 copy-done.4
  31.9 0.0 copy-done.5
  31.9 0.0 copy-done.10
  31.9 0.0 copy-done.1
  31.9 0.0 copy-done.2
  31.9 0.0 copy-done.3
  31.9 0.0 copy-done
  32.0 0.0 copy-done.6
  32.0 0.0 copy-done.7
  32.0 0.0 copy-done.8
  32.0 1.8 %middle.1 = (f32[16,48,128]{2,1,0:T(8,128)S(1)}, f32[192,512]{1,0:T(8,128)S(1)}) custom-call(f32[8,128]{1,0:T(8,128)S(1)} %get-tuple-element.13.macro_ref, s32[128,128]{1,0:T(8,128)S(1)} %bitcast.24, s32[384,128]{1,0:T(8,128)S(1)} %bitcast.19, f32[768,128]{1,0:T(8,128)S(1)} %bitcast.22, f32[16,48,128]{2,1,0:T(8,128)S(1)} %all_to_all.31.in_ref, ...), custom_call_target="tpu_custom_call" | custom-call | flops 800000000 | bytes 4000000 | tf_op jit(solution)/shard_map/middle/pallas_call | solution.py:581
  33.8 10.9 %all_to_all.32.in_ref = f32[16,48,128]{2,1,0:T(8,128)S(1)} all-to-all(f32[16,48,128]{2,1,0:T(8,128)S(1)} %get-tuple-element.16), channel_id=1, replica_groups=mesh['rve'=32,'slab'=16] {'slab'}, dimensions={0} | all-to-all | bytes 786432 | tf_op jit(solution)/shard_map/all_to_all | solution.py:493
  44.7 1.4 %columns.3 = f32[16,48,128]{2,1,0:T(8,128)S(1)} custom-call(f32[16,48,128]{2,1,0:T(8,128)S(1)} %all_to_all.32.in_ref, bf16[128,128]{1,0:T(8,128)(2,1)S(1)} %copy-done.18, bf16[128,128]{1,0:T(8,128)(2,1)S(1)} %copy-done.17, bf16[128,128]{1,0:T(8,128)(2,1)S(1)} %copy-done.16, bf16[128,128]{1,0:T(8,128)(2,1)S(1)} %copy-done.15, f32[2,64,128]{2,1,0:T(8,128)S(1)} %copy-done.14, ...), custom_call_target="tpu_custom_call" | custom-call | flops 400000000 | bytes 2000000 | tf_op jit(solution)/shard_map/columns/pallas_call | solution.py:574
  46.1 10.9 %all_to_all.33.in_ref = f32[16,48,128]{2,1,0:T(8,128)S(1)} all-to-all(f32[16,48,128]{2,1,0:T(8,128)S(1)} %columns.3), channel_id=1, replica_groups=mesh['rve'=32,'slab'=16] {'slab'}, dimensions={0} | all-to-all | bytes 786432 | tf_op jit(solution)/shard_map/all_to_all | solution.py:493
  56.9 1.2 %last.1 = f32[16,1,128]{2,1,0:T(1,128)S(1)} custom-call(s32[128,128]{1,0:T(8,128)S(1)} %bitcast.25, s32[384,128]{1,0:T(8,128)S(1)} %bitcast.20, f32[192,512]{1,0:T(8,128)S(1)} %get-tuple-element.15.elastic_ref, f32[16,48,128]{2,1,0:T(8,128)S(1)} %all_to_all.33.in_ref, bf16[512,512]{1,0:T(8,128)(2,1)S(1)} %copy-done.3, bf16[512,512]{1,0:T(8,128)(2,1)S(1)} %copy-done.2, ...), custom_call_target="tpu_custom_call" | custom-call | flops 400000000 | bytes 2000000 | tf_op jit(solution)/shard_map/last/pallas_call | solution.py:585
  58.2 9.1 %all_to_all.34.in_ref = f32[16,1,128]{2,1,0:T(1,128)S(1)} all-to-all(f32[16,1,128]{2,1,0:T(1,128)S(1)} %last.1), channel_id=1, replica_groups=mesh['rve'=32,'slab'=16] {'slab'}, dimensions={0} | all-to-all | bytes 16384 | tf_op jit(solution)/shard_map/all_to_all | solution.py:493
  67.3 0.7 totals.1
  68.0 28.9 %all_to_all.35.in_ref = f32[32,1,128]{2,1,0:T(1,128)S(1)} all-to-all(f32[32,1,128]{2,1,0:T(1,128)S(1)} %get-tuple-element.19), channel_id=1, replica_groups={{256,272,288,304,320,336,352,368,384,400,416,432,448,464,480,496,0,16,3..., dimensions={0} | all-to-all | bytes 32768 | tf_op jit(solution)/shard_map/all_to_all | solution.py:589
  96.9 1.7 %assembly.1 = (f32[60,60]{1,0:T(8,128)}, f32[3,20]{1,0:T(4,128)}) custom-call(s32[4,8]{1,0:T(4,128)S(1)} %copy-done.11, f32[32,1,128]{2,1,0:T(1,128)S(1)} %all_to_all.35.in_ref), custom_call_target="tpu_custom_call" | custom-call | flops 10000000 | bytes 200000 | tf_op jit(solution)/shard_map/assembly/pallas_call | solution.py:592
  (3 shorter events, 0.0 us)
Async XLA Ops:
  0.6 18.5 %copy-start.13 = (bf16[256,256]{1,0:T(8,128)(2,1)S(1)}, bf16[256,256]{1,0:T(8,128)(2,1)}, u32[]{:S(2)}) copy-start(bf16[256,256]{1,0:T(8,128)(2,1)} %constant.43.clone.four) | copy-start | bytes 393220
  0.6 18.5 %copy-start.14 = (f32[2,64,128]{2,1,0:T(8,128)S(1)}, f32[2,64,128]{2,1,0:T(8,128)}, u32[]{:S(2)}) copy-start(f32[2,64,128]{2,1,0:T(8,128)} %constant.42.clone.twist_ref) | copy-start | bytes 196612
  0.7 18.5 %copy-start.16 = (bf16[128,128]{1,0:T(8,128)(2,1)S(1)}, bf16[128,128]{1,0:T(8,128)(2,1)}, u32[]{:S(2)}) copy-start(bf16[128,128]{1,0:T(8,128)(2,1)} %constant.40.clone.bh_table) | copy-start | bytes 98308
  0.7 18.5 %copy-start.17 = (bf16[128,128]{1,0:T(8,128)(2,1)S(1)}, bf16[128,128]{1,0:T(8,128)(2,1)}, u32[]{:S(2)}) copy-start(bf16[128,128]{1,0:T(8,128)(2,1)} %constant.39.clone.tl) | copy-start | bytes 98308
  0.7 18.5 %copy-start.18 = (bf16[128,128]{1,0:T(8,128)(2,1)S(1)}, bf16[128,128]{1,0:T(8,128)(2,1)}, u32[]{:S(2)}) copy-start(bf16[128,128]{1,0:T(8,128)(2,1)} %constant.38.clone.th) | copy-start | bytes 98308
  3.1 16.1 %copy-start.12 = (bf16[256,256]{1,0:T(8,128)(2,1)S(1)}, bf16[256,256]{1,0:T(8,128)(2,1)}, u32[]{:S(2)}) copy-start(bf16[256,256]{1,0:T(8,128)(2,1)} %constant.44.clone.fourback) | copy-start | bytes 393220
  3.1 16.1 %copy-start.15 = (bf16[128,128]{1,0:T(8,128)(2,1)S(1)}, bf16[128,128]{1,0:T(8,128)(2,1)}, u32[]{:S(2)}) copy-start(bf16[128,128]{1,0:T(8,128)(2,1)} %constant.41.clone.bl_table) | copy-start | bytes 98308
  3.1 28.8 %copy-start.4 = (s32[1,3,4,4096]{3,2,1,0:T(4,128)S(1)}, s32[1,3,4,4096]{3,2,1,0:T(4,128)}, u32[]{:S(2)}) copy-start(s32[1,3,4,4096]{3,2,1,0:T(4,128)} %param.21) | copy-start | bytes 589828
  3.1 28.8 %copy-start.5 = (f32[1,6,4,4096]{3,2,1,0:T(4,128)S(1)}, f32[1,6,4,4096]{3,2,1,0:T(4,128)}, u32[]{:S(2)}) copy-start(f32[1,6,4,4096]{3,2,1,0:T(4,128)} %param.22) | copy-start | bytes 1179652
  3.1 28.8 %copy-start.10 = (bf16[128,128]{1,0:T(8,128)(2,1)S(1)}, bf16[128,128]{1,0:T(8,128)(2,1)}, u32[]{:S(2)}) copy-start(bf16[128,128]{1,0:T(8,128)(2,1)} %constant.34.clone.th_hbm.th) | copy-start | bytes 98308
  19.2 12.7 %copy-start.1 = (bf16[512,512]{1,0:T(8,128)(2,1)S(1)}, bf16[512,512]{1,0:T(8,128)(2,1)}, u32[]{:S(2)}) copy-start(bf16[512,512]{1,0:T(8,128)(2,1)} %constant.30.clone.wh_hbm.wh) | copy-start | bytes 1572868
  19.2 12.7 %copy-start.2 = (bf16[512,512]{1,0:T(8,128)(2,1)S(1)}, bf16[512,512]{1,0:T(8,128)(2,1)}, u32[]{:S(2)}) copy-start(bf16[512,512]{1,0:T(8,128)(2,1)} %constant.33.clone.vl) | copy-start | bytes 1572868
  19.2 12.7 %copy-start.3 = (bf16[512,512]{1,0:T(8,128)(2,1)S(1)}, bf16[512,512]{1,0:T(8,128)(2,1)}, u32[]{:S(2)}) copy-start(bf16[512,512]{1,0:T(8,128)(2,1)} %constant.32.clone.vh) | copy-start | bytes 1572868
  20.6 11.3 %copy-start = (bf16[512,512]{1,0:T(8,128)(2,1)S(1)}, bf16[512,512]{1,0:T(8,128)(2,1)}, u32[]{:S(2)}) copy-start(bf16[512,512]{1,0:T(8,128)(2,1)} %constant.31.clone.wl_hbm.wl) | copy-start | bytes 1572868
  20.6 11.3 %copy-start.6 = (s32[4,4096]{1,0:T(4,128)S(1)}, s32[4,4096]{1,0:T(4,128)}, u32[]{:S(2)}) copy-start(s32[4,4096]{1,0:T(4,128)} %param.20) | copy-start | bytes 196612
  20.7 11.3 %copy-start.7 = (bf16[128,128]{1,0:T(8,128)(2,1)S(1)}, bf16[128,128]{1,0:T(8,128)(2,1)}, u32[]{:S(2)}) copy-start(bf16[128,128]{1,0:T(8,128)(2,1)} %constant.37.clone.ul) | copy-start | bytes 98308
  20.7 11.3 %copy-start.8 = (bf16[128,128]{1,0:T(8,128)(2,1)S(1)}, bf16[128,128]{1,0:T(8,128)(2,1)}, u32[]{:S(2)}) copy-start(bf16[128,128]{1,0:T(8,128)(2,1)} %constant.36.clone.uh) | copy-start | bytes 98308
  20.7 11.3 %copy-start.9 = (bf16[128,128]{1,0:T(8,128)(2,1)S(1)}, bf16[128,128]{1,0:T(8,128)(2,1)}, u32[]{:S(2)}) copy-start(bf16[128,128]{1,0:T(8,128)(2,1)} %constant.35.clone.tl_hbm.tl) | copy-start | bytes 98308
  68.0 28.9 %copy-start.11 = (s32[4,8]{1,0:T(4,128)S(1)}, s32[4,8]{1,0:T(4,128)}, u32[]{:S(2)}) copy-start(s32[4,8]{1,0:T(4,128)} %conn_ref.1) | copy-start | bytes 388

commit v3 on v2

v3 whole, which is shorter than its diff:
```python
import functools
import math

import jax
import jax.numpy as jnp
import ml_dtypes
import numpy as np
from jax import lax
from jax.experimental import pallas as pl
from jax.experimental.pallas import tpu as pltpu
from jax.sharding import PartitionSpec as P

GRID = 64
ITERS = 2
SLABS = 16
PLANES = GRID // SLABS
KEPT = GRID // 2

SHEAR_MODULUS = 80.0
BULK_MODULUS = 160.0
REFERENCE_SHEAR = 80.0
REFERENCE_LAME = 160.0 - 160.0 / 3.0
TANGENT_UNIT = 100.0
QUADRATURE_WEIGHT = 0.125
PAIR_WEIGHTS = (1.0, 1.0, 1.0, 2.0, 2.0, 2.0)
TENSOR_PAIRS = ((0, 0), (1, 1), (2, 2), (1, 2), (0, 2), (0, 1))
VOXELS = float(GRID**3)
GAUSS_LOW = 0.5 - 0.5 / math.sqrt(3.0)
GAUSS_HIGH = 0.5 + 0.5 / math.sqrt(3.0)
OUTER_AT = 8
FIELDS = 5


def halves(table):
    high = table.astype(np.float32).astype(ml_dtypes.bfloat16)
    low = (table - high.astype(np.float64)).astype(np.float32).astype(ml_dtypes.bfloat16)
    return high, low


def depth_tables():
    z = np.arange(GRID)
    k = np.arange(KEPT)
    theta = 2.0 * np.pi * np.outer(z, k) / GRID
    forward = np.stack([np.cos(theta), -np.sin(theta)], axis=0)
    weight = np.where(k == 0, 1.0, 2.0) / VOXELS
    inverse = forward * weight[None, None, :]
    pair = np.eye(2)
    there = np.einsum("rR,pzk->rzRpk", pair, forward)
    back = np.einsum("rR,pzk->Rpkrz", pair, inverse)
    return there.reshape(128, 128), back.reshape(128, 128)


def row_tables():
    y = 2 * np.arange(32)[None, :] + np.arange(2)[:, None]
    ky = 4 * np.arange(16)[:, None] + np.arange(4)[None, :]
    theta = 2.0 * np.pi * np.einsum("de,rm->derm", ky, y) / GRID
    c, s = np.cos(theta), np.sin(theta)
    there = np.zeros((16, 2, 4, 2, 2, 32))
    there[:, 0, :, :, 0, :] = c
    there[:, 0, :, :, 1, :] = s
    there[:, 1, :, :, 0, :] = -s
    there[:, 1, :, :, 1, :] = c
    back = np.zeros((2, 2, 32, 16, 2, 4))
    ct, st = np.einsum("derm->rmde", c), np.einsum("derm->rmde", s)
    back[:, 0, :, :, 0, :] = ct
    back[:, 0, :, :, 1, :] = -st
    back[:, 1, :, :, 0, :] = st
    back[:, 1, :, :, 1, :] = ct
    return there.reshape(128, 128), back.reshape(128, 128)


def column_tables():
    d = np.arange(16)
    theta = 2.0 * np.pi * np.outer(d, d) / 16.0
    c, s = np.cos(theta), np.sin(theta)
    same = np.eye(4)
    there = np.zeros((2, 16, 4, 16, 2, 4))
    there[0, :, :, :, 0, :] = np.einsum("bd,ef->bedf", c, same)
    there[0, :, :, :, 1, :] = np.einsum("bd,ef->bedf", s, same)
    there[1, :, :, :, 0, :] = np.einsum("bd,ef->bedf", -s, same)
    there[1, :, :, :, 1, :] = np.einsum("bd,ef->bedf", c, same)
    there = there.reshape(128, 128)
    phi = 2.0 * np.pi * np.outer(np.arange(16), np.arange(4)) / GRID
    twist = np.stack([np.cos(phi), np.sin(phi)])[:, :, None, :, None]
    twist = np.broadcast_to(twist, (2, 16, 4, 4, KEPT)).reshape(2, 64, 128)
    quarter = 2.0 * np.pi * np.outer(np.arange(4), np.arange(4)) / 4.0
    cq, sq = np.rint(np.cos(quarter)), np.rint(np.sin(quarter))
    kept = np.eye(KEPT)
    four = np.zeros((2, 4, KEPT, 2, 4, KEPT))
    four[0, :, :, 0] = np.einsum("la,kK->lkaK", cq, kept)
    four[1, :, :, 0] = np.einsum("la,kK->lkaK", sq, kept)
    four[0, :, :, 1] = np.einsum("la,kK->lkaK", -sq, kept)
    four[1, :, :, 1] = np.einsum("la,kK->lkaK", cq, kept)
    four = four.reshape(256, 256)
    return there, there.T.copy(), twist.astype(np.float32), four, four.T.copy()


def right_table(table):
    high, low = halves(table)
    return np.block([[high, low], [high, np.zeros_like(low)]])


def left_table(table):
    return np.ascontiguousarray(right_table(table.T).T)


def split(x):
    high = x.astype(jnp.bfloat16)
    low = (x - high.astype(jnp.float32)).astype(jnp.bfloat16)
    return high, low


def mm(a, b):
    return jnp.dot(a, b, preferred_element_type=jnp.float32)


def from_left(table_ref, data_ref):
    both = mm(table_ref[...], data_ref[...])
    return both[:128] + both[128:]


def from_right(data_ref, table_ref):
    both = mm(data_ref[...], table_ref[...])
    return both[:, :128] + both[:, 128:]


def swap_chunks(tiles):
    lane = lax.broadcasted_iota(jnp.int32, tiles[0].shape, 1)
    low = lane < 64
    even = lax.bitwise_and(lane, 32) == 0
    halfway = [None] * 4
    for i in range(2):
        first, second = tiles[i], tiles[i + 2]
        halfway[i] = jnp.where(low, first, pltpu.roll(second, 64, 1))
        halfway[i + 2] = jnp.where(low, pltpu.roll(first, 64, 1), second)
    result = []
    for i in (0, 2):
        first, second = halfway[i], halfway[i + 1]
        result.append(jnp.where(even, first, pltpu.roll(second, 32, 1)))
        result.append(jnp.where(even, pltpu.roll(first, 96, 1), second))
    return result


def slopes_of(bits, low, high):
    at = [jnp.where(bit == 1, high, low) for bit in bits]
    far = [jnp.where(bit == 1, low, high) for bit in bits]

    def slope(corner, axis):
        value = None
        for other in range(3):
            if other != axis:
                factor = at[other] if corner >> other & 1 else far[other]
                value = factor if value is None else value * factor
        return value if corner >> axis & 1 else -value

    return slope


def macro_strain(point, conn_ref, disp_ref):
    low, high = jnp.float32(GAUSS_LOW), jnp.float32(GAUSS_HIGH)
    bits = [lax.bitwise_and(lax.shift_right_logical(point, d), 1) for d in range(3)]
    slope = slopes_of(bits, low, high)
    element = lax.shift_right_logical(point, 3)
    grad = [[jnp.float32(0.0)] * 3 for _ in range(3)]
    for corner in range(8):
        node = conn_ref[element, corner]
        for k in range(3):
            u = disp_ref[k, node]
            for d in range(3):
                grad[k][d] = grad[k][d] + slope(corner, d) * u
    strain = []
    for i, j in TENSOR_PAIRS:
        strain.append(grad[i][i] if i == j else 0.5 * (grad[i][j] + grad[j][i]))
    return strain


def material(elastic, phases, flags):
    hard = phases == 1
    limit = jnp.where(hard, 1.2, 0.3)
    ratio = jnp.where(
        hard,
        3.0 * SHEAR_MODULUS / (3.0 * SHEAR_MODULUS + 10.0),
        3.0 * SHEAR_MODULUS / (3.0 * SHEAR_MODULUS + 2.0),
    )
    active = flags.astype(jnp.float32)
    volume = elastic[0] + elastic[1] + elastic[2]
    third = volume * (1.0 / 3.0)
    trial = [2.0 * SHEAR_MODULUS * (elastic[a] - third) for a in range(3)]
    trial += [2.0 * SHEAR_MODULUS * elastic[a] for a in range(3, 6)]
    normal = trial[0] * trial[0] + trial[1] * trial[1] + trial[2] * trial[2]
    shear = trial[3] * trial[3] + trial[4] * trial[4] + trial[5] * trial[5]
    equivalent = jnp.sqrt(1.5 * (normal + 2.0 * shear))
    bounded = jnp.maximum(equivalent, limit)
    inverse = 1.0 / bounded
    scaled = ratio * active
    softening = 1.0 - scaled * (equivalent - limit) * inverse
    pressure = BULK_MODULUS * volume
    stress = [trial[a] * softening + pressure for a in range(3)]
    stress += [trial[a] * softening for a in range(3, 6)]
    weight = 3.0 * SHEAR_MODULUS * scaled * limit * (inverse * inverse * inverse)
    return stress, trial, softening, weight


def every_fourth(ref, start, plane):
    return ref[pl.ds(start + plane, 32, stride=4), :]


def put_rows(ref, rows, value):
    high, low = split(value)
    ref[rows, 0:128] = high
    ref[rows, 128:256] = low


def put_columns(ref, start, count, columns, value):
    high, low = split(value)
    ref[pl.ds(start, count), columns] = high
    ref[pl.ds(128 + start, count), columns] = low


def plane_waves():
    row = lax.broadcasted_iota(jnp.int32, (128, 128), 0)
    lane = lax.broadcasted_iota(jnp.int32, (128, 128), 1)
    ky = 4 * lax.shift_right_logical(row, 3) + lax.bitwise_and(row, 3)
    ky = jnp.where(ky < GRID // 2, ky, ky - GRID)
    return ky.astype(jnp.float32), lax.bitwise_and(lane, 31).astype(jnp.float32)


def forward_planes(xs, bs, depth, rows, out_ref):
    turned = from_right(xs, depth)
    tiles = swap_chunks([turned[l * 192 : (l + 1) * 192] for l in range(PLANES)])
    for c in range(6):
        for s in range(4):
            block = tiles[s][c * 32 : (c + 1) * 32]
            put_columns(bs, s * 32, 32, pl.ds(c * 128, 128), block)
    spectrum = from_left(rows, bs)
    xx, yy, zz, yz, xz, xy = (spectrum[:, c * 128 : (c + 1) * 128] for c in range(6))
    wave_y, wave_z = plane_waves()
    fields = (xx, xy, xz, wave_y * yy + wave_z * yz, wave_y * yz + wave_z * zz)
    for c, field in enumerate(fields):
        out_ref[:, c * 8 : (c + 1) * 8, :] = field.reshape(16, 8, 128)


def backward_planes(in_ref, bs, xs, depth, rows):
    xx, xy, xz, y, z = (
        in_ref[:, c * 8 : (c + 1) * 8, :].reshape(128, 128) for c in range(FIELDS)
    )
    wave_y, wave_z = plane_waves()
    yy, zz = 2.0 * (wave_y * y), 2.0 * (wave_z * z)
    for c, value in enumerate((xx, yy, zz, wave_y * z + wave_z * y, xz, xy)):
        put_columns(bs, 0, 128, pl.ds(c * 128, 128), value)
    lines = from_left(rows, bs)
    tiles = [
        jnp.concatenate(
            [lines[s * 32 : (s + 1) * 32, c * 128 : (c + 1) * 128] for c in range(6)], axis=0
        )
        for s in range(4)
    ]
    for l, tile in enumerate(swap_chunks(tiles)):
        put_rows(xs, pl.ds(l * 192, 192), tile)
    return from_right(xs, depth)


def basis_of(points, conn_ref):
    shape = (points, 128)
    lane = lax.broadcasted_iota(jnp.int32, shape, 1)
    point = lax.broadcasted_iota(jnp.int32, shape, 0)
    element = lax.shift_right_logical(point, 3)
    bits = [lax.bitwise_and(lax.shift_right_logical(point, d), 1) for d in range(3)]
    slope = slopes_of(bits, GAUSS_LOW, GAUSS_HIGH)
    node = lane // 3
    part = lane - 3 * node
    elements = conn_ref.shape[0]
    grad = [jnp.zeros(shape, jnp.float32) for _ in range(3)]
    for corner in range(8):
        owner = jnp.full(shape, conn_ref[0, corner], jnp.int32)
        for e in range(1, elements):
            owner = jnp.where(element == e, conn_ref[e, corner], owner)
        here = (owner == node) & (lane < 60)
        for d in range(3):
            grad[d] = grad[d] + jnp.where(here, slope(corner, d), 0.0)
    basis = []
    for i, k in TENSOR_PAIRS:
        if i == k:
            basis.append(jnp.where(part == i, grad[i], 0.0))
        else:
            value = jnp.where(part == i, 0.5 * grad[k], 0.0)
            basis.append(value + jnp.where(part == k, 0.5 * grad[i], 0.0))
    return jnp.concatenate(basis, axis=0)


def first_kernel(
    points, conn_hbm, disp_hbm, phase_hbm, flag_hbm, plastic_hbm, depth_hbm, rows_hbm,
    out_ref, macro_ref, basis_ref, turned_ref,
    conn_ref, disp_ref, phase_ref, flag_ref, plastic_ref, depth, rows, sems, xs, bs,
):
    pairs = (
        (conn_hbm, conn_ref), (disp_hbm, disp_ref), (plastic_hbm, plastic_ref),
        (phase_hbm, phase_ref), (flag_hbm.at[pl.ds(0, 128)], flag_ref),
        (depth_hbm, depth), (rows_hbm, rows),
    )
    copies = [pltpu.make_async_copy(a, b, sems.at[i]) for i, (a, b) in enumerate(pairs)]
    for copy in copies:
        copy.start()
    for copy in copies[:2]:
        copy.wait()
    macro = macro_strain(lax.axis_index("rve"), conn_ref, disp_ref)
    row = lax.broadcasted_iota(jnp.int32, (8, 128), 0)
    table = jnp.zeros((8, 128), jnp.float32)
    for c in range(6):
        table = jnp.where(row == c, macro[c], table)
    macro_ref[...] = table
    basis = basis_of(points, conn_ref)
    basis_ref[...] = basis
    high, low = split(jnp.transpose(basis))
    turned_ref[0] = high
    turned_ref[1] = low
    for copy in copies[2:5]:
        copy.wait()
    for plane in range(PLANES):
        elastic = [macro[c] - every_fourth(plastic_ref, c * 128, plane) for c in range(6)]
        phases = every_fourth(phase_ref, 0, plane)
        flags = every_fourth(flag_ref, 0, plane)
        stress = material(elastic, phases, flags)[0]
        for c in range(6):
            put_rows(xs, pl.ds(plane * 192 + c * 32, 32), stress[c])
    for copy in copies[5:]:
        copy.wait()
    forward_planes(xs, bs, depth, rows, out_ref)


def middle_kernel(
    macro_ref, phase_ref, flag_ref, plastic_ref, in_ref, back_depth, back_rows, depth, rows,
    out_ref, elastic_ref, xs, bs,
):
    macro = [macro_ref[c : c + 1, :] for c in range(6)]
    correction = backward_planes(in_ref, bs, xs, back_depth, back_rows)
    for plane in range(PLANES):
        elastic = []
        for c in range(6):
            at = plane * 192 + c * 32
            before = macro[c] - every_fourth(plastic_ref, c * 128, plane)
            after = before - correction[at : at + 32]
            elastic_ref[at : at + 32, :] = after
            elastic.append(after)
        phases = every_fourth(phase_ref, 0, plane)
        flags = every_fourth(flag_ref, 128, plane)
        stress = material(elastic, phases, flags)[0]
        for c in range(6):
            put_rows(xs, pl.ds(plane * 192 + c * 32, 32), stress[c])
    forward_planes(xs, bs, depth, rows, out_ref)


def last_kernel(
    phase_ref, flag_ref, elastic_ref, in_ref, back_depth, back_rows, out_ref, xs, bs
):
    correction = backward_planes(in_ref, bs, xs, back_depth, back_rows)
    sums = [None] * 28

    def collect(at, value):
        part = value.reshape(4, 8, 128)
        part = (part[0] + part[1]) + (part[2] + part[3])
        sums[at] = part if sums[at] is None else sums[at] + part

    for plane in range(PLANES):
        starts = [plane * 192 + c * 32 for c in range(6)]
        elastic = [elastic_ref[at : at + 32, :] - correction[at : at + 32] for at in starts]
        phases = every_fourth(phase_ref, 0, plane)
        flags = every_fourth(flag_ref, 256, plane)
        stress, trial, softening, weight = material(elastic, phases, flags)
        for c in range(6):
            collect(c, stress[c])
        collect(6, softening)
        at = 7
        for a in range(6):
            scaled = weight * trial[a]
            for b in range(a, 6):
                collect(at, scaled * trial[b])
                at += 1
    row = lax.broadcasted_iota(jnp.int32, (128, 128), 0)
    lines = jnp.zeros((128, 128), jnp.float32)

    def place(at, value):
        return jnp.where(row == at, jnp.broadcast_to(value, (128, 128)), lines)

    totals = [jnp.sum(value, axis=0, keepdims=True) for value in sums]
    for c in range(7):
        lines = place(c, totals[c])
    at = 7
    for a in range(6):
        for b in range(a, 6):
            lines = place(OUTER_AT + 6 * a + b, totals[at])
            if a != b:
                lines = place(OUTER_AT + 6 * b + a, totals[at])
            at += 1
    ones = jnp.ones((SLABS, 128), jnp.float32)
    line = lax.dot_general(
        ones, lines, (((1,), (1,)), ((), ())),
        precision=lax.Precision.HIGHEST, preferred_element_type=jnp.float32,
    )
    out_ref[...] = line.reshape(SLABS, 1, 128)


def column_kernel(in_ref, columns, back_columns, twist_ref, four, back_four, out_ref, bs, ys):
    count = 64 * FIELDS
    for c in range(FIELDS):
        block = in_ref[:, c * 8 : (c + 1) * 8, :].reshape(128, 128)
        put_columns(bs, 0, 128, pl.ds(c * 128, 128), block)
    mixed = from_left(columns, bs)
    cosine, sine = twist_ref[0], twist_ref[1]

    def put(c, lanes, value):
        high, low = split(value)
        ys[pl.ds(c * 64, 64), lanes] = high
        ys[pl.ds(count + c * 64, 64), lanes] = low

    for c in range(FIELDS):
        lanes = slice(c * 128, (c + 1) * 128)
        real, imag = mixed[:64, lanes], mixed[64:, lanes]
        put(c, pl.ds(0, 128), real * cosine + imag * sine)
        put(c, pl.ds(128, 128), imag * cosine - real * sine)
    both = mm(ys[...], four[...])
    spectrum = both[:count] + both[count:]
    xx, xy, xz, y, z = (spectrum[c * 64 : (c + 1) * 64] for c in range(FIELDS))

    shape = (64, 256)
    row = lax.broadcasted_iota(jnp.int32, shape, 0)
    lane = lax.broadcasted_iota(jnp.int32, shape, 1)
    lane = lax.bitwise_and(lane, 127)
    kx = 16 * lax.shift_right_logical(lane, 5) + lax.shift_right_logical(row, 2)
    ky = 4 * lax.axis_index("slab") + lax.bitwise_and(row, 3)
    kz = lax.bitwise_and(lane, 31)
    half = GRID // 2
    keep = (kx != half) & (ky != half) & (kx + ky + kz > 0)
    xi = [
        jnp.where(kx < half, kx, kx - GRID).astype(jnp.float32),
        jnp.where(ky < half, ky, ky - GRID).astype(jnp.float32),
        kz.astype(jnp.float32),
    ]
    length = xi[0] * xi[0] + xi[1] * xi[1] + xi[2] * xi[2]
    inverse = jnp.where(keep, 1.0 / jnp.maximum(length, 1.0), 0.0)
    coupling = (REFERENCE_LAME + REFERENCE_SHEAR) / (
        REFERENCE_SHEAR * (REFERENCE_LAME + 2.0 * REFERENCE_SHEAR)
    )
    scaled = inverse * (1.0 / (2.0 * REFERENCE_SHEAR))
    traction = [xi[0] * xx + xi[1] * xy + xi[2] * xz, xi[0] * xy + y, xi[0] * xz + z]
    load = xi[0] * traction[0] + xi[1] * traction[1] + xi[2] * traction[2]
    load = load * (inverse * (REFERENCE_SHEAR * coupling))
    field = [scaled * (traction[i] - xi[i] * load) for i in range(3)]
    put(0, slice(None), 2.0 * (xi[0] * field[0]))
    put(1, slice(None), xi[0] * field[1] + xi[1] * field[0])
    put(2, slice(None), xi[0] * field[2] + xi[2] * field[0])
    put(3, slice(None), field[1])
    put(4, slice(None), field[2])
    both = mm(ys[...], back_four[...])
    turned = both[:count] + both[count:]
    for c in range(FIELDS):
        real, imag = turned[c * 64 : (c + 1) * 64, :128], turned[c * 64 : (c + 1) * 64, 128:]
        lanes = pl.ds(c * 128, 128)
        put_columns(bs, 0, 64, lanes, real * cosine - imag * sine)
        put_columns(bs, 64, 64, lanes, real * sine + imag * cosine)
    result = from_left(back_columns, bs)
    for c in range(FIELDS):
        out_ref[:, c * 8 : (c + 1) * 8, :] = result[:, c * 128 : (c + 1) * 128].reshape(16, 8, 128)


def totals_kernel(in_ref, all_ref, stress_ref, tangent_ref):
    line = jnp.sum(in_ref[...].reshape(SLABS, 128), axis=0, keepdims=True)
    all_ref[...] = jnp.broadcast_to(line[None], all_ref.shape)
    line = line * (1.0 / VOXELS)
    stress_ref[...] = line[:, :6]
    at = lax.broadcasted_iota(jnp.int32, (1, 128), 1) - OUTER_AT
    a = at // 6
    b = at - 6 * a
    both = (a < 3) & (b < 3)
    shear = jnp.broadcast_to(line[:, 6:7], (1, 128)) * (2.0 * SHEAR_MODULUS)
    fixed = jnp.where(both, BULK_MODULUS - shear * (1.0 / 3.0), 0.0)
    fixed = fixed + jnp.where(a == b, shear, 0.0)
    whole = (fixed - line * jnp.where(b < 3, 1.0, 2.0)) * (1.0 / TANGENT_UNIT)
    for i in range(6):
        tangent_ref[i] = whole[:, OUTER_AT + 6 * i : OUTER_AT + 6 * i + 6]


def assembly_kernel(points, basis_ref, turned_ref, in_ref, stiffness_ref, forces_ref):
    half = points // 2
    shape = (points, 128)
    sums = in_ref[...].reshape(points, 128) * (1.0 / VOXELS)
    sums = jnp.concatenate([sums[half:], sums[:half]], axis=0)
    basis = [basis_ref[a * points : (a + 1) * points, :] for a in range(6)]
    mean_shear = 2.0 * SHEAR_MODULUS * sums[:, 6:7]

    def column(at):
        return jnp.broadcast_to(sums[:, at : at + 1], shape)

    mean_shear = jnp.broadcast_to(mean_shear, shape)
    on_diagonal = BULK_MODULUS + mean_shear * (2.0 / 3.0)
    off_diagonal = BULK_MODULUS - mean_shear * (1.0 / 3.0)
    answers = []
    force = jnp.zeros(shape, jnp.float32)
    scale = QUADRATURE_WEIGHT / TANGENT_UNIT
    for a in range(6):
        total = jnp.zeros(shape, jnp.float32)
        for b in range(6):
            low, high = min(a, b), max(a, b)
            entry = -PAIR_WEIGHTS[b] * column(OUTER_AT + 6 * low + high)
            if a == b:
                entry = entry + (on_diagonal if a < 3 else mean_shear)
            elif a < 3 and b < 3:
                entry = entry + off_diagonal
            total = total + entry * basis[b]
        answers.append(total * (PAIR_WEIGHTS[a] * scale))
        force = force + basis[a] * (column(a) * (PAIR_WEIGHTS[a] * QUADRATURE_WEIGHT))
    high, low = split(jnp.concatenate(answers, axis=0))
    left_high, left_low = turned_ref[0], turned_ref[1]
    whole = mm(left_high, high) + (mm(left_low, high) + mm(left_high, low))
    stiffness_ref[...] = whole[:60, :60]
    line = jnp.sum(force, axis=0, keepdims=True)
    part8 = lax.broadcasted_iota(jnp.int32, (8, 128), 0)
    lane8 = lax.broadcasted_iota(jnp.int32, (8, 128), 1)
    spread = jnp.where(lane8 % 3 == part8, jnp.broadcast_to(line, (8, 128)), 0.0)
    pick_row = lax.broadcasted_iota(jnp.int32, (128, 128), 0)
    pick_col = lax.broadcasted_iota(jnp.int32, (128, 128), 1)
    pick = (pick_row // 3 == pick_col).astype(jnp.float32)
    forces = jnp.dot(
        spread, pick, precision=lax.Precision.HIGHEST, preferred_element_type=jnp.float32
    )
    forces_ref[...] = forces[:3, :20]


VMEM = pl.BlockSpec(memory_space=pltpu.VMEM)
HBM = pl.BlockSpec(memory_space=pltpu.HBM)
BF16 = jnp.bfloat16
F32 = jnp.float32
LIMIT = 16 * 1024 * 1024


def params():
    return pltpu.CompilerParams(vmem_limit_bytes=LIMIT)


def cost(flops, size):
    return pl.CostEstimate(flops=flops, bytes_accessed=size, transcendentals=0)


def plane_scratch():
    return [pltpu.VMEM((768, 256), BF16), pltpu.VMEM((256, 768), BF16)]


def exchange(array):
    return lax.all_to_all(array, "slab", split_axis=0, concat_axis=0, tiled=True)


def on_device(phase_ids, yield_flags, plastic_strain, displacements, connectivity):
    points = lax.axis_size("rve")

    def rows(array):
        lead = math.prod(array.shape[:-2])
        array = array.reshape(lead, PLANES, 32, 128)
        return jnp.transpose(array, (0, 2, 1, 3)).reshape(lead * 128, 128)

    phases = rows(phase_ids)
    flags = rows(yield_flags)
    plastic = rows(plastic_strain)

    there, back = depth_tables()
    depth, back_depth = jnp.asarray(right_table(there)), jnp.asarray(right_table(back))
    there, back = row_tables()
    line, back_line = jnp.asarray(left_table(there)), jnp.asarray(left_table(back))
    there, back, twist, four, back_four = column_tables()
    column, back_column = jnp.asarray(left_table(there)), jnp.asarray(left_table(back))
    twist = jnp.asarray(twist)
    four = jnp.asarray(four.astype(ml_dtypes.bfloat16))
    back_four = jnp.asarray(back_four.astype(ml_dtypes.bfloat16))

    block = jax.ShapeDtypeStruct((16, 8 * FIELDS, 128), F32)

    first = pl.pallas_call(
        functools.partial(first_kernel, points),
        out_shape=(
            block, jax.ShapeDtypeStruct((8, 128), F32),
            jax.ShapeDtypeStruct((6 * points, 128), F32),
            jax.ShapeDtypeStruct((2, 128, 6 * points), BF16),
        ),
        in_specs=[HBM] * 7, out_specs=(VMEM,) * 4,
        scratch_shapes=[
            pltpu.SMEM(connectivity.shape, jnp.int32), pltpu.SMEM(displacements.shape[::-1], F32),
            pltpu.VMEM((128, 128), jnp.int32), pltpu.VMEM((128, 128), jnp.int32),
            pltpu.VMEM((768, 128), F32), pltpu.VMEM((256, 256), BF16), pltpu.VMEM((256, 256), BF16),
            pltpu.SemaphoreType.DMA((7,)), *plane_scratch(),
        ],
        compiler_params=params(), cost_estimate=cost(400_000_000, 2_000_000), name="first",
    )
    columns = pl.pallas_call(
        column_kernel, out_shape=block,
        in_specs=[VMEM] * 6, out_specs=VMEM,
        scratch_shapes=[
            pltpu.VMEM((256, 128 * FIELDS), BF16), pltpu.VMEM((128 * FIELDS, 256), BF16),
        ],
        compiler_params=params(), cost_estimate=cost(400_000_000, 2_000_000), name="columns",
    )
    middle = pl.pallas_call(
        middle_kernel, out_shape=(block, jax.ShapeDtypeStruct((768, 128), F32)),
        in_specs=[VMEM] * 9, out_specs=(VMEM, VMEM),
        scratch_shapes=plane_scratch(), compiler_params=params(),
        cost_estimate=cost(800_000_000, 4_000_000), name="middle",
    )
    last = pl.pallas_call(
        last_kernel, out_shape=jax.ShapeDtypeStruct((SLABS, 1, 128), F32),
        in_specs=[VMEM] * 6, out_specs=VMEM,
        scratch_shapes=plane_scratch(), compiler_params=params(),
        cost_estimate=cost(400_000_000, 2_000_000), name="last",
    )
    totals = pl.pallas_call(
        totals_kernel,
        out_shape=(
            jax.ShapeDtypeStruct((points, 1, 128), F32), jax.ShapeDtypeStruct((1, 6), F32),
            jax.ShapeDtypeStruct((6, 1, 6), F32),
        ),
        in_specs=[VMEM], out_specs=(VMEM, VMEM, VMEM), compiler_params=params(),
        cost_estimate=cost(10_000, 50_000), name="totals",
    )
    assembly = pl.pallas_call(
        functools.partial(assembly_kernel, points),
        out_shape=(jax.ShapeDtypeStruct((60, 60), F32), jax.ShapeDtypeStruct((3, 20), F32)),
        in_specs=[VMEM] * 3, out_specs=(VMEM, VMEM), compiler_params=params(),
        cost_estimate=cost(10_000_000, 200_000), name="assembly",
    )

    def apply_columns(array):
        return exchange(
            columns(exchange(array), column, back_column, twist, four, back_four)
        )

    operands = (connectivity, displacements.T, phases, flags, plastic, depth, line)
    spectrum, macro, basis, turned_basis = first(
        *(pltpu.with_memory_space_constraint(operand, pltpu.HBM) for operand in operands)
    )
    planes = apply_columns(spectrum)
    spectrum, elastic = middle(
        macro, phases, flags, plastic, planes, back_depth, back_line, depth, line
    )
    planes = apply_columns(spectrum)
    partial = last(phases, flags, elastic, planes, back_depth, back_line)
    everyone, stress, tangent = totals(exchange(partial))
    half = points // 2
    turned = [*range(half, points), *range(half)]
    everyone = lax.all_to_all(
        everyone, "rve", 0, 0, tiled=True, axis_index_groups=[turned]
    )
    stiffness, forces = assembly(basis, turned_basis, everyone)
    return (stress, jnp.transpose(tangent, (1, 0, 2)), forces.T, stiffness)


def solution(mesh):
    return jax.shard_map(
        on_device,
        mesh=mesh,
        in_specs=(
            P("slab", None),
            P("rve", None, "slab", None),
            P("rve", None, "slab", None),
            P(),
            P(),
        ),
        out_specs=(P("rve", None), P("rve", None, None), P(), P()),
        check_vma=False,
    )
```

time: 99 us -> 95.2 us (0.962)
  blocking collectives: 86.8 us -> 84.8 us
  Pallas kernels: 10.7 us -> 9.21 us
    all_to_all x5, blocking collectives: 58 us -> 56.3 us  [exchange(): lax.all_to_all(array, 'slab', split_axis=0, concat_axis=0, tiled=True)]
    pallas_call x5, Pallas kernels: 7.59 us -> 6.25 us  [the longest x2 2.42 us: apply_columns(): columns(exchange(array), column, back_column, twist, four, back_four)]
where the time goes in v3:
time: 95.2 us; the launch traced here: 94.9 us
  blocking collectives  84.8 us (89%)
  Pallas kernels  9.21 us (10%)
    all_to_all x5, blocking collectives, exchange(): lax.all_to_all(array, 'slab', split_axis=0, concat_axis=0, tiled=True)  56.3 us
    all_to_all x1, blocking collectives, on_device(): lax.all_to_all(everyone, 'rve', 0, 0, tiled=True, axis_index_groups=[turn...  28.5 us
    pallas_call x2, Pallas kernels, apply_columns(): columns(exchange(array), column, back_column, twist, four, back_four)  2.42 us
    pallas_call x1, Pallas kernels, on_device(): first(*(pltpu.with_memory_space_constraint(operand, pltpu.HBM) for operan...  2.21 us

profile of v3, /device:TPU:1, one launch (start us, length us, event | category | flops | bytes accessed | tf_op | source)
XLA Modules:
  0.0 94.9 jit_solution(10678565564360891933)
XLA Ops:
  0.6 2.2 %first.1 = (f32[16,40,128]{2,1,0:T(8,128)S(1)}, f32[8,128]{1,0:T(8,128)S(1)}, f32[192,128]{1,0:T(8,128)S(1)}, bf16[2,128,192]{2,1,0:T(8,128)(2,1)S(1)}) custom-call(s32[4,8]{1,0:T(4,128)} %conn_hbm.1, f32[3,20]{1,0:T(4,128)} %bitcast.27, s32[128,128]{1,0:T(8,128)} %bitcast.23, s32[384,128]{1,0:T(8,128)} %bitcast.20, f32[768,128]{1,0:T(8,128)} %bitcast.18, ...), custom_call_target="tpu_custom_call" | custom-call | flops 400000000 | bytes 2000000 | tf_op jit(solution)/shard_map/first/pallas_call | solution.py:634
  2.8 0.0 copy-start.6
  2.9 0.0 copy-start.7
  2.9 0.0 copy-start.8
  2.9 0.0 copy-start.9
  2.9 0.0 copy-start.11
  2.9 15.5 %all_to_all.30.in_ref = f32[16,40,128]{2,1,0:T(8,128)S(1)} all-to-all(f32[16,40,128]{2,1,0:T(8,128)S(1)} %get-tuple-element.16), channel_id=1, replica_groups=mesh['rve'=32,'slab'=16] {'slab'}, dimensions={0} | all-to-all | bytes 655360 | tf_op jit(solution)/shard_map/all_to_all | solution.py:549
  18.4 0.0 copy-done.6
  18.4 0.0 copy-done.7
  18.4 0.0 copy-done.8
  18.4 0.0 copy-done.9
  18.4 0.0 copy-done.11
  18.4 0.0 copy-start.3
  18.4 0.0 copy-start.4
  18.4 0.0 copy-start.5
  18.5 0.0 copy-start.10
  18.5 1.2 %columns.4 = f32[16,40,128]{2,1,0:T(8,128)S(1)} custom-call(f32[16,40,128]{2,1,0:T(8,128)S(1)} %all_to_all.30.in_ref, bf16[256,256]{1,0:T(8,128)(2,1)S(1)} %copy-done.9, bf16[256,256]{1,0:T(8,128)(2,1)S(1)} %copy-done.8, f32[2,64,128]{2,1,0:T(8,128)S(1)} %copy-done.11, bf16[256,256]{1,0:T(8,128)(2,1)S(1)} %copy-done.7, bf16[256,256]{1,0:T(8,128)(2,1)S(1)} %copy-done.6), custom_call_target="tpu_custom_call" | custom-call | flops 400000000 | bytes 2000000 | tf_op jit(solution)/shard_map/columns/pallas_call | solution.py:630
  19.7 0.0 copy-start
  19.7 0.0 copy-start.1
  19.7 0.0 copy-start.2
  19.7 10.8 %all_to_all.31.in_ref = f32[16,40,128]{2,1,0:T(8,128)S(1)} all-to-all(f32[16,40,128]{2,1,0:T(8,128)S(1)} %columns.4), channel_id=1, replica_groups=mesh['rve'=32,'slab'=16] {'slab'}, dimensions={0} | all-to-all | bytes 655360 | tf_op jit(solution)/shard_map/all_to_all | solution.py:549
  30.5 0.0 copy-done.3
  30.5 0.0 copy-done.4
  30.5 0.0 copy-done.5
  30.5 0.0 copy-done.10
  30.5 0.0 copy-done
  30.5 0.0 copy-done.1
  30.5 0.0 copy-done.2
  30.5 1.6 %middle.1 = (f32[16,40,128]{2,1,0:T(8,128)S(1)}, f32[768,128]{1,0:T(8,128)S(1)}) custom-call(f32[8,128]{1,0:T(8,128)S(1)} %get-tuple-element.15.macro_ref, s32[128,128]{1,0:T(8,128)S(1)} %bitcast.24, s32[384,128]{1,0:T(8,128)S(1)} %bitcast.21, f32[768,128]{1,0:T(8,128)S(1)} %bitcast.19, f32[16,40,128]{2,1,0:T(8,128)S(1)} %all_to_all.31.in_ref, ...), custom_call_target="tpu_custom_call" | custom-call | flops 800000000 | bytes 4000000 | tf_op jit(solution)/shard_map/middle/pallas_call | solution.py:638
  32.1 10.5 %all_to_all.32.in_ref = f32[16,40,128]{2,1,0:T(8,128)S(1)} all-to-all(f32[16,40,128]{2,1,0:T(8,128)S(1)} %get-tuple-element.18), channel_id=1, replica_groups=mesh['rve'=32,'slab'=16] {'slab'}, dimensions={0} | all-to-all | bytes 655360 | tf_op jit(solution)/shard_map/all_to_all | solution.py:549
  42.6 1.2 %columns.5 = f32[16,40,128]{2,1,0:T(8,128)S(1)} custom-call(f32[16,40,128]{2,1,0:T(8,128)S(1)} %all_to_all.32.in_ref, bf16[256,256]{1,0:T(8,128)(2,1)S(1)} %copy-done.9, bf16[256,256]{1,0:T(8,128)(2,1)S(1)} %copy-done.8, f32[2,64,128]{2,1,0:T(8,128)S(1)} %copy-done.11, bf16[256,256]{1,0:T(8,128)(2,1)S(1)} %copy-done.7, bf16[256,256]{1,0:T(8,128)(2,1)S(1)} %copy-done.6), custom_call_target="tpu_custom_call" | custom-call | flops 400000000 | bytes 2000000 | tf_op jit(solution)/shard_map/columns/pallas_call | solution.py:630
  43.8 10.5 %all_to_all.33.in_ref = f32[16,40,128]{2,1,0:T(8,128)S(1)} all-to-all(f32[16,40,128]{2,1,0:T(8,128)S(1)} %columns.5), channel_id=1, replica_groups=mesh['rve'=32,'slab'=16] {'slab'}, dimensions={0} | all-to-all | bytes 655360 | tf_op jit(solution)/shard_map/all_to_all | solution.py:549
  54.3 1.2 %last.1 = f32[16,1,128]{2,1,0:T(1,128)S(1)} custom-call(s32[128,128]{1,0:T(8,128)S(1)} %bitcast.25, s32[384,128]{1,0:T(8,128)S(1)} %bitcast.22, f32[768,128]{1,0:T(8,128)S(1)} %get-tuple-element.17.elastic_ref, f32[16,40,128]{2,1,0:T(8,128)S(1)} %all_to_all.33.in_ref, bf16[256,256]{1,0:T(8,128)(2,1)S(1)} %copy-done.4, bf16[256,256]{1,0:T(8,128)(2,1)S(1)} %copy-done.3), custom_call_target="tpu_custom_call" | custom-call | flops 400000000 | bytes 2000000 | tf_op jit(solution)/shard_map/last/pallas_call | solution.py:642
  55.5 9.0 %all_to_all.34.in_ref = f32[16,1,128]{2,1,0:T(1,128)S(1)} all-to-all(f32[16,1,128]{2,1,0:T(1,128)S(1)} %last.1), channel_id=1, replica_groups=mesh['rve'=32,'slab'=16] {'slab'}, dimensions={0} | all-to-all | bytes 16384 | tf_op jit(solution)/shard_map/all_to_all | solution.py:549
  64.6 0.7 totals.1
  65.3 28.5 %all_to_all.35.in_ref = f32[32,1,128]{2,1,0:T(1,128)S(1)} all-to-all(f32[32,1,128]{2,1,0:T(1,128)S(1)} %get-tuple-element.23), channel_id=1, replica_groups={{256,272,288,304,320,336,352,368,384,400,416,432,448,464,480,496,0,16,3..., dimensions={0} | all-to-all | bytes 32768 | tf_op jit(solution)/shard_map/all_to_all | solution.py:646
  93.8 1.1 %assembly.1 = (f32[60,60]{1,0:T(8,128)}, f32[3,20]{1,0:T(4,128)}) custom-call(f32[192,128]{1,0:T(8,128)S(1)} %get-tuple-element.21.basis_ref, bf16[2,128,192]{2,1,0:T(8,128)(2,1)S(1)} %get-tuple-element.22.turned_ref, f32[32,1,128]{2,1,0:T(1,128)S(1)} %all_to_all.35.in_ref), custom_call_target="tpu_custom_call" | custom-call | flops 10000000 | bytes 200000 | tf_op jit(solution)/shard_map/assembly/pallas_call | solution.py:649
Async XLA Ops:
  2.8 15.5 %copy-start.6 = (bf16[256,256]{1,0:T(8,128)(2,1)S(1)}, bf16[256,256]{1,0:T(8,128)(2,1)}, u32[]{:S(2)}) copy-start(bf16[256,256]{1,0:T(8,128)(2,1)} %constant.26.clone.back_four) | copy-start | bytes 393220
  2.9 15.5 %copy-start.7 = (bf16[256,256]{1,0:T(8,128)(2,1)S(1)}, bf16[256,256]{1,0:T(8,128)(2,1)}, u32[]{:S(2)}) copy-start(bf16[256,256]{1,0:T(8,128)(2,1)} %constant.25.clone.four) | copy-start | bytes 393220
  2.9 15.5 %copy-start.8 = (bf16[256,256]{1,0:T(8,128)(2,1)S(1)}, bf16[256,256]{1,0:T(8,128)(2,1)}, u32[]{:S(2)}) copy-start(bf16[256,256]{1,0:T(8,128)(2,1)} %constant.23.clone.back_columns) | copy-start | bytes 393220
  2.9 15.5 %copy-start.9 = (bf16[256,256]{1,0:T(8,128)(2,1)S(1)}, bf16[256,256]{1,0:T(8,128)(2,1)}, u32[]{:S(2)}) copy-start(bf16[256,256]{1,0:T(8,128)(2,1)} %constant.22.clone.columns) | copy-start | bytes 393220
  2.9 15.5 %copy-start.11 = (f32[2,64,128]{2,1,0:T(8,128)S(1)}, f32[2,64,128]{2,1,0:T(8,128)}, u32[]{:S(2)}) copy-start(f32[2,64,128]{2,1,0:T(8,128)} %constant.24.clone.twist_ref) | copy-start | bytes 196612
  18.4 12.1 %copy-start.3 = (bf16[256,256]{1,0:T(8,128)(2,1)S(1)}, bf16[256,256]{1,0:T(8,128)(2,1)}, u32[]{:S(2)}) copy-start(bf16[256,256]{1,0:T(8,128)(2,1)} %constant.21.clone.back_rows) | copy-start | bytes 393220
  18.4 12.1 %copy-start.4 = (bf16[256,256]{1,0:T(8,128)(2,1)S(1)}, bf16[256,256]{1,0:T(8,128)(2,1)}, u32[]{:S(2)}) copy-start(bf16[256,256]{1,0:T(8,128)(2,1)} %constant.19.clone.back_depth) | copy-start | bytes 393220
  18.4 12.1 %copy-start.5 = (bf16[256,256]{1,0:T(8,128)(2,1)S(1)}, bf16[256,256]{1,0:T(8,128)(2,1)}, u32[]{:S(2)}) copy-start(bf16[256,256]{1,0:T(8,128)(2,1)} %constant.20.clone.rows_hbm.rows) | copy-start | bytes 393220
  18.5 12.1 %copy-start.10 = (bf16[256,256]{1,0:T(8,128)(2,1)S(1)}, bf16[256,256]{1,0:T(8,128)(2,1)}, u32[]{:S(2)}) copy-start(bf16[256,256]{1,0:T(8,128)(2,1)} %constant.18.clone.depth_hbm.depth) | copy-start | bytes 393220
  19.7 10.8 %copy-start = (f32[1,6,4,4096]{3,2,1,0:T(4,128)S(1)}, f32[1,6,4,4096]{3,2,1,0:T(4,128)}, u32[]{:S(2)}) copy-start(f32[1,6,4,4096]{3,2,1,0:T(4,128)} %param.16) | copy-start | bytes 1179652
  19.7 10.8 %copy-start.1 = (s32[1,3,4,4096]{3,2,1,0:T(4,128)S(1)}, s32[1,3,4,4096]{3,2,1,0:T(4,128)}, u32[]{:S(2)}) copy-start(s32[1,3,4,4096]{3,2,1,0:T(4,128)} %param.15) | copy-start | bytes 589828
  19.7 10.8 %copy-start.2 = (s32[4,4096]{1,0:T(4,128)S(1)}, s32[4,4096]{1,0:T(4,128)}, u32[]{:S(2)}) copy-start(s32[4,4096]{1,0:T(4,128)} %param.14) | copy-start | bytes 196612

commit v4 on v3

--- a/solution.py
+++ b/solution.py
@@ -463,10 +463,12 @@
         out_ref[:, c * 8 : (c + 1) * 8, :] = result[:, c * 128 : (c + 1) * 128].reshape(16, 8, 128)
 
 
-def totals_kernel(in_ref, all_ref, stress_ref, tangent_ref):
+def totals_kernel(in_ref, all_ref):
     line = jnp.sum(in_ref[...].reshape(SLABS, 128), axis=0, keepdims=True)
     all_ref[...] = jnp.broadcast_to(line[None], all_ref.shape)
-    line = line * (1.0 / VOXELS)
+
+
+def own_outputs(line, stress_ref, tangent_ref):
     stress_ref[...] = line[:, :6]
     at = lax.broadcasted_iota(jnp.int32, (1, 128), 1) - OUTER_AT
     a = at // 6
@@ -480,8 +482,12 @@
         tangent_ref[i] = whole[:, OUTER_AT + 6 * i : OUTER_AT + 6 * i + 6]
 
 
-def assembly_kernel(points, basis_ref, turned_ref, in_ref, stiffness_ref, forces_ref):
+def assembly_kernel(
+    points, basis_ref, turned_ref, in_ref, stress_ref, tangent_ref, stiffness_ref, forces_ref
+):
     half = points // 2
+    own = lax.rem(lax.axis_index("rve") + points - half, points)
+    own_outputs(in_ref[own] * (1.0 / VOXELS), stress_ref, tangent_ref)
     shape = (points, 128)
     sums = in_ref[...].reshape(points, 128) * (1.0 / VOXELS)
     sums = jnp.concatenate([sums[half:], sums[:half]], axis=0)
@@ -610,18 +616,17 @@
         cost_estimate=cost(400_000_000, 2_000_000), name="last",
     )
     totals = pl.pallas_call(
-        totals_kernel,
-        out_shape=(
-            jax.ShapeDtypeStruct((points, 1, 128), F32), jax.ShapeDtypeStruct((1, 6), F32),
-            jax.ShapeDtypeStruct((6, 1, 6), F32),
-        ),
-        in_specs=[VMEM], out_specs=(VMEM, VMEM, VMEM), compiler_params=params(),
+        totals_kernel, out_shape=jax.ShapeDtypeStruct((points, 1, 128), F32),
+        in_specs=[VMEM], out_specs=VMEM, compiler_params=params(),
         cost_estimate=cost(10_000, 50_000), name="totals",
     )
     assembly = pl.pallas_call(
         functools.partial(assembly_kernel, points),
-        out_shape=(jax.ShapeDtypeStruct((60, 60), F32), jax.ShapeDtypeStruct((3, 20), F32)),
-        in_specs=[VMEM] * 3, out_specs=(VMEM, VMEM), compiler_params=params(),
+        out_shape=(
+            jax.ShapeDtypeStruct((1, 6), F32), jax.ShapeDtypeStruct((6, 1, 6), F32),
+            jax.ShapeDtypeStruct((60, 60), F32), jax.ShapeDtypeStruct((3, 20), F32),
+        ),
+        in_specs=[VMEM] * 3, out_specs=(VMEM,) * 4, compiler_params=params(),
         cost_estimate=cost(10_000_000, 200_000), name="assembly",
     )
 
@@ -640,13 +645,13 @@
     )
     planes = apply_columns(spectrum)
     partial = last(phases, flags, elastic, planes, back_depth, back_line)
-    everyone, stress, tangent = totals(exchange(partial))
+    everyone = totals(exchange(partial))
     half = points // 2
     turned = [*range(half, points), *range(half)]
     everyone = lax.all_to_all(
         everyone, "rve", 0, 0, tiled=True, axis_index_groups=[turned]
     )
-    stiffness, forces = assembly(basis, turned_basis, everyone)
+    stress, tangent, stiffness, forces = assembly(basis, turned_basis, everyone)
     return (stress, jnp.transpose(tangent, (1, 0, 2)), forces.T, stiffness)
 
 

time: 95.2 us -> 94.5 us (level)
  no operation moved by 1% of the time
where the time goes in v4:
time: 94.5 us; the launch traced here: 94.2 us
  blocking collectives  84.8 us (90%)
  Pallas kernels  8.49 us (9%)
    all_to_all x5, blocking collectives, exchange(): lax.all_to_all(array, 'slab', split_axis=0, concat_axis=0, tiled=True)  56.3 us
    all_to_all x1, blocking collectives, on_device(): lax.all_to_all(everyone, 'rve', 0, 0, tiled=True, axis_index_groups=[turn...  28.5 us
    pallas_call x2, Pallas kernels, apply_columns(): columns(exchange(array), column, back_column, twist, four, back_four)  2.42 us
    pallas_call x1, Pallas kernels, on_device(): first(*(pltpu.with_memory_space_constraint(operand, pltpu.HBM) for operan...  2.21 us

profile of v4, /device:TPU:1, one launch (start us, length us, event | category | flops | bytes accessed | tf_op | source)
XLA Modules:
  0.0 94.2 jit_solution(15162404448117595527)
XLA Ops:
  0.6 2.2 %first.1 = (f32[16,40,128]{2,1,0:T(8,128)S(1)}, f32[8,128]{1,0:T(8,128)S(1)}, f32[192,128]{1,0:T(8,128)S(1)}, bf16[2,128,192]{2,1,0:T(8,128)(2,1)S(1)}) custom-call(s32[4,8]{1,0:T(4,128)} %conn_hbm.1, f32[3,20]{1,0:T(4,128)} %bitcast.27, s32[128,128]{1,0:T(8,128)} %bitcast.23, s32[384,128]{1,0:T(8,128)} %bitcast.20, f32[768,128]{1,0:T(8,128)} %bitcast.18, ...), custom_call_target="tpu_custom_call" | custom-call | flops 400000000 | bytes 2000000 | tf_op jit(solution)/shard_map/first/pallas_call | solution.py:639
  2.8 0.0 copy-start.6
  2.9 0.0 copy-start.7
  2.9 0.0 copy-start.8
  2.9 0.0 copy-start.9
  2.9 0.0 copy-start.11
  2.9 15.5 %all_to_all.30.in_ref = f32[16,40,128]{2,1,0:T(8,128)S(1)} all-to-all(f32[16,40,128]{2,1,0:T(8,128)S(1)} %get-tuple-element.17), channel_id=1, replica_groups=mesh['rve'=32,'slab'=16] {'slab'}, dimensions={0} | all-to-all | bytes 655360 | tf_op jit(solution)/shard_map/all_to_all | solution.py:555
  18.4 0.0 copy-done.6
  18.4 0.0 copy-done.7
  18.4 0.0 copy-done.8
  18.4 0.0 copy-done.9
  18.4 0.0 copy-done.11
  18.4 0.0 copy-start.3
  18.4 0.0 copy-start.4
  18.4 0.0 copy-start.5
  18.5 0.0 copy-start.10
  18.5 1.2 %columns.4 = f32[16,40,128]{2,1,0:T(8,128)S(1)} custom-call(f32[16,40,128]{2,1,0:T(8,128)S(1)} %all_to_all.30.in_ref, bf16[256,256]{1,0:T(8,128)(2,1)S(1)} %copy-done.9, bf16[256,256]{1,0:T(8,128)(2,1)S(1)} %copy-done.8, f32[2,64,128]{2,1,0:T(8,128)S(1)} %copy-done.11, bf16[256,256]{1,0:T(8,128)(2,1)S(1)} %copy-done.7, bf16[256,256]{1,0:T(8,128)(2,1)S(1)} %copy-done.6), custom_call_target="tpu_custom_call" | custom-call | flops 400000000 | bytes 2000000 | tf_op jit(solution)/shard_map/columns/pallas_call | solution.py:635
  19.7 0.0 copy-start
  19.7 0.0 copy-start.1
  19.7 0.0 copy-start.2
  19.7 10.8 %all_to_all.31.in_ref = f32[16,40,128]{2,1,0:T(8,128)S(1)} all-to-all(f32[16,40,128]{2,1,0:T(8,128)S(1)} %columns.4), channel_id=1, replica_groups=mesh['rve'=32,'slab'=16] {'slab'}, dimensions={0} | all-to-all | bytes 655360 | tf_op jit(solution)/shard_map/all_to_all | solution.py:555
  30.5 0.0 copy-done.3
  30.5 0.0 copy-done.4
  30.5 0.0 copy-done.5
  30.5 0.0 copy-done.10
  30.5 0.0 copy-done
  30.5 0.0 copy-done.1
  30.5 0.0 copy-done.2
  30.5 1.6 %middle.1 = (f32[16,40,128]{2,1,0:T(8,128)S(1)}, f32[768,128]{1,0:T(8,128)S(1)}) custom-call(f32[8,128]{1,0:T(8,128)S(1)} %get-tuple-element.16.macro_ref, s32[128,128]{1,0:T(8,128)S(1)} %bitcast.24, s32[384,128]{1,0:T(8,128)S(1)} %bitcast.21, f32[768,128]{1,0:T(8,128)S(1)} %bitcast.19, f32[16,40,128]{2,1,0:T(8,128)S(1)} %all_to_all.31.in_ref, ...), custom_call_target="tpu_custom_call" | custom-call | flops 800000000 | bytes 4000000 | tf_op jit(solution)/shard_map/middle/pallas_call | solution.py:643
  32.1 10.5 %all_to_all.32.in_ref = f32[16,40,128]{2,1,0:T(8,128)S(1)} all-to-all(f32[16,40,128]{2,1,0:T(8,128)S(1)} %get-tuple-element.19), channel_id=1, replica_groups=mesh['rve'=32,'slab'=16] {'slab'}, dimensions={0} | all-to-all | bytes 655360 | tf_op jit(solution)/shard_map/all_to_all | solution.py:555
  42.6 1.2 %columns.5 = f32[16,40,128]{2,1,0:T(8,128)S(1)} custom-call(f32[16,40,128]{2,1,0:T(8,128)S(1)} %all_to_all.32.in_ref, bf16[256,256]{1,0:T(8,128)(2,1)S(1)} %copy-done.9, bf16[256,256]{1,0:T(8,128)(2,1)S(1)} %copy-done.8, f32[2,64,128]{2,1,0:T(8,128)S(1)} %copy-done.11, bf16[256,256]{1,0:T(8,128)(2,1)S(1)} %copy-done.7, bf16[256,256]{1,0:T(8,128)(2,1)S(1)} %copy-done.6), custom_call_target="tpu_custom_call" | custom-call | flops 400000000 | bytes 2000000 | tf_op jit(solution)/shard_map/columns/pallas_call | solution.py:635
  43.8 10.5 %all_to_all.33.in_ref = f32[16,40,128]{2,1,0:T(8,128)S(1)} all-to-all(f32[16,40,128]{2,1,0:T(8,128)S(1)} %columns.5), channel_id=1, replica_groups=mesh['rve'=32,'slab'=16] {'slab'}, dimensions={0} | all-to-all | bytes 655360 | tf_op jit(solution)/shard_map/all_to_all | solution.py:555
  54.3 1.2 %last.1 = f32[16,1,128]{2,1,0:T(1,128)S(1)} custom-call(s32[128,128]{1,0:T(8,128)S(1)} %bitcast.25, s32[384,128]{1,0:T(8,128)S(1)} %bitcast.22, f32[768,128]{1,0:T(8,128)S(1)} %get-tuple-element.18.elastic_ref, f32[16,40,128]{2,1,0:T(8,128)S(1)} %all_to_all.33.in_ref, bf16[256,256]{1,0:T(8,128)(2,1)S(1)} %copy-done.4, bf16[256,256]{1,0:T(8,128)(2,1)S(1)} %copy-done.3), custom_call_target="tpu_custom_call" | custom-call | flops 400000000 | bytes 2000000 | tf_op jit(solution)/shard_map/last/pallas_call | solution.py:647
  55.5 9.0 %all_to_all.34.in_ref = f32[16,1,128]{2,1,0:T(1,128)S(1)} all-to-all(f32[16,1,128]{2,1,0:T(1,128)S(1)} %last.1), channel_id=1, replica_groups=mesh['rve'=32,'slab'=16] {'slab'}, dimensions={0} | all-to-all | bytes 16384 | tf_op jit(solution)/shard_map/all_to_all | solution.py:555
  64.6 28.5 %all_to_all.35.in_ref = f32[32,1,128]{2,1,0:T(1,128)S(1)} all-to-all(f32[32,1,128]{2,1,0:T(1,128)S(1)} %totals.1), channel_id=1, replica_groups={{256,272,288,304,320,336,352,368,384,400,416,432,448,464,480,496,0,16,3..., dimensions={0} | all-to-all | bytes 32768 | tf_op jit(solution)/shard_map/all_to_all | solution.py:651
  93.1 1.1 %assembly.1 = (f32[1,6]{1,0:T(1,128)}, f32[6,1,6]{2,1,0:T(1,128)}, f32[60,60]{1,0:T(8,128)}, f32[3,20]{1,0:T(4,128)}) custom-call(f32[192,128]{1,0:T(8,128)S(1)} %get-tuple-element.14.basis_ref, bf16[2,128,192]{2,1,0:T(8,128)(2,1)S(1)} %get-tuple-element.15.turned_ref, f32[32,1,128]{2,1,0:T(1,128)S(1)} %all_to_all.35.in_ref), custom_call_target="tpu_custom_call" | custom-call | flops 10000000 | bytes 200000 | tf_op jit(solution)/shard_map/assembly/pallas_call | solution.py:654
  (1 shorter events, 0.0 us)
Async XLA Ops:
  2.8 15.5 %copy-start.6 = (bf16[256,256]{1,0:T(8,128)(2,1)S(1)}, bf16[256,256]{1,0:T(8,128)(2,1)}, u32[]{:S(2)}) copy-start(bf16[256,256]{1,0:T(8,128)(2,1)} %constant.26.clone.back_four) | copy-start | bytes 393220
  2.9 15.5 %copy-start.7 = (bf16[256,256]{1,0:T(8,128)(2,1)S(1)}, bf16[256,256]{1,0:T(8,128)(2,1)}, u32[]{:S(2)}) copy-start(bf16[256,256]{1,0:T(8,128)(2,1)} %constant.25.clone.four) | copy-start | bytes 393220
  2.9 15.5 %copy-start.8 = (bf16[256,256]{1,0:T(8,128)(2,1)S(1)}, bf16[256,256]{1,0:T(8,128)(2,1)}, u32[]{:S(2)}) copy-start(bf16[256,256]{1,0:T(8,128)(2,1)} %constant.23.clone.back_columns) | copy-start | bytes 393220
  2.9 15.5 %copy-start.9 = (bf16[256,256]{1,0:T(8,128)(2,1)S(1)}, bf16[256,256]{1,0:T(8,128)(2,1)}, u32[]{:S(2)}) copy-start(bf16[256,256]{1,0:T(8,128)(2,1)} %constant.22.clone.columns) | copy-start | bytes 393220
  2.9 15.5 %copy-start.11 = (f32[2,64,128]{2,1,0:T(8,128)S(1)}, f32[2,64,128]{2,1,0:T(8,128)}, u32[]{:S(2)}) copy-start(f32[2,64,128]{2,1,0:T(8,128)} %constant.24.clone.twist_ref) | copy-start | bytes 196612
  18.4 12.1 %copy-start.3 = (bf16[256,256]{1,0:T(8,128)(2,1)S(1)}, bf16[256,256]{1,0:T(8,128)(2,1)}, u32[]{:S(2)}) copy-start(bf16[256,256]{1,0:T(8,128)(2,1)} %constant.21.clone.back_rows) | copy-start | bytes 393220
  18.4 12.1 %copy-start.4 = (bf16[256,256]{1,0:T(8,128)(2,1)S(1)}, bf16[256,256]{1,0:T(8,128)(2,1)}, u32[]{:S(2)}) copy-start(bf16[256,256]{1,0:T(8,128)(2,1)} %constant.19.clone.back_depth) | copy-start | bytes 393220
  18.4 12.1 %copy-start.5 = (bf16[256,256]{1,0:T(8,128)(2,1)S(1)}, bf16[256,256]{1,0:T(8,128)(2,1)}, u32[]{:S(2)}) copy-start(bf16[256,256]{1,0:T(8,128)(2,1)} %constant.20.clone.rows_hbm.rows) | copy-start | bytes 393220
  18.5 12.1 %copy-start.10 = (bf16[256,256]{1,0:T(8,128)(2,1)S(1)}, bf16[256,256]{1,0:T(8,128)(2,1)}, u32[]{:S(2)}) copy-start(bf16[256,256]{1,0:T(8,128)(2,1)} %constant.18.clone.depth_hbm.depth) | copy-start | bytes 393220
  19.7 10.8 %copy-start = (f32[1,6,4,4096]{3,2,1,0:T(4,128)S(1)}, f32[1,6,4,4096]{3,2,1,0:T(4,128)}, u32[]{:S(2)}) copy-start(f32[1,6,4,4096]{3,2,1,0:T(4,128)} %param.16) | copy-start | bytes 1179652
  19.7 10.8 %copy-start.1 = (s32[1,3,4,4096]{3,2,1,0:T(4,128)S(1)}, s32[1,3,4,4096]{3,2,1,0:T(4,128)}, u32[]{:S(2)}) copy-start(s32[1,3,4,4096]{3,2,1,0:T(4,128)} %param.15) | copy-start | bytes 589828
  19.7 10.8 %copy-start.2 = (s32[4,4096]{1,0:T(4,128)S(1)}, s32[4,4096]{1,0:T(4,128)}, u32[]{:S(2)}) copy-start(s32[4,4096]{1,0:T(4,128)} %param.14) | copy-start | bytes 196612

commit v5 on v4

--- a/solution.py
+++ b/solution.py
@@ -119,26 +119,30 @@
     return both[:128] + both[128:]
 
 
+def from_left_chained(table_ref, data_ref):
+    total = mm(table_ref[:128, :], data_ref[...])
+    return total + mm(table_ref[128:, :128], data_ref[:128, :])
+
+
 def from_right(data_ref, table_ref):
-    both = mm(data_ref[...], table_ref[...])
-    return both[:, :128] + both[:, 128:]
-
-
-def swap_chunks(tiles):
+    results = []
+    for l in range(PLANES):
+        both = mm(data_ref[l * 192 : (l + 1) * 192, :], table_ref[l])
+        results.append(both[:, :128] + both[:, 128:])
+    return results
+
+
+def gather_chunks(tiles):
     lane = lax.broadcasted_iota(jnp.int32, tiles[0].shape, 1)
-    low = lane < 64
-    even = lax.bitwise_and(lane, 32) == 0
-    halfway = [None] * 4
-    for i in range(2):
-        first, second = tiles[i], tiles[i + 2]
-        halfway[i] = jnp.where(low, first, pltpu.roll(second, 64, 1))
-        halfway[i + 2] = jnp.where(low, pltpu.roll(first, 64, 1), second)
-    result = []
-    for i in (0, 2):
-        first, second = halfway[i], halfway[i + 1]
-        result.append(jnp.where(even, first, pltpu.roll(second, 32, 1)))
-        result.append(jnp.where(even, pltpu.roll(first, 96, 1), second))
-    return result
+    odd = lax.bitwise_and(lane, 32) != 0
+    upper = lax.bitwise_and(lane, 64) != 0
+    tiles = [jnp.where(odd, tiles[(j + 1) % 4], tiles[j]) for j in range(4)]
+    tiles = [jnp.where(upper, tiles[(j + 2) % 4], tiles[j]) for j in range(4)]
+    return [tiles[-k % 4] for k in range(4)]
+
+
+def roll_chunks(tile, count):
+    return pltpu.roll(tile, 32 * (count % 4), 1) if count % 4 else tile
 
 
 def slopes_of(bits, low, high):
@@ -226,8 +230,8 @@
 
 
 def forward_planes(xs, bs, depth, rows, out_ref):
-    turned = from_right(xs, depth)
-    tiles = swap_chunks([turned[l * 192 : (l + 1) * 192] for l in range(PLANES)])
+    tiles = gather_chunks(from_right(xs, depth))
+    tiles = [roll_chunks(tile, -s) for s, tile in enumerate(tiles)]
     for c in range(6):
         for s in range(4):
             block = tiles[s][c * 32 : (c + 1) * 32]
@@ -255,7 +259,8 @@
         )
         for s in range(4)
     ]
-    for l, tile in enumerate(swap_chunks(tiles)):
+    tiles = [roll_chunks(tile, s) for s, tile in enumerate(tiles)]
+    for l, tile in enumerate(gather_chunks(tiles)):
         put_rows(xs, pl.ds(l * 192, 192), tile)
     return from_right(xs, depth)
 
@@ -309,12 +314,7 @@
     for c in range(6):
         table = jnp.where(row == c, macro[c], table)
     macro_ref[...] = table
-    basis = basis_of(points, conn_ref)
-    basis_ref[...] = basis
-    high, low = split(jnp.transpose(basis))
-    turned_ref[0] = high
-    turned_ref[1] = low
-    for copy in copies[2:5]:
+    for copy in copies[2:]:
         copy.wait()
     for plane in range(PLANES):
         elastic = [macro[c] - every_fourth(plastic_ref, c * 128, plane) for c in range(6)]
@@ -323,8 +323,11 @@
         stress = material(elastic, phases, flags)[0]
         for c in range(6):
             put_rows(xs, pl.ds(plane * 192 + c * 32, 32), stress[c])
-    for copy in copies[5:]:
-        copy.wait()
+    basis = basis_of(points, conn_ref)
+    basis_ref[...] = basis
+    high, low = split(jnp.transpose(basis))
+    turned_ref[0] = high
+    turned_ref[1] = low
     forward_planes(xs, bs, depth, rows, out_ref)
 
 
@@ -339,7 +342,7 @@
         for c in range(6):
             at = plane * 192 + c * 32
             before = macro[c] - every_fourth(plastic_ref, c * 128, plane)
-            after = before - correction[at : at + 32]
+            after = before - correction[plane][c * 32 : (c + 1) * 32]
             elastic_ref[at : at + 32, :] = after
             elastic.append(after)
         phases = every_fourth(phase_ref, 0, plane)
@@ -362,8 +365,11 @@
         sums[at] = part if sums[at] is None else sums[at] + part
 
     for plane in range(PLANES):
-        starts = [plane * 192 + c * 32 for c in range(6)]
-        elastic = [elastic_ref[at : at + 32, :] - correction[at : at + 32] for at in starts]
+        elastic = [
+            elastic_ref[plane * 192 + c * 32 : plane * 192 + (c + 1) * 32, :]
+            - correction[plane][c * 32 : (c + 1) * 32]
+            for c in range(6)
+        ]
         phases = every_fourth(phase_ref, 0, plane)
         flags = every_fourth(flag_ref, 256, plane)
         stress, trial, softening, weight = material(elastic, phases, flags)
@@ -405,7 +411,7 @@
     for c in range(FIELDS):
         block = in_ref[:, c * 8 : (c + 1) * 8, :].reshape(128, 128)
         put_columns(bs, 0, 128, pl.ds(c * 128, 128), block)
-    mixed = from_left(columns, bs)
+    mixed = from_left_chained(columns, bs)
     cosine, sine = twist_ref[0], twist_ref[1]
 
     def put(c, lanes, value):
@@ -418,8 +424,8 @@
         real, imag = mixed[:64, lanes], mixed[64:, lanes]
         put(c, pl.ds(0, 128), real * cosine + imag * sine)
         put(c, pl.ds(128, 128), imag * cosine - real * sine)
-    both = mm(ys[...], four[...])
-    spectrum = both[:count] + both[count:]
+    spectrum = mm(ys[:count, :], four[...])
+    spectrum = spectrum + mm(ys[count:, :], four[...])
     xx, xy, xz, y, z = (spectrum[c * 64 : (c + 1) * 64] for c in range(FIELDS))
 
     shape = (64, 256)
@@ -451,14 +457,14 @@
     put(2, slice(None), xi[0] * field[2] + xi[2] * field[0])
     put(3, slice(None), field[1])
     put(4, slice(None), field[2])
-    both = mm(ys[...], back_four[...])
-    turned = both[:count] + both[count:]
+    turned = mm(ys[:count, :], back_four[...])
+    turned = turned + mm(ys[count:, :], back_four[...])
     for c in range(FIELDS):
         real, imag = turned[c * 64 : (c + 1) * 64, :128], turned[c * 64 : (c + 1) * 64, 128:]
         lanes = pl.ds(c * 128, 128)
         put_columns(bs, 0, 64, lanes, real * cosine - imag * sine)
         put_columns(bs, 64, 64, lanes, real * sine + imag * cosine)
-    result = from_left(back_columns, bs)
+    result = from_left_chained(back_columns, bs)
     for c in range(FIELDS):
         out_ref[:, c * 8 : (c + 1) * 8, :] = result[:, c * 128 : (c + 1) * 128].reshape(16, 8, 128)
 
@@ -568,7 +574,10 @@
     plastic = rows(plastic_strain)
 
     there, back = depth_tables()
-    depth, back_depth = jnp.asarray(right_table(there)), jnp.asarray(right_table(back))
+    depth, back_depth = (
+        jnp.asarray(np.stack([right_table(np.roll(t, 32 * l, axis)) for l in range(PLANES)]))
+        for t, axis in ((there, 1), (back, 0))
+    )
     there, back = row_tables()
     line, back_line = jnp.asarray(left_table(there)), jnp.asarray(left_table(back))
     there, back, twist, four, back_four = column_tables()
@@ -590,7 +599,8 @@
         scratch_shapes=[
             pltpu.SMEM(connectivity.shape, jnp.int32), pltpu.SMEM(displacements.shape[::-1], F32),
             pltpu.VMEM((128, 128), jnp.int32), pltpu.VMEM((128, 128), jnp.int32),
-            pltpu.VMEM((768, 128), F32), pltpu.VMEM((256, 256), BF16), pltpu.VMEM((256, 256), BF16),
+            pltpu.VMEM((768, 128), F32), pltpu.VMEM((PLANES, 256, 256), BF16),
+            pltpu.VMEM((256, 256), BF16),
             pltpu.SemaphoreType.DMA((7,)), *plane_scratch(),
         ],
         compiler_params=params(), cost_estimate=cost(400_000_000, 2_000_000), name="first",

time: 94.5 us -> 94 us (level)
  no operation moved by 1% of the time
where the time goes in v5:
time: 94 us; the launch traced here: 93.6 us
  blocking collectives  84.8 us (90%)
  Pallas kernels  7.93 us (8%)
    all_to_all x5, blocking collectives, exchange(): lax.all_to_all(array, 'slab', split_axis=0, concat_axis=0, tiled=True)  56.3 us
    all_to_all x1, blocking collectives, on_device(): lax.all_to_all(everyone, 'rve', 0, 0, tiled=True, axis_index_groups=[turn...  28.5 us
    pallas_call x2, Pallas kernels, apply_columns(): columns(exchange(array), column, back_column, twist, four, back_four)  2.39 us
    pallas_call x1, Pallas kernels, on_device(): first(*(pltpu.with_memory_space_constraint(operand, pltpu.HBM) for operan...  2.05 us

profile of v5, /device:TPU:1, one launch (start us, length us, event | category | flops | bytes accessed | tf_op | source)
XLA Modules:
  0.0 93.6 jit_solution(4886004895287583394)
XLA Ops:
  0.6 2.0 %first.1 = (f32[16,40,128]{2,1,0:T(8,128)S(1)}, f32[8,128]{1,0:T(8,128)S(1)}, f32[192,128]{1,0:T(8,128)S(1)}, bf16[2,128,192]{2,1,0:T(8,128)(2,1)S(1)}) custom-call(s32[4,8]{1,0:T(4,128)} %conn_hbm.1, f32[3,20]{1,0:T(4,128)} %bitcast.27, s32[128,128]{1,0:T(8,128)} %bitcast.21, s32[384,128]{1,0:T(8,128)} %bitcast.18, f32[768,128]{1,0:T(8,128)} %bitcast.24, ...), custom_call_target="tpu_custom_call" | custom-call | flops 400000000 | bytes 2000000 | tf_op jit(solution)/shard_map/first/pallas_call | solution.py:649
  2.7 0.0 copy-start.7
  2.7 0.0 copy-start.8
  2.7 0.0 copy-start.9
  2.7 0.0 copy-start.10
  2.7 0.0 copy-start.11
  2.8 15.5 %all_to_all.30.in_ref = f32[16,40,128]{2,1,0:T(8,128)S(1)} all-to-all(f32[16,40,128]{2,1,0:T(8,128)S(1)} %get-tuple-element.17), channel_id=1, replica_groups=mesh['rve'=32,'slab'=16] {'slab'}, dimensions={0} | all-to-all | bytes 655360 | tf_op jit(solution)/shard_map/all_to_all | solution.py:561
  18.2 0.0 copy-done.7
  18.2 0.0 copy-done.8
  18.2 0.0 copy-done.9
  18.2 0.0 copy-done.10
  18.2 0.0 copy-done.11
  18.3 0.0 copy-start.1
  18.3 0.0 copy-start.3
  18.3 0.0 copy-start.4
  18.3 0.0 copy-start.5
  18.3 0.0 copy-start.6
  18.3 1.2 %columns.4 = f32[16,40,128]{2,1,0:T(8,128)S(1)} custom-call(f32[16,40,128]{2,1,0:T(8,128)S(1)} %all_to_all.30.in_ref, bf16[256,256]{1,0:T(8,128)(2,1)S(1)} %copy-done.10, bf16[256,256]{1,0:T(8,128)(2,1)S(1)} %copy-done.9, f32[2,64,128]{2,1,0:T(8,128)S(1)} %copy-done.11, bf16[256,256]{1,0:T(8,128)(2,1)S(1)} %copy-done.8, bf16[256,256]{1,0:T(8,128)(2,1)S(1)} %copy-done.7), custom_call_target="tpu_custom_call" | custom-call | flops 400000000 | bytes 2000000 | tf_op jit(solution)/shard_map/columns/pallas_call | solution.py:645
  19.5 0.0 copy-start
  19.5 0.0 copy-start.2
  19.5 10.8 %all_to_all.31.in_ref = f32[16,40,128]{2,1,0:T(8,128)S(1)} all-to-all(f32[16,40,128]{2,1,0:T(8,128)S(1)} %columns.4), channel_id=1, replica_groups=mesh['rve'=32,'slab'=16] {'slab'}, dimensions={0} | all-to-all | bytes 655360 | tf_op jit(solution)/shard_map/all_to_all | solution.py:561
  30.3 0.0 copy-done.1
  30.3 0.0 copy-done.3
  30.3 0.0 copy-done.4
  30.3 0.0 copy-done.5
  30.4 0.0 copy-done.6
  30.4 0.0 copy-done
  30.4 0.0 copy-done.2
  30.4 1.4 %middle.1 = (f32[16,40,128]{2,1,0:T(8,128)S(1)}, f32[768,128]{1,0:T(8,128)S(1)}) custom-call(f32[8,128]{1,0:T(8,128)S(1)} %get-tuple-element.16.macro_ref, s32[128,128]{1,0:T(8,128)S(1)} %bitcast.22, s32[384,128]{1,0:T(8,128)S(1)} %bitcast.19, f32[768,128]{1,0:T(8,128)S(1)} %bitcast.25, f32[16,40,128]{2,1,0:T(8,128)S(1)} %all_to_all.31.in_ref, ...), custom_call_target="tpu_custom_call" | custom-call | flops 800000000 | bytes 4000000 | tf_op jit(solution)/shard_map/middle/pallas_call | solution.py:653
  31.8 10.5 %all_to_all.32.in_ref = f32[16,40,128]{2,1,0:T(8,128)S(1)} all-to-all(f32[16,40,128]{2,1,0:T(8,128)S(1)} %get-tuple-element.19), channel_id=1, replica_groups=mesh['rve'=32,'slab'=16] {'slab'}, dimensions={0} | all-to-all | bytes 655360 | tf_op jit(solution)/shard_map/all_to_all | solution.py:561
  42.3 1.2 %columns.5 = f32[16,40,128]{2,1,0:T(8,128)S(1)} custom-call(f32[16,40,128]{2,1,0:T(8,128)S(1)} %all_to_all.32.in_ref, bf16[256,256]{1,0:T(8,128)(2,1)S(1)} %copy-done.10, bf16[256,256]{1,0:T(8,128)(2,1)S(1)} %copy-done.9, f32[2,64,128]{2,1,0:T(8,128)S(1)} %copy-done.11, bf16[256,256]{1,0:T(8,128)(2,1)S(1)} %copy-done.8, bf16[256,256]{1,0:T(8,128)(2,1)S(1)} %copy-done.7), custom_call_target="tpu_custom_call" | custom-call | flops 400000000 | bytes 2000000 | tf_op jit(solution)/shard_map/columns/pallas_call | solution.py:645
  43.5 10.5 %all_to_all.33.in_ref = f32[16,40,128]{2,1,0:T(8,128)S(1)} all-to-all(f32[16,40,128]{2,1,0:T(8,128)S(1)} %columns.5), channel_id=1, replica_groups=mesh['rve'=32,'slab'=16] {'slab'}, dimensions={0} | all-to-all | bytes 655360 | tf_op jit(solution)/shard_map/all_to_all | solution.py:561
  54.0 1.0 %last.1 = f32[16,1,128]{2,1,0:T(1,128)S(1)} custom-call(s32[128,128]{1,0:T(8,128)S(1)} %bitcast.23, s32[384,128]{1,0:T(8,128)S(1)} %bitcast.20, f32[768,128]{1,0:T(8,128)S(1)} %get-tuple-element.18.elastic_ref, f32[16,40,128]{2,1,0:T(8,128)S(1)} %all_to_all.33.in_ref, bf16[4,256,256]{2,1,0:T(8,128)(2,1)S(1)} %copy-done, bf16[256,256]{1,0:T(8,128)(2,1)S(1)} %copy-done.2), custom_call_target="tpu_custom_call" | custom-call | flops 400000000 | bytes 2000000 | tf_op jit(solution)/shard_map/last/pallas_call | solution.py:657
  55.0 9.0 %all_to_all.34.in_ref = f32[16,1,128]{2,1,0:T(1,128)S(1)} all-to-all(f32[16,1,128]{2,1,0:T(1,128)S(1)} %last.1), channel_id=1, replica_groups=mesh['rve'=32,'slab'=16] {'slab'}, dimensions={0} | all-to-all | bytes 16384 | tf_op jit(solution)/shard_map/all_to_all | solution.py:561
  64.1 28.5 %all_to_all.35.in_ref = f32[32,1,128]{2,1,0:T(1,128)S(1)} all-to-all(f32[32,1,128]{2,1,0:T(1,128)S(1)} %totals.1), channel_id=1, replica_groups={{256,272,288,304,320,336,352,368,384,400,416,432,448,464,480,496,0,16,3..., dimensions={0} | all-to-all | bytes 32768 | tf_op jit(solution)/shard_map/all_to_all | solution.py:661
  92.6 1.1 %assembly.1 = (f32[1,6]{1,0:T(1,128)}, f32[6,1,6]{2,1,0:T(1,128)}, f32[60,60]{1,0:T(8,128)}, f32[3,20]{1,0:T(4,128)}) custom-call(f32[192,128]{1,0:T(8,128)S(1)} %get-tuple-element.14.basis_ref, bf16[2,128,192]{2,1,0:T(8,128)(2,1)S(1)} %get-tuple-element.15.turned_ref, f32[32,1,128]{2,1,0:T(1,128)S(1)} %all_to_all.35.in_ref), custom_call_target="tpu_custom_call" | custom-call | flops 10000000 | bytes 200000 | tf_op jit(solution)/shard_map/assembly/pallas_call | solution.py:664
  (1 shorter events, 0.0 us)
Async XLA Ops:
  2.7 15.5 %copy-start.7 = (bf16[256,256]{1,0:T(8,128)(2,1)S(1)}, bf16[256,256]{1,0:T(8,128)(2,1)}, u32[]{:S(2)}) copy-start(bf16[256,256]{1,0:T(8,128)(2,1)} %constant.26.clone.back_four) | copy-start | bytes 393220
  2.7 15.5 %copy-start.8 = (bf16[256,256]{1,0:T(8,128)(2,1)S(1)}, bf16[256,256]{1,0:T(8,128)(2,1)}, u32[]{:S(2)}) copy-start(bf16[256,256]{1,0:T(8,128)(2,1)} %constant.25.clone.four) | copy-start | bytes 393220
  2.7 15.5 %copy-start.9 = (bf16[256,256]{1,0:T(8,128)(2,1)S(1)}, bf16[256,256]{1,0:T(8,128)(2,1)}, u32[]{:S(2)}) copy-start(bf16[256,256]{1,0:T(8,128)(2,1)} %constant.23.clone.back_columns) | copy-start | bytes 393220
  2.7 15.5 %copy-start.10 = (bf16[256,256]{1,0:T(8,128)(2,1)S(1)}, bf16[256,256]{1,0:T(8,128)(2,1)}, u32[]{:S(2)}) copy-start(bf16[256,256]{1,0:T(8,128)(2,1)} %constant.22.clone.columns) | copy-start | bytes 393220
  2.7 15.5 %copy-start.11 = (f32[2,64,128]{2,1,0:T(8,128)S(1)}, f32[2,64,128]{2,1,0:T(8,128)}, u32[]{:S(2)}) copy-start(f32[2,64,128]{2,1,0:T(8,128)} %constant.24.clone.twist_ref) | copy-start | bytes 196612
  18.3 12.1 %copy-start.1 = (s32[1,3,4,4096]{3,2,1,0:T(4,128)S(1)}, s32[1,3,4,4096]{3,2,1,0:T(4,128)}, u32[]{:S(2)}) copy-start(s32[1,3,4,4096]{3,2,1,0:T(4,128)} %param.15) | copy-start | bytes 589828
  18.3 12.1 %copy-start.3 = (s32[4,4096]{1,0:T(4,128)S(1)}, s32[4,4096]{1,0:T(4,128)}, u32[]{:S(2)}) copy-start(s32[4,4096]{1,0:T(4,128)} %param.14) | copy-start | bytes 196612
  18.3 12.1 %copy-start.4 = (f32[1,6,4,4096]{3,2,1,0:T(4,128)S(1)}, f32[1,6,4,4096]{3,2,1,0:T(4,128)}, u32[]{:S(2)}) copy-start(f32[1,6,4,4096]{3,2,1,0:T(4,128)} %param.16) | copy-start | bytes 1179652
  18.3 12.1 %copy-start.5 = (bf16[4,256,256]{2,1,0:T(8,128)(2,1)S(1)}, bf16[4,256,256]{2,1,0:T(8,128)(2,1)}, u32[]{:S(2)}) copy-start(bf16[4,256,256]{2,1,0:T(8,128)(2,1)} %constant.18.clone.depth_hbm.depth) | copy-start | bytes 1572868
  18.3 12.1 %copy-start.6 = (bf16[256,256]{1,0:T(8,128)(2,1)S(1)}, bf16[256,256]{1,0:T(8,128)(2,1)}, u32[]{:S(2)}) copy-start(bf16[256,256]{1,0:T(8,128)(2,1)} %constant.20.clone.rows_hbm.rows) | copy-start | bytes 393220
  19.5 10.8 %copy-start = (bf16[4,256,256]{2,1,0:T(8,128)(2,1)S(1)}, bf16[4,256,256]{2,1,0:T(8,128)(2,1)}, u32[]{:S(2)}) copy-start(bf16[4,256,256]{2,1,0:T(8,128)(2,1)} %constant.19.clone.back_depth) | copy-start | bytes 1572868
  19.5 10.8 %copy-start.2 = (bf16[256,256]{1,0:T(8,128)(2,1)S(1)}, bf16[256,256]{1,0:T(8,128)(2,1)}, u32[]{:S(2)}) copy-start(bf16[256,256]{1,0:T(8,128)(2,1)} %constant.21.clone.back_rows) | copy-start | bytes 393220

commit v6 on v5

--- a/solution.py
+++ b/solution.py
@@ -222,11 +222,13 @@
 
 
 def plane_waves():
-    row = lax.broadcasted_iota(jnp.int32, (128, 128), 0)
-    lane = lax.broadcasted_iota(jnp.int32, (128, 128), 1)
-    ky = 4 * lax.shift_right_logical(row, 3) + lax.bitwise_and(row, 3)
-    ky = jnp.where(ky < GRID // 2, ky, ky - GRID)
-    return ky.astype(jnp.float32), lax.bitwise_and(lane, 31).astype(jnp.float32)
+    row = lax.broadcasted_iota(jnp.int32, (8, 128), 0)
+    lane = lax.broadcasted_iota(jnp.int32, (8, 128), 1)
+    inner = lax.bitwise_and(row, 3).astype(jnp.float32)
+    depth = lax.bitwise_and(lane, 31).astype(jnp.float32)
+    starts = [4.0 * d if d < 8 else 4.0 * d - GRID for d in range(16)]
+    wave_y = jnp.concatenate([inner + start for start in starts], axis=0)
+    return wave_y, jnp.concatenate([depth] * 16, axis=0)
 
 
 def forward_planes(xs, bs, depth, rows, out_ref):
@@ -314,7 +316,7 @@
     for c in range(6):
         table = jnp.where(row == c, macro[c], table)
     macro_ref[...] = table
-    for copy in copies[2:]:
+    for copy in copies[2:5]:
         copy.wait()
     for plane in range(PLANES):
         elastic = [macro[c] - every_fourth(plastic_ref, c * 128, plane) for c in range(6)]
@@ -323,6 +325,8 @@
         stress = material(elastic, phases, flags)[0]
         for c in range(6):
             put_rows(xs, pl.ds(plane * 192 + c * 32, 32), stress[c])
+    for copy in copies[5:]:
+        copy.wait()
     basis = basis_of(points, conn_ref)
     basis_ref[...] = basis
     high, low = split(jnp.transpose(basis))
@@ -382,22 +386,24 @@
             for b in range(a, 6):
                 collect(at, scaled * trial[b])
                 at += 1
-    row = lax.broadcasted_iota(jnp.int32, (128, 128), 0)
-    lines = jnp.zeros((128, 128), jnp.float32)
+    row = lax.broadcasted_iota(jnp.int32, (8, 128), 0)
+    groups = [jnp.zeros((8, 128), jnp.float32)] * 16
+    totals = [jnp.sum(value, axis=0, keepdims=True) for value in sums]
 
     def place(at, value):
-        return jnp.where(row == at, jnp.broadcast_to(value, (128, 128)), lines)
-
-    totals = [jnp.sum(value, axis=0, keepdims=True) for value in sums]
+        here = jnp.broadcast_to(value, (8, 128))
+        groups[at // 8] = jnp.where(row == at % 8, here, groups[at // 8])
+
     for c in range(7):
-        lines = place(c, totals[c])
+        place(c, totals[c])
     at = 7
     for a in range(6):
         for b in range(a, 6):
-            lines = place(OUTER_AT + 6 * a + b, totals[at])
+            place(OUTER_AT + 6 * a + b, totals[at])
             if a != b:
-                lines = place(OUTER_AT + 6 * b + a, totals[at])
+                place(OUTER_AT + 6 * b + a, totals[at])
             at += 1
+    lines = jnp.concatenate(groups, axis=0)
     ones = jnp.ones((SLABS, 128), jnp.float32)
     line = lax.dot_general(
         ones, lines, (((1,), (1,)), ((), ())),
@@ -428,10 +434,9 @@
     spectrum = spectrum + mm(ys[count:, :], four[...])
     xx, xy, xz, y, z = (spectrum[c * 64 : (c + 1) * 64] for c in range(FIELDS))
 
-    shape = (64, 256)
+    shape = (64, 128)
     row = lax.broadcasted_iota(jnp.int32, shape, 0)
     lane = lax.broadcasted_iota(jnp.int32, shape, 1)
-    lane = lax.bitwise_and(lane, 127)
     kx = 16 * lax.shift_right_logical(lane, 5) + lax.shift_right_logical(row, 2)
     ky = 4 * lax.axis_index("slab") + lax.bitwise_and(row, 3)
     kz = lax.bitwise_and(lane, 31)
@@ -447,6 +452,8 @@
     coupling = (REFERENCE_LAME + REFERENCE_SHEAR) / (
         REFERENCE_SHEAR * (REFERENCE_LAME + 2.0 * REFERENCE_SHEAR)
     )
+    xi = [jnp.concatenate([value, value], axis=1) for value in xi]
+    inverse = jnp.concatenate([inverse, inverse], axis=1)
     scaled = inverse * (1.0 / (2.0 * REFERENCE_SHEAR))
     traction = [xi[0] * xx + xi[1] * xy + xi[2] * xz, xi[0] * xy + y, xi[0] * xz + z]
     load = xi[0] * traction[0] + xi[1] * traction[1] + xi[2] * traction[2]
@@ -491,12 +498,12 @@
 def assembly_kernel(
     points, basis_ref, turned_ref, in_ref, stress_ref, tangent_ref, stiffness_ref, forces_ref
 ):
-    half = points // 2
-    own = lax.rem(lax.axis_index("rve") + points - half, points)
+    start = first_of(points)
+    own = lax.rem(lax.axis_index("rve") + points - start, points)
     own_outputs(in_ref[own] * (1.0 / VOXELS), stress_ref, tangent_ref)
     shape = (points, 128)
     sums = in_ref[...].reshape(points, 128) * (1.0 / VOXELS)
-    sums = jnp.concatenate([sums[half:], sums[:half]], axis=0)
+    sums = jnp.concatenate([sums[points - start :], sums[: points - start]], axis=0)
     basis = [basis_ref[a * points : (a + 1) * points, :] for a in range(6)]
     mean_shear = 2.0 * SHEAR_MODULUS * sums[:, 6:7]
 
@@ -557,6 +564,10 @@
     return [pltpu.VMEM((768, 256), BF16), pltpu.VMEM((256, 768), BF16)]
 
 
+def first_of(points):
+    return points // 2 + 1 if points > 1 else 0
+
+
 def exchange(array):
     return lax.all_to_all(array, "slab", split_axis=0, concat_axis=0, tiled=True)
 
@@ -656,8 +667,7 @@
     planes = apply_columns(spectrum)
     partial = last(phases, flags, elastic, planes, back_depth, back_line)
     everyone = totals(exchange(partial))
-    half = points // 2
-    turned = [*range(half, points), *range(half)]
+    turned = [(g + first_of(points)) % points for g in range(points)]
     everyone = lax.all_to_all(
         everyone, "rve", 0, 0, tiled=True, axis_index_groups=[turned]
     )

time: 94 us -> 93.6 us (level)
  no operation moved by 1% of the time
where the time goes in v6:
time: 93.6 us; the launch traced here: 93.2 us
  blocking collectives  84.5 us (90%)
  Pallas kernels  7.77 us (8%)
    all_to_all x5, blocking collectives, exchange(): lax.all_to_all(array, 'slab', split_axis=0, concat_axis=0, tiled=True)  56.3 us
    all_to_all x1, blocking collectives, on_device(): lax.all_to_all(everyone, 'rve', 0, 0, tiled=True, axis_index_groups=[turn...  28.3 us
    pallas_call x2, Pallas kernels, apply_columns(): columns(exchange(array), column, back_column, twist, four, back_four)  2.38 us
    pallas_call x1, Pallas kernels, on_device(): first(*(pltpu.with_memory_space_constraint(operand, pltpu.HBM) for operan...  1.92 us

profile of v6, /device:TPU:1, one launch (start us, length us, event | category | flops | bytes accessed | tf_op | source)
XLA Modules:
  0.0 93.2 jit_solution(16534763299754898000)
XLA Ops:
  0.6 1.9 %first.1 = (f32[16,40,128]{2,1,0:T(8,128)S(1)}, f32[8,128]{1,0:T(8,128)S(1)}, f32[192,128]{1,0:T(8,128)S(1)}, bf16[2,128,192]{2,1,0:T(8,128)(2,1)S(1)}) custom-call(s32[4,8]{1,0:T(4,128)} %conn_hbm.1, f32[3,20]{1,0:T(4,128)} %bitcast.27, s32[128,128]{1,0:T(8,128)} %bitcast.21, s32[384,128]{1,0:T(8,128)} %bitcast.18, f32[768,128]{1,0:T(8,128)} %bitcast.24, ...), custom_call_target="tpu_custom_call" | custom-call | flops 400000000 | bytes 2000000 | tf_op jit(solution)/shard_map/first/pallas_call | solution.py:660
  2.6 0.0 copy-start.7
  2.6 0.0 copy-start.8
  2.6 0.0 copy-start.9
  2.6 0.0 copy-start.10
  2.6 0.0 copy-start.11
  2.6 15.5 %all_to_all.30.in_ref = f32[16,40,128]{2,1,0:T(8,128)S(1)} all-to-all(f32[16,40,128]{2,1,0:T(8,128)S(1)} %get-tuple-element.17), channel_id=1, replica_groups=mesh['rve'=32,'slab'=16] {'slab'}, dimensions={0} | all-to-all | bytes 655360 | tf_op jit(solution)/shard_map/all_to_all | solution.py:572
  18.1 0.0 copy-done.7
  18.1 0.0 copy-done.8
  18.1 0.0 copy-done.9
  18.1 0.0 copy-done.10
  18.1 0.0 copy-done.11
  18.1 0.0 copy-start.1
  18.1 0.0 copy-start.3
  18.1 0.0 copy-start.4
  18.2 0.0 copy-start.5
  18.2 0.0 copy-start.6
  18.2 1.2 %columns.4 = f32[16,40,128]{2,1,0:T(8,128)S(1)} custom-call(f32[16,40,128]{2,1,0:T(8,128)S(1)} %all_to_all.30.in_ref, bf16[256,256]{1,0:T(8,128)(2,1)S(1)} %copy-done.10, bf16[256,256]{1,0:T(8,128)(2,1)S(1)} %copy-done.9, f32[2,64,128]{2,1,0:T(8,128)S(1)} %copy-done.11, bf16[256,256]{1,0:T(8,128)(2,1)S(1)} %copy-done.8, bf16[256,256]{1,0:T(8,128)(2,1)S(1)} %copy-done.7), custom_call_target="tpu_custom_call" | custom-call | flops 400000000 | bytes 2000000 | tf_op jit(solution)/shard_map/columns/pallas_call | solution.py:656
  19.4 0.0 copy-start
  19.4 0.0 copy-start.2
  19.4 10.8 %all_to_all.31.in_ref = f32[16,40,128]{2,1,0:T(8,128)S(1)} all-to-all(f32[16,40,128]{2,1,0:T(8,128)S(1)} %columns.4), channel_id=1, replica_groups=mesh['rve'=32,'slab'=16] {'slab'}, dimensions={0} | all-to-all | bytes 655360 | tf_op jit(solution)/shard_map/all_to_all | solution.py:572
  30.2 0.0 copy-done.1
  30.2 0.0 copy-done.3
  30.2 0.0 copy-done.4
  30.2 0.0 copy-done.5
  30.2 0.0 copy-done.6
  30.2 0.0 copy-done
  30.2 0.0 copy-done.2
  30.2 1.4 %middle.1 = (f32[16,40,128]{2,1,0:T(8,128)S(1)}, f32[768,128]{1,0:T(8,128)S(1)}) custom-call(f32[8,128]{1,0:T(8,128)S(1)} %get-tuple-element.16.macro_ref, s32[128,128]{1,0:T(8,128)S(1)} %bitcast.22, s32[384,128]{1,0:T(8,128)S(1)} %bitcast.19, f32[768,128]{1,0:T(8,128)S(1)} %bitcast.25, f32[16,40,128]{2,1,0:T(8,128)S(1)} %all_to_all.31.in_ref, ...), custom_call_target="tpu_custom_call" | custom-call | flops 800000000 | bytes 4000000 | tf_op jit(solution)/shard_map/middle/pallas_call | solution.py:664
  31.6 10.5 %all_to_all.32.in_ref = f32[16,40,128]{2,1,0:T(8,128)S(1)} all-to-all(f32[16,40,128]{2,1,0:T(8,128)S(1)} %get-tuple-element.19), channel_id=1, replica_groups=mesh['rve'=32,'slab'=16] {'slab'}, dimensions={0} | all-to-all | bytes 655360 | tf_op jit(solution)/shard_map/all_to_all | solution.py:572
  42.1 1.2 %columns.5 = f32[16,40,128]{2,1,0:T(8,128)S(1)} custom-call(f32[16,40,128]{2,1,0:T(8,128)S(1)} %all_to_all.32.in_ref, bf16[256,256]{1,0:T(8,128)(2,1)S(1)} %copy-done.10, bf16[256,256]{1,0:T(8,128)(2,1)S(1)} %copy-done.9, f32[2,64,128]{2,1,0:T(8,128)S(1)} %copy-done.11, bf16[256,256]{1,0:T(8,128)(2,1)S(1)} %copy-done.8, bf16[256,256]{1,0:T(8,128)(2,1)S(1)} %copy-done.7), custom_call_target="tpu_custom_call" | custom-call | flops 400000000 | bytes 2000000 | tf_op jit(solution)/shard_map/columns/pallas_call | solution.py:656
  43.3 10.5 %all_to_all.33.in_ref = f32[16,40,128]{2,1,0:T(8,128)S(1)} all-to-all(f32[16,40,128]{2,1,0:T(8,128)S(1)} %columns.5), channel_id=1, replica_groups=mesh['rve'=32,'slab'=16] {'slab'}, dimensions={0} | all-to-all | bytes 655360 | tf_op jit(solution)/shard_map/all_to_all | solution.py:572
  53.8 1.0 %last.1 = f32[16,1,128]{2,1,0:T(1,128)S(1)} custom-call(s32[128,128]{1,0:T(8,128)S(1)} %bitcast.23, s32[384,128]{1,0:T(8,128)S(1)} %bitcast.20, f32[768,128]{1,0:T(8,128)S(1)} %get-tuple-element.18.elastic_ref, f32[16,40,128]{2,1,0:T(8,128)S(1)} %all_to_all.33.in_ref, bf16[4,256,256]{2,1,0:T(8,128)(2,1)S(1)} %copy-done, bf16[256,256]{1,0:T(8,128)(2,1)S(1)} %copy-done.2), custom_call_target="tpu_custom_call" | custom-call | flops 400000000 | bytes 2000000 | tf_op jit(solution)/shard_map/last/pallas_call | solution.py:668
  54.8 9.0 %all_to_all.34.in_ref = f32[16,1,128]{2,1,0:T(1,128)S(1)} all-to-all(f32[16,1,128]{2,1,0:T(1,128)S(1)} %last.1), channel_id=1, replica_groups=mesh['rve'=32,'slab'=16] {'slab'}, dimensions={0} | all-to-all | bytes 16384 | tf_op jit(solution)/shard_map/all_to_all | solution.py:572
  63.9 28.3 %all_to_all.35.in_ref = f32[32,1,128]{2,1,0:T(1,128)S(1)} all-to-all(f32[32,1,128]{2,1,0:T(1,128)S(1)} %totals.1), channel_id=1, replica_groups={{272,288,304,320,336,352,368,384,400,416,432,448,464,480,496,0,16,32,48..., dimensions={0} | all-to-all | bytes 32768 | tf_op jit(solution)/shard_map/all_to_all | solution.py:671
  92.2 1.1 %assembly.1 = (f32[1,6]{1,0:T(1,128)}, f32[6,1,6]{2,1,0:T(1,128)}, f32[60,60]{1,0:T(8,128)}, f32[3,20]{1,0:T(4,128)}) custom-call(f32[192,128]{1,0:T(8,128)S(1)} %get-tuple-element.14.basis_ref, bf16[2,128,192]{2,1,0:T(8,128)(2,1)S(1)} %get-tuple-element.15.turned_ref, f32[32,1,128]{2,1,0:T(1,128)S(1)} %all_to_all.35.in_ref), custom_call_target="tpu_custom_call" | custom-call | flops 10000000 | bytes 200000 | tf_op jit(solution)/shard_map/assembly/pallas_call | solution.py:674
  (1 shorter events, 0.0 us)
Async XLA Ops:
  2.6 15.5 %copy-start.7 = (bf16[256,256]{1,0:T(8,128)(2,1)S(1)}, bf16[256,256]{1,0:T(8,128)(2,1)}, u32[]{:S(2)}) copy-start(bf16[256,256]{1,0:T(8,128)(2,1)} %constant.26.clone.back_four) | copy-start | bytes 393220
  2.6 15.5 %copy-start.8 = (bf16[256,256]{1,0:T(8,128)(2,1)S(1)}, bf16[256,256]{1,0:T(8,128)(2,1)}, u32[]{:S(2)}) copy-start(bf16[256,256]{1,0:T(8,128)(2,1)} %constant.25.clone.four) | copy-start | bytes 393220
  2.6 15.5 %copy-start.9 = (bf16[256,256]{1,0:T(8,128)(2,1)S(1)}, bf16[256,256]{1,0:T(8,128)(2,1)}, u32[]{:S(2)}) copy-start(bf16[256,256]{1,0:T(8,128)(2,1)} %constant.23.clone.back_columns) | copy-start | bytes 393220
  2.6 15.5 %copy-start.10 = (bf16[256,256]{1,0:T(8,128)(2,1)S(1)}, bf16[256,256]{1,0:T(8,128)(2,1)}, u32[]{:S(2)}) copy-start(bf16[256,256]{1,0:T(8,128)(2,1)} %constant.22.clone.columns) | copy-start | bytes 393220
  2.6 15.5 %copy-start.11 = (f32[2,64,128]{2,1,0:T(8,128)S(1)}, f32[2,64,128]{2,1,0:T(8,128)}, u32[]{:S(2)}) copy-start(f32[2,64,128]{2,1,0:T(8,128)} %constant.24.clone.twist_ref) | copy-start | bytes 196612
  18.1 12.1 %copy-start.1 = (s32[1,3,4,4096]{3,2,1,0:T(4,128)S(1)}, s32[1,3,4,4096]{3,2,1,0:T(4,128)}, u32[]{:S(2)}) copy-start(s32[1,3,4,4096]{3,2,1,0:T(4,128)} %param.15) | copy-start | bytes 589828
  18.1 12.1 %copy-start.3 = (s32[4,4096]{1,0:T(4,128)S(1)}, s32[4,4096]{1,0:T(4,128)}, u32[]{:S(2)}) copy-start(s32[4,4096]{1,0:T(4,128)} %param.14) | copy-start | bytes 196612
  18.1 12.0 %copy-start.4 = (f32[1,6,4,4096]{3,2,1,0:T(4,128)S(1)}, f32[1,6,4,4096]{3,2,1,0:T(4,128)}, u32[]{:S(2)}) copy-start(f32[1,6,4,4096]{3,2,1,0:T(4,128)} %param.16) | copy-start | bytes 1179652
  18.2 12.0 %copy-start.5 = (bf16[4,256,256]{2,1,0:T(8,128)(2,1)S(1)}, bf16[4,256,256]{2,1,0:T(8,128)(2,1)}, u32[]{:S(2)}) copy-start(bf16[4,256,256]{2,1,0:T(8,128)(2,1)} %constant.18.clone.depth_hbm.depth) | copy-start | bytes 1572868
  18.2 12.0 %copy-start.6 = (bf16[256,256]{1,0:T(8,128)(2,1)S(1)}, bf16[256,256]{1,0:T(8,128)(2,1)}, u32[]{:S(2)}) copy-start(bf16[256,256]{1,0:T(8,128)(2,1)} %constant.20.clone.rows_hbm.rows) | copy-start | bytes 393220
  19.4 10.8 %copy-start = (bf16[4,256,256]{2,1,0:T(8,128)(2,1)S(1)}, bf16[4,256,256]{2,1,0:T(8,128)(2,1)}, u32[]{:S(2)}) copy-start(bf16[4,256,256]{2,1,0:T(8,128)(2,1)} %constant.19.clone.back_depth) | copy-start | bytes 1572868
  19.4 10.8 %copy-start.2 = (bf16[256,256]{1,0:T(8,128)(2,1)S(1)}, bf16[256,256]{1,0:T(8,128)(2,1)}, u32[]{:S(2)}) copy-start(bf16[256,256]{1,0:T(8,128)(2,1)} %constant.21.clone.back_rows) | copy-start | bytes 393220

commit v7 on v6

--- a/solution.py
+++ b/solution.py
@@ -114,20 +114,22 @@
     return jnp.dot(a, b, preferred_element_type=jnp.float32)
 
 
-def from_left(table_ref, data_ref):
-    both = mm(table_ref[...], data_ref[...])
+def from_left_values(table_ref, pairs):
+    both = jnp.concatenate([jnp.concatenate(pair, axis=0) for pair in pairs], axis=1)
+    total = mm(table_ref[:128, :], both)
+    return total + mm(table_ref[128:, :128], both[:128])
+
+
+def from_left_halves(table_ref, pairs):
+    both = jnp.concatenate([jnp.concatenate(pair, axis=0) for pair in pairs], axis=1)
+    both = mm(table_ref[...], both)
     return both[:128] + both[128:]
 
 
-def from_left_chained(table_ref, data_ref):
-    total = mm(table_ref[:128, :], data_ref[...])
-    return total + mm(table_ref[128:, :128], data_ref[:128, :])
-
-
-def from_right(data_ref, table_ref):
+def from_right(tiles, table_ref):
     results = []
-    for l in range(PLANES):
-        both = mm(data_ref[l * 192 : (l + 1) * 192, :], table_ref[l])
+    for l, tile in enumerate(tiles):
+        both = mm(jnp.concatenate(split(tile), axis=1), table_ref[l])
         results.append(both[:, :128] + both[:, 128:])
     return results
 
@@ -160,10 +162,14 @@
     return slope
 
 
-def macro_strain(point, conn_ref, disp_ref):
+def point_slopes(point):
     low, high = jnp.float32(GAUSS_LOW), jnp.float32(GAUSS_HIGH)
     bits = [lax.bitwise_and(lax.shift_right_logical(point, d), 1) for d in range(3)]
     slope = slopes_of(bits, low, high)
+    return [[slope(corner, d) for d in range(3)] for corner in range(8)]
+
+
+def macro_strain(point, slopes, conn_ref, disp_ref):
     element = lax.shift_right_logical(point, 3)
     grad = [[jnp.float32(0.0)] * 3 for _ in range(3)]
     for corner in range(8):
@@ -171,7 +177,7 @@
         for k in range(3):
             u = disp_ref[k, node]
             for d in range(3):
-                grad[k][d] = grad[k][d] + slope(corner, d) * u
+                grad[k][d] = grad[k][d] + slopes[corner][d] * u
     strain = []
     for i, j in TENSOR_PAIRS:
         strain.append(grad[i][i] if i == j else 0.5 * (grad[i][j] + grad[j][i]))
@@ -209,18 +215,6 @@
     return ref[pl.ds(start + plane, 32, stride=4), :]
 
 
-def put_rows(ref, rows, value):
-    high, low = split(value)
-    ref[rows, 0:128] = high
-    ref[rows, 128:256] = low
-
-
-def put_columns(ref, start, count, columns, value):
-    high, low = split(value)
-    ref[pl.ds(start, count), columns] = high
-    ref[pl.ds(128 + start, count), columns] = low
-
-
 def plane_waves():
     row = lax.broadcasted_iota(jnp.int32, (8, 128), 0)
     lane = lax.broadcasted_iota(jnp.int32, (8, 128), 1)
@@ -231,14 +225,14 @@
     return wave_y, jnp.concatenate([depth] * 16, axis=0)
 
 
-def forward_planes(xs, bs, depth, rows, out_ref):
-    tiles = gather_chunks(from_right(xs, depth))
+def forward_planes(stresses, depth, rows, out_ref):
+    tiles = gather_chunks(from_right(stresses, depth))
     tiles = [roll_chunks(tile, -s) for s, tile in enumerate(tiles)]
-    for c in range(6):
-        for s in range(4):
-            block = tiles[s][c * 32 : (c + 1) * 32]
-            put_columns(bs, s * 32, 32, pl.ds(c * 128, 128), block)
-    spectrum = from_left(rows, bs)
+    pairs = [
+        split(jnp.concatenate([tile[c * 32 : (c + 1) * 32] for tile in tiles], axis=0))
+        for c in range(6)
+    ]
+    spectrum = from_left_halves(rows, pairs)
     xx, yy, zz, yz, xz, xy = (spectrum[:, c * 128 : (c + 1) * 128] for c in range(6))
     wave_y, wave_z = plane_waves()
     fields = (xx, xy, xz, wave_y * yy + wave_z * yz, wave_y * yz + wave_z * zz)
@@ -246,15 +240,14 @@
         out_ref[:, c * 8 : (c + 1) * 8, :] = field.reshape(16, 8, 128)
 
 
-def backward_planes(in_ref, bs, xs, depth, rows):
+def backward_planes(in_ref, depth, rows):
     xx, xy, xz, y, z = (
         in_ref[:, c * 8 : (c + 1) * 8, :].reshape(128, 128) for c in range(FIELDS)
     )
     wave_y, wave_z = plane_waves()
     yy, zz = 2.0 * (wave_y * y), 2.0 * (wave_z * z)
-    for c, value in enumerate((xx, yy, zz, wave_y * z + wave_z * y, xz, xy)):
-        put_columns(bs, 0, 128, pl.ds(c * 128, 128), value)
-    lines = from_left(rows, bs)
+    pairs = [split(value) for value in (xx, yy, zz, wave_y * z + wave_z * y, xz, xy)]
+    lines = from_left_values(rows, pairs)
     tiles = [
         jnp.concatenate(
             [lines[s * 32 : (s + 1) * 32, c * 128 : (c + 1) * 128] for c in range(6)], axis=0
@@ -262,9 +255,7 @@
         for s in range(4)
     ]
     tiles = [roll_chunks(tile, s) for s, tile in enumerate(tiles)]
-    for l, tile in enumerate(gather_chunks(tiles)):
-        put_rows(xs, pl.ds(l * 192, 192), tile)
-    return from_right(xs, depth)
+    return from_right(gather_chunks(tiles), depth)
 
 
 def basis_of(points, conn_ref):
@@ -298,7 +289,7 @@
 def first_kernel(
     points, conn_hbm, disp_hbm, phase_hbm, flag_hbm, plastic_hbm, depth_hbm, rows_hbm,
     out_ref, macro_ref, basis_ref, turned_ref,
-    conn_ref, disp_ref, phase_ref, flag_ref, plastic_ref, depth, rows, sems, xs, bs,
+    conn_ref, disp_ref, phase_ref, flag_ref, plastic_ref, depth, rows, sems,
 ):
     pairs = (
         (conn_hbm, conn_ref), (disp_hbm, disp_ref), (plastic_hbm, plastic_ref),
@@ -308,9 +299,11 @@
     copies = [pltpu.make_async_copy(a, b, sems.at[i]) for i, (a, b) in enumerate(pairs)]
     for copy in copies:
         copy.start()
+    point = lax.axis_index("rve")
+    slopes = point_slopes(point)
     for copy in copies[:2]:
         copy.wait()
-    macro = macro_strain(lax.axis_index("rve"), conn_ref, disp_ref)
+    macro = macro_strain(point, slopes, conn_ref, disp_ref)
     row = lax.broadcasted_iota(jnp.int32, (8, 128), 0)
     table = jnp.zeros((8, 128), jnp.float32)
     for c in range(6):
@@ -318,13 +311,13 @@
     macro_ref[...] = table
     for copy in copies[2:5]:
         copy.wait()
+    stresses = []
     for plane in range(PLANES):
         elastic = [macro[c] - every_fourth(plastic_ref, c * 128, plane) for c in range(6)]
         phases = every_fourth(phase_ref, 0, plane)
         flags = every_fourth(flag_ref, 0, plane)
         stress = material(elastic, phases, flags)[0]
-        for c in range(6):
-            put_rows(xs, pl.ds(plane * 192 + c * 32, 32), stress[c])
+        stresses.append(jnp.concatenate(stress, axis=0))
     for copy in copies[5:]:
         copy.wait()
     basis = basis_of(points, conn_ref)
@@ -332,15 +325,16 @@
     high, low = split(jnp.transpose(basis))
     turned_ref[0] = high
     turned_ref[1] = low
-    forward_planes(xs, bs, depth, rows, out_ref)
+    forward_planes(stresses, depth, rows, out_ref)
 
 
 def middle_kernel(
     macro_ref, phase_ref, flag_ref, plastic_ref, in_ref, back_depth, back_rows, depth, rows,
-    out_ref, elastic_ref, xs, bs,
+    out_ref, elastic_ref,
 ):
     macro = [macro_ref[c : c + 1, :] for c in range(6)]
-    correction = backward_planes(in_ref, bs, xs, back_depth, back_rows)
+    correction = backward_planes(in_ref, back_depth, back_rows)
+    stresses = []
     for plane in range(PLANES):
         elastic = []
         for c in range(6):
@@ -352,15 +346,14 @@
         phases = every_fourth(phase_ref, 0, plane)
         flags = every_fourth(flag_ref, 128, plane)
         stress = material(elastic, phases, flags)[0]
-        for c in range(6):
-            put_rows(xs, pl.ds(plane * 192 + c * 32, 32), stress[c])
-    forward_planes(xs, bs, depth, rows, out_ref)
+        stresses.append(jnp.concatenate(stress, axis=0))
+    forward_planes(stresses, depth, rows, out_ref)
 
 
 def last_kernel(
-    phase_ref, flag_ref, elastic_ref, in_ref, back_depth, back_rows, out_ref, xs, bs
+    phase_ref, flag_ref, elastic_ref, in_ref, back_depth, back_rows, out_ref
 ):
-    correction = backward_planes(in_ref, bs, xs, back_depth, back_rows)
+    correction = backward_planes(in_ref, back_depth, back_rows)
     sums = [None] * 28
 
     def collect(at, value):
@@ -412,26 +405,22 @@
     out_ref[...] = line.reshape(SLABS, 1, 128)
 
 
-def column_kernel(in_ref, columns, back_columns, twist_ref, four, back_four, out_ref, bs, ys):
-    count = 64 * FIELDS
-    for c in range(FIELDS):
-        block = in_ref[:, c * 8 : (c + 1) * 8, :].reshape(128, 128)
-        put_columns(bs, 0, 128, pl.ds(c * 128, 128), block)
-    mixed = from_left_chained(columns, bs)
+def column_kernel(in_ref, columns, back_columns, twist_ref, four, back_four, out_ref):
+    pairs = [split(in_ref[:, c * 8 : (c + 1) * 8, :].reshape(128, 128)) for c in range(FIELDS)]
+    mixed = from_left_values(columns, pairs)
     cosine, sine = twist_ref[0], twist_ref[1]
 
-    def put(c, lanes, value):
-        high, low = split(value)
-        ys[pl.ds(c * 64, 64), lanes] = high
-        ys[pl.ds(count + c * 64, 64), lanes] = low
-
+    def turn(values, table_ref):
+        high, low = split(jnp.concatenate(values, axis=0))
+        return mm(high, table_ref[...]) + mm(low, table_ref[...])
+
+    values = []
     for c in range(FIELDS):
         lanes = slice(c * 128, (c + 1) * 128)
         real, imag = mixed[:64, lanes], mixed[64:, lanes]
-        put(c, pl.ds(0, 128), real * cosine + imag * sine)
-        put(c, pl.ds(128, 128), imag * cosine - real * sine)
-    spectrum = mm(ys[:count, :], four[...])
-    spectrum = spectrum + mm(ys[count:, :], four[...])
+        turned = (real * cosine + imag * sine, imag * cosine - real * sine)
+        values.append(jnp.concatenate(turned, axis=1))
+    spectrum = turn(values, four)
     xx, xy, xz, y, z = (spectrum[c * 64 : (c + 1) * 64] for c in range(FIELDS))
 
     shape = (64, 128)
@@ -459,19 +448,19 @@
     load = xi[0] * traction[0] + xi[1] * traction[1] + xi[2] * traction[2]
     load = load * (inverse * (REFERENCE_SHEAR * coupling))
     field = [scaled * (traction[i] - xi[i] * load) for i in range(3)]
-    put(0, slice(None), 2.0 * (xi[0] * field[0]))
-    put(1, slice(None), xi[0] * field[1] + xi[1] * field[0])
-    put(2, slice(None), xi[0] * field[2] + xi[2] * field[0])
-    put(3, slice(None), field[1])
-    put(4, slice(None), field[2])
-    turned = mm(ys[:count, :], back_four[...])
-    turned = turned + mm(ys[count:, :], back_four[...])
+    values = [
+        2.0 * (xi[0] * field[0]),
+        xi[0] * field[1] + xi[1] * field[0],
+        xi[0] * field[2] + xi[2] * field[0],
+        field[1],
+        field[2],
+    ]
+    turned = turn(values, back_four)
     for c in range(FIELDS):
         real, imag = turned[c * 64 : (c + 1) * 64, :128], turned[c * 64 : (c + 1) * 64, 128:]
-        lanes = pl.ds(c * 128, 128)
-        put_columns(bs, 0, 64, lanes, real * cosine - imag * sine)
-        put_columns(bs, 64, 64, lanes, real * sine + imag * cosine)
-    result = from_left_chained(back_columns, bs)
+        first, second = real * cosine - imag * sine, real * sine + imag * cosine
+        pairs[c] = split(jnp.concatenate([first, second], axis=0))
+    result = from_left_values(back_columns, pairs)
     for c in range(FIELDS):
         out_ref[:, c * 8 : (c + 1) * 8, :] = result[:, c * 128 : (c + 1) * 128].reshape(16, 8, 128)
 
@@ -560,10 +549,6 @@
     return pl.CostEstimate(flops=flops, bytes_accessed=size, transcendentals=0)
 
 
-def plane_scratch():
-    return [pltpu.VMEM((768, 256), BF16), pltpu.VMEM((256, 768), BF16)]
-
-
 def first_of(points):
     return points // 2 + 1 if points > 1 else 0
 
@@ -612,28 +597,25 @@
             pltpu.VMEM((128, 128), jnp.int32), pltpu.VMEM((128, 128), jnp.int32),
             pltpu.VMEM((768, 128), F32), pltpu.VMEM((PLANES, 256, 256), BF16),
             pltpu.VMEM((256, 256), BF16),
-            pltpu.SemaphoreType.DMA((7,)), *plane_scratch(),
+            pltpu.SemaphoreType.DMA((7,)),
         ],
         compiler_params=params(), cost_estimate=cost(400_000_000, 2_000_000), name="first",
     )
     columns = pl.pallas_call(
         column_kernel, out_shape=block,
         in_specs=[VMEM] * 6, out_specs=VMEM,
-        scratch_shapes=[
-            pltpu.VMEM((256, 128 * FIELDS), BF16), pltpu.VMEM((128 * FIELDS, 256), BF16),
-        ],
         compiler_params=params(), cost_estimate=cost(400_000_000, 2_000_000), name="columns",
     )
     middle = pl.pallas_call(
         middle_kernel, out_shape=(block, jax.ShapeDtypeStruct((768, 128), F32)),
         in_specs=[VMEM] * 9, out_specs=(VMEM, VMEM),
-        scratch_shapes=plane_scratch(), compiler_params=params(),
+        compiler_params=params(),
         cost_estimate=cost(800_000_000, 4_000_000), name="middle",
     )
     last = pl.pallas_call(
         last_kernel, out_shape=jax.ShapeDtypeStruct((SLABS, 1, 128), F32),
         in_specs=[VMEM] * 6, out_specs=VMEM,
-        scratch_shapes=plane_scratch(), compiler_params=params(),
+        compiler_params=params(),
         cost_estimate=cost(400_000_000, 2_000_000), name="last",
     )
     totals = pl.pallas_call(

time: 93.6 us -> 93.1 us (level)
  no operation moved by 1% of the time
where the time goes in v7:
time: 93.1 us; the launch traced here: 92.7 us
  blocking collectives  84.5 us (91%)
  Pallas kernels  7.29 us (8%)
    all_to_all x5, blocking collectives, exchange(): lax.all_to_all(array, 'slab', split_axis=0, concat_axis=0, tiled=True)  56.3 us
    all_to_all x1, blocking collectives, on_device(): lax.all_to_all(everyone, 'rve', 0, 0, tiled=True, axis_index_groups=[turn...  28.3 us
    pallas_call x2, Pallas kernels, apply_columns(): columns(exchange(array), column, back_column, twist, four, back_four)  2.13 us
    pallas_call x1, Pallas kernels, on_device(): first(*(pltpu.with_memory_space_constraint(operand, pltpu.HBM) for operan...  1.91 us

profile of v7, /device:TPU:1, one launch (start us, length us, event | category | flops | bytes accessed | tf_op | source)
XLA Modules:
  0.0 92.7 jit_solution(6676955272813875352)
XLA Ops:
  0.6 1.9 %first.1 = (f32[16,40,128]{2,1,0:T(8,128)S(1)}, f32[8,128]{1,0:T(8,128)S(1)}, f32[192,128]{1,0:T(8,128)S(1)}, bf16[2,128,192]{2,1,0:T(8,128)(2,1)S(1)}) custom-call(s32[4,8]{1,0:T(4,128)} %conn_hbm.1, f32[3,20]{1,0:T(4,128)} %bitcast.27, s32[128,128]{1,0:T(8,128)} %bitcast.21, s32[384,128]{1,0:T(8,128)} %bitcast.18, f32[768,128]{1,0:T(8,128)} %bitcast.24, ...), custom_call_target="tpu_custom_call" | custom-call | flops 400000000 | bytes 2000000 | tf_op jit(solution)/shard_map/first/pallas_call | solution.py:642
  2.5 0.0 copy-start.7
  2.6 0.0 copy-start.8
  2.6 0.0 copy-start.9
  2.6 0.0 copy-start.10
  2.6 0.0 copy-start.11
  2.6 15.5 %all_to_all.30.in_ref = f32[16,40,128]{2,1,0:T(8,128)S(1)} all-to-all(f32[16,40,128]{2,1,0:T(8,128)S(1)} %get-tuple-element.17), channel_id=1, replica_groups=mesh['rve'=32,'slab'=16] {'slab'}, dimensions={0} | all-to-all | bytes 655360 | tf_op jit(solution)/shard_map/all_to_all | solution.py:557
  18.1 0.0 copy-done.7
  18.1 0.0 copy-done.8
  18.1 0.0 copy-done.9
  18.1 0.0 copy-done.10
  18.1 0.0 copy-done.11
  18.1 0.0 copy-start.1
  18.1 0.0 copy-start.3
  18.1 0.0 copy-start.4
  18.1 0.0 copy-start.5
  18.2 0.0 copy-start.6
  18.2 1.1 %columns.4 = f32[16,40,128]{2,1,0:T(8,128)S(1)} custom-call(f32[16,40,128]{2,1,0:T(8,128)S(1)} %all_to_all.30.in_ref, bf16[256,256]{1,0:T(8,128)(2,1)S(1)} %copy-done.10, bf16[256,256]{1,0:T(8,128)(2,1)S(1)} %copy-done.9, f32[2,64,128]{2,1,0:T(8,128)S(1)} %copy-done.11, bf16[256,256]{1,0:T(8,128)(2,1)S(1)} %copy-done.8, bf16[256,256]{1,0:T(8,128)(2,1)S(1)} %copy-done.7), custom_call_target="tpu_custom_call" | custom-call | flops 400000000 | bytes 2000000 | tf_op jit(solution)/shard_map/columns/pallas_call | solution.py:638
  19.2 0.0 copy-start
  19.3 0.0 copy-start.2
  19.3 10.8 %all_to_all.31.in_ref = f32[16,40,128]{2,1,0:T(8,128)S(1)} all-to-all(f32[16,40,128]{2,1,0:T(8,128)S(1)} %columns.4), channel_id=1, replica_groups=mesh['rve'=32,'slab'=16] {'slab'}, dimensions={0} | all-to-all | bytes 655360 | tf_op jit(solution)/shard_map/all_to_all | solution.py:557
  30.1 0.0 copy-done.1
  30.1 0.0 copy-done.3
  30.1 0.0 copy-done.4
  30.1 0.0 copy-done.5
  30.1 0.0 copy-done.6
  30.1 0.0 copy-done
  30.1 0.0 copy-done.2
  30.1 1.2 %middle.1 = (f32[16,40,128]{2,1,0:T(8,128)S(1)}, f32[768,128]{1,0:T(8,128)S(1)}) custom-call(f32[8,128]{1,0:T(8,128)S(1)} %get-tuple-element.16.macro_ref, s32[128,128]{1,0:T(8,128)S(1)} %bitcast.22, s32[384,128]{1,0:T(8,128)S(1)} %bitcast.19, f32[768,128]{1,0:T(8,128)S(1)} %bitcast.25, f32[16,40,128]{2,1,0:T(8,128)S(1)} %all_to_all.31.in_ref, ...), custom_call_target="tpu_custom_call" | custom-call | flops 800000000 | bytes 4000000 | tf_op jit(solution)/shard_map/middle/pallas_call | solution.py:646
  31.3 10.5 %all_to_all.32.in_ref = f32[16,40,128]{2,1,0:T(8,128)S(1)} all-to-all(f32[16,40,128]{2,1,0:T(8,128)S(1)} %get-tuple-element.19), channel_id=1, replica_groups=mesh['rve'=32,'slab'=16] {'slab'}, dimensions={0} | all-to-all | bytes 655360 | tf_op jit(solution)/shard_map/all_to_all | solution.py:557
  41.8 1.1 %columns.5 = f32[16,40,128]{2,1,0:T(8,128)S(1)} custom-call(f32[16,40,128]{2,1,0:T(8,128)S(1)} %all_to_all.32.in_ref, bf16[256,256]{1,0:T(8,128)(2,1)S(1)} %copy-done.10, bf16[256,256]{1,0:T(8,128)(2,1)S(1)} %copy-done.9, f32[2,64,128]{2,1,0:T(8,128)S(1)} %copy-done.11, bf16[256,256]{1,0:T(8,128)(2,1)S(1)} %copy-done.8, bf16[256,256]{1,0:T(8,128)(2,1)S(1)} %copy-done.7), custom_call_target="tpu_custom_call" | custom-call | flops 400000000 | bytes 2000000 | tf_op jit(solution)/shard_map/columns/pallas_call | solution.py:638
  42.9 10.5 %all_to_all.33.in_ref = f32[16,40,128]{2,1,0:T(8,128)S(1)} all-to-all(f32[16,40,128]{2,1,0:T(8,128)S(1)} %columns.5), channel_id=1, replica_groups=mesh['rve'=32,'slab'=16] {'slab'}, dimensions={0} | all-to-all | bytes 655360 | tf_op jit(solution)/shard_map/all_to_all | solution.py:557
  53.4 1.0 %last.1 = f32[16,1,128]{2,1,0:T(1,128)S(1)} custom-call(s32[128,128]{1,0:T(8,128)S(1)} %bitcast.23, s32[384,128]{1,0:T(8,128)S(1)} %bitcast.20, f32[768,128]{1,0:T(8,128)S(1)} %get-tuple-element.18.elastic_ref, f32[16,40,128]{2,1,0:T(8,128)S(1)} %all_to_all.33.in_ref, bf16[4,256,256]{2,1,0:T(8,128)(2,1)S(1)} %copy-done, bf16[256,256]{1,0:T(8,128)(2,1)S(1)} %copy-done.2), custom_call_target="tpu_custom_call" | custom-call | flops 400000000 | bytes 2000000 | tf_op jit(solution)/shard_map/last/pallas_call | solution.py:650
  54.3 9.0 %all_to_all.34.in_ref = f32[16,1,128]{2,1,0:T(1,128)S(1)} all-to-all(f32[16,1,128]{2,1,0:T(1,128)S(1)} %last.1), channel_id=1, replica_groups=mesh['rve'=32,'slab'=16] {'slab'}, dimensions={0} | all-to-all | bytes 16384 | tf_op jit(solution)/shard_map/all_to_all | solution.py:557
  63.4 28.3 %all_to_all.35.in_ref = f32[32,1,128]{2,1,0:T(1,128)S(1)} all-to-all(f32[32,1,128]{2,1,0:T(1,128)S(1)} %totals.1), channel_id=1, replica_groups={{272,288,304,320,336,352,368,384,400,416,432,448,464,480,496,0,16,32,48..., dimensions={0} | all-to-all | bytes 32768 | tf_op jit(solution)/shard_map/all_to_all | solution.py:653
  91.6 1.1 %assembly.1 = (f32[1,6]{1,0:T(1,128)}, f32[6,1,6]{2,1,0:T(1,128)}, f32[60,60]{1,0:T(8,128)}, f32[3,20]{1,0:T(4,128)}) custom-call(f32[192,128]{1,0:T(8,128)S(1)} %get-tuple-element.14.basis_ref, bf16[2,128,192]{2,1,0:T(8,128)(2,1)S(1)} %get-tuple-element.15.turned_ref, f32[32,1,128]{2,1,0:T(1,128)S(1)} %all_to_all.35.in_ref), custom_call_target="tpu_custom_call" | custom-call | flops 10000000 | bytes 200000 | tf_op jit(solution)/shard_map/assembly/pallas_call | solution.py:656
  (1 shorter events, 0.0 us)
Async XLA Ops:
  2.5 15.5 %copy-start.7 = (bf16[256,256]{1,0:T(8,128)(2,1)S(1)}, bf16[256,256]{1,0:T(8,128)(2,1)}, u32[]{:S(2)}) copy-start(bf16[256,256]{1,0:T(8,128)(2,1)} %constant.26.clone.back_four) | copy-start | bytes 393220
  2.6 15.5 %copy-start.8 = (bf16[256,256]{1,0:T(8,128)(2,1)S(1)}, bf16[256,256]{1,0:T(8,128)(2,1)}, u32[]{:S(2)}) copy-start(bf16[256,256]{1,0:T(8,128)(2,1)} %constant.25.clone.four) | copy-start | bytes 393220
  2.6 15.5 %copy-start.9 = (bf16[256,256]{1,0:T(8,128)(2,1)S(1)}, bf16[256,256]{1,0:T(8,128)(2,1)}, u32[]{:S(2)}) copy-start(bf16[256,256]{1,0:T(8,128)(2,1)} %constant.23.clone.back_columns) | copy-start | bytes 393220
  2.6 15.5 %copy-start.10 = (bf16[256,256]{1,0:T(8,128)(2,1)S(1)}, bf16[256,256]{1,0:T(8,128)(2,1)}, u32[]{:S(2)}) copy-start(bf16[256,256]{1,0:T(8,128)(2,1)} %constant.22.clone.columns) | copy-start | bytes 393220
  2.6 15.5 %copy-start.11 = (f32[2,64,128]{2,1,0:T(8,128)S(1)}, f32[2,64,128]{2,1,0:T(8,128)}, u32[]{:S(2)}) copy-start(f32[2,64,128]{2,1,0:T(8,128)} %constant.24.clone.twist_ref) | copy-start | bytes 196612
  18.1 11.9 %copy-start.1 = (s32[1,3,4,4096]{3,2,1,0:T(4,128)S(1)}, s32[1,3,4,4096]{3,2,1,0:T(4,128)}, u32[]{:S(2)}) copy-start(s32[1,3,4,4096]{3,2,1,0:T(4,128)} %param.15) | copy-start | bytes 589828
  18.1 11.9 %copy-start.3 = (s32[4,4096]{1,0:T(4,128)S(1)}, s32[4,4096]{1,0:T(4,128)}, u32[]{:S(2)}) copy-start(s32[4,4096]{1,0:T(4,128)} %param.14) | copy-start | bytes 196612
  18.1 11.9 %copy-start.4 = (f32[1,6,4,4096]{3,2,1,0:T(4,128)S(1)}, f32[1,6,4,4096]{3,2,1,0:T(4,128)}, u32[]{:S(2)}) copy-start(f32[1,6,4,4096]{3,2,1,0:T(4,128)} %param.16) | copy-start | bytes 1179652
  18.1 11.9 %copy-start.5 = (bf16[4,256,256]{2,1,0:T(8,128)(2,1)S(1)}, bf16[4,256,256]{2,1,0:T(8,128)(2,1)}, u32[]{:S(2)}) copy-start(bf16[4,256,256]{2,1,0:T(8,128)(2,1)} %constant.18.clone.depth_hbm.depth) | copy-start | bytes 1572868
  18.2 11.9 %copy-start.6 = (bf16[256,256]{1,0:T(8,128)(2,1)S(1)}, bf16[256,256]{1,0:T(8,128)(2,1)}, u32[]{:S(2)}) copy-start(bf16[256,256]{1,0:T(8,128)(2,1)} %constant.20.clone.rows_hbm.rows) | copy-start | bytes 393220
  19.2 10.8 %copy-start = (bf16[4,256,256]{2,1,0:T(8,128)(2,1)S(1)}, bf16[4,256,256]{2,1,0:T(8,128)(2,1)}, u32[]{:S(2)}) copy-start(bf16[4,256,256]{2,1,0:T(8,128)(2,1)} %constant.19.clone.back_depth) | copy-start | bytes 1572868
  19.3 10.8 %copy-start.2 = (bf16[256,256]{1,0:T(8,128)(2,1)S(1)}, bf16[256,256]{1,0:T(8,128)(2,1)}, u32[]{:S(2)}) copy-start(bf16[256,256]{1,0:T(8,128)(2,1)} %constant.21.clone.back_rows) | copy-start | bytes 393220

commit v8 on v7

--- a/solution.py
+++ b/solution.py
@@ -29,6 +29,7 @@
 GAUSS_HIGH = 0.5 + 0.5 / math.sqrt(3.0)
 OUTER_AT = 8
 FIELDS = 5
+FAR = 10
 
 
 def halves(table):
@@ -553,8 +554,11 @@
     return points // 2 + 1 if points > 1 else 0
 
 
-def exchange(array):
-    return lax.all_to_all(array, "slab", split_axis=0, concat_axis=0, tiled=True)
+def exchange(array, turn=0):
+    groups = [[(d + turn) % SLABS for d in range(SLABS)]] if turn else None
+    return lax.all_to_all(
+        array, "slab", split_axis=0, concat_axis=0, tiled=True, axis_index_groups=groups
+    )
 
 
 def on_device(phase_ids, yield_flags, plastic_strain, displacements, connectivity):
@@ -648,7 +652,7 @@
     )
     planes = apply_columns(spectrum)
     partial = last(phases, flags, elastic, planes, back_depth, back_line)
-    everyone = totals(exchange(partial))
+    everyone = totals(exchange(partial, FAR))
     turned = [(g + first_of(points)) % points for g in range(points)]
     everyone = lax.all_to_all(
         everyone, "rve", 0, 0, tiled=True, axis_index_groups=[turned]

time: 93.1 us -> 92 us (0.988)
  blocking collectives: 84.5 us -> 83.4 us
    all_to_all x5, blocking collectives: 56.3 us -> 55.2 us  [exchange(): lax.all_to_all(array, 'slab', split_axis=0, concat_axis=0, tiled=True, ax...]
where the time goes in v8:
time: 92 us; the launch traced here: 91.6 us
  blocking collectives  83.4 us (91%)
  Pallas kernels  7.29 us (8%)
    all_to_all x5, blocking collectives, exchange(): lax.all_to_all(array, 'slab', split_axis=0, concat_axis=0, tiled=True, ax...  55.2 us
    all_to_all x1, blocking collectives, on_device(): lax.all_to_all(everyone, 'rve', 0, 0, tiled=True, axis_index_groups=[turn...  28.2 us
    pallas_call x2, Pallas kernels, apply_columns(): columns(exchange(array), column, back_column, twist, four, back_four)  2.13 us
    pallas_call x1, Pallas kernels, on_device(): first(*(pltpu.with_memory_space_constraint(operand, pltpu.HBM) for operan...  1.91 us

profile of v8, /device:TPU:1, one launch (start us, length us, event | category | flops | bytes accessed | tf_op | source)
XLA Modules:
  0.0 91.6 jit_solution(7473251046396065264)
XLA Ops:
  0.6 1.9 %first.1 = (f32[16,40,128]{2,1,0:T(8,128)S(1)}, f32[8,128]{1,0:T(8,128)S(1)}, f32[192,128]{1,0:T(8,128)S(1)}, bf16[2,128,192]{2,1,0:T(8,128)(2,1)S(1)}) custom-call(s32[4,8]{1,0:T(4,128)} %conn_hbm.1, f32[3,20]{1,0:T(4,128)} %bitcast.27, s32[128,128]{1,0:T(8,128)} %bitcast.21, s32[384,128]{1,0:T(8,128)} %bitcast.18, f32[768,128]{1,0:T(8,128)} %bitcast.24, ...), custom_call_target="tpu_custom_call" | custom-call | flops 400000000 | bytes 2000000 | tf_op jit(solution)/shard_map/first/pallas_call | solution.py:646
  2.5 0.0 copy-start.7
  2.6 0.0 copy-start.8
  2.6 0.0 copy-start.9
  2.6 0.0 copy-start.10
  2.6 0.0 copy-start.11
  2.6 15.5 %all_to_all.30.in_ref = f32[16,40,128]{2,1,0:T(8,128)S(1)} all-to-all(f32[16,40,128]{2,1,0:T(8,128)S(1)} %get-tuple-element.17), channel_id=1, replica_groups=mesh['rve'=32,'slab'=16] {'slab'}, dimensions={0} | all-to-all | bytes 655360 | tf_op jit(solution)/shard_map/all_to_all | solution.py:559
  18.1 0.0 copy-done.7
  18.1 0.0 copy-done.8
  18.1 0.0 copy-done.9
  18.1 0.0 copy-done.10
  18.1 0.0 copy-done.11
  18.1 0.0 copy-start.1
  18.1 0.0 copy-start.3
  18.1 0.0 copy-start.4
  18.1 0.0 copy-start.5
  18.2 0.0 copy-start.6
  18.2 1.1 %columns.4 = f32[16,40,128]{2,1,0:T(8,128)S(1)} custom-call(f32[16,40,128]{2,1,0:T(8,128)S(1)} %all_to_all.30.in_ref, bf16[256,256]{1,0:T(8,128)(2,1)S(1)} %copy-done.10, bf16[256,256]{1,0:T(8,128)(2,1)S(1)} %copy-done.9, f32[2,64,128]{2,1,0:T(8,128)S(1)} %copy-done.11, bf16[256,256]{1,0:T(8,128)(2,1)S(1)} %copy-done.8, bf16[256,256]{1,0:T(8,128)(2,1)S(1)} %copy-done.7), custom_call_target="tpu_custom_call" | custom-call | flops 400000000 | bytes 2000000 | tf_op jit(solution)/shard_map/columns/pallas_call | solution.py:642
  19.2 0.0 copy-start
  19.3 0.0 copy-start.2
  19.3 10.8 %all_to_all.31.in_ref = f32[16,40,128]{2,1,0:T(8,128)S(1)} all-to-all(f32[16,40,128]{2,1,0:T(8,128)S(1)} %columns.4), channel_id=1, replica_groups=mesh['rve'=32,'slab'=16] {'slab'}, dimensions={0} | all-to-all | bytes 655360 | tf_op jit(solution)/shard_map/all_to_all | solution.py:559
  30.1 0.0 copy-done.1
  30.1 0.0 copy-done.3
  30.1 0.0 copy-done.4
  30.1 0.0 copy-done.5
  30.1 0.0 copy-done.6
  30.1 0.0 copy-done
  30.1 0.0 copy-done.2
  30.1 1.2 %middle.1 = (f32[16,40,128]{2,1,0:T(8,128)S(1)}, f32[768,128]{1,0:T(8,128)S(1)}) custom-call(f32[8,128]{1,0:T(8,128)S(1)} %get-tuple-element.16.macro_ref, s32[128,128]{1,0:T(8,128)S(1)} %bitcast.22, s32[384,128]{1,0:T(8,128)S(1)} %bitcast.19, f32[768,128]{1,0:T(8,128)S(1)} %bitcast.25, f32[16,40,128]{2,1,0:T(8,128)S(1)} %all_to_all.31.in_ref, ...), custom_call_target="tpu_custom_call" | custom-call | flops 800000000 | bytes 4000000 | tf_op jit(solution)/shard_map/middle/pallas_call | solution.py:650
  31.3 10.5 %all_to_all.32.in_ref = f32[16,40,128]{2,1,0:T(8,128)S(1)} all-to-all(f32[16,40,128]{2,1,0:T(8,128)S(1)} %get-tuple-element.19), channel_id=1, replica_groups=mesh['rve'=32,'slab'=16] {'slab'}, dimensions={0} | all-to-all | bytes 655360 | tf_op jit(solution)/shard_map/all_to_all | solution.py:559
  41.8 1.1 %columns.5 = f32[16,40,128]{2,1,0:T(8,128)S(1)} custom-call(f32[16,40,128]{2,1,0:T(8,128)S(1)} %all_to_all.32.in_ref, bf16[256,256]{1,0:T(8,128)(2,1)S(1)} %copy-done.10, bf16[256,256]{1,0:T(8,128)(2,1)S(1)} %copy-done.9, f32[2,64,128]{2,1,0:T(8,128)S(1)} %copy-done.11, bf16[256,256]{1,0:T(8,128)(2,1)S(1)} %copy-done.8, bf16[256,256]{1,0:T(8,128)(2,1)S(1)} %copy-done.7), custom_call_target="tpu_custom_call" | custom-call | flops 400000000 | bytes 2000000 | tf_op jit(solution)/shard_map/columns/pallas_call | solution.py:642
  42.9 10.5 %all_to_all.33.in_ref = f32[16,40,128]{2,1,0:T(8,128)S(1)} all-to-all(f32[16,40,128]{2,1,0:T(8,128)S(1)} %columns.5), channel_id=1, replica_groups=mesh['rve'=32,'slab'=16] {'slab'}, dimensions={0} | all-to-all | bytes 655360 | tf_op jit(solution)/shard_map/all_to_all | solution.py:559
  53.4 1.0 %last.1 = f32[16,1,128]{2,1,0:T(1,128)S(1)} custom-call(s32[128,128]{1,0:T(8,128)S(1)} %bitcast.23, s32[384,128]{1,0:T(8,128)S(1)} %bitcast.20, f32[768,128]{1,0:T(8,128)S(1)} %get-tuple-element.18.elastic_ref, f32[16,40,128]{2,1,0:T(8,128)S(1)} %all_to_all.33.in_ref, bf16[4,256,256]{2,1,0:T(8,128)(2,1)S(1)} %copy-done, bf16[256,256]{1,0:T(8,128)(2,1)S(1)} %copy-done.2), custom_call_target="tpu_custom_call" | custom-call | flops 400000000 | bytes 2000000 | tf_op jit(solution)/shard_map/last/pallas_call | solution.py:654
  54.3 8.0 %all_to_all.34.in_ref = f32[16,1,128]{2,1,0:T(1,128)S(1)} all-to-all(f32[16,1,128]{2,1,0:T(1,128)S(1)} %last.1), channel_id=1, replica_groups={{10,11,12,13,14,15,0,1,2,3,4,5,6,7,8,9},{26,27,28,29,30,31,16,17,18,19,..., dimensions={0} | all-to-all | bytes 16384 | tf_op jit(solution)/shard_map/all_to_all | solution.py:559
  62.3 28.2 %all_to_all.35.in_ref = f32[32,1,128]{2,1,0:T(1,128)S(1)} all-to-all(f32[32,1,128]{2,1,0:T(1,128)S(1)} %totals.1), channel_id=1, replica_groups={{272,288,304,320,336,352,368,384,400,416,432,448,464,480,496,0,16,32,48..., dimensions={0} | all-to-all | bytes 32768 | tf_op jit(solution)/shard_map/all_to_all | solution.py:657
  90.6 1.1 %assembly.1 = (f32[1,6]{1,0:T(1,128)}, f32[6,1,6]{2,1,0:T(1,128)}, f32[60,60]{1,0:T(8,128)}, f32[3,20]{1,0:T(4,128)}) custom-call(f32[192,128]{1,0:T(8,128)S(1)} %get-tuple-element.14.basis_ref, bf16[2,128,192]{2,1,0:T(8,128)(2,1)S(1)} %get-tuple-element.15.turned_ref, f32[32,1,128]{2,1,0:T(1,128)S(1)} %all_to_all.35.in_ref), custom_call_target="tpu_custom_call" | custom-call | flops 10000000 | bytes 200000 | tf_op jit(solution)/shard_map/assembly/pallas_call | solution.py:660
  (1 shorter events, 0.0 us)
Async XLA Ops:
  2.5 15.5 %copy-start.7 = (bf16[256,256]{1,0:T(8,128)(2,1)S(1)}, bf16[256,256]{1,0:T(8,128)(2,1)}, u32[]{:S(2)}) copy-start(bf16[256,256]{1,0:T(8,128)(2,1)} %constant.26.clone.back_four) | copy-start | bytes 393220
  2.6 15.5 %copy-start.8 = (bf16[256,256]{1,0:T(8,128)(2,1)S(1)}, bf16[256,256]{1,0:T(8,128)(2,1)}, u32[]{:S(2)}) copy-start(bf16[256,256]{1,0:T(8,128)(2,1)} %constant.25.clone.four) | copy-start | bytes 393220
  2.6 15.5 %copy-start.9 = (bf16[256,256]{1,0:T(8,128)(2,1)S(1)}, bf16[256,256]{1,0:T(8,128)(2,1)}, u32[]{:S(2)}) copy-start(bf16[256,256]{1,0:T(8,128)(2,1)} %constant.23.clone.back_columns) | copy-start | bytes 393220
  2.6 15.5 %copy-start.10 = (bf16[256,256]{1,0:T(8,128)(2,1)S(1)}, bf16[256,256]{1,0:T(8,128)(2,1)}, u32[]{:S(2)}) copy-start(bf16[256,256]{1,0:T(8,128)(2,1)} %constant.22.clone.columns) | copy-start | bytes 393220
  2.6 15.5 %copy-start.11 = (f32[2,64,128]{2,1,0:T(8,128)S(1)}, f32[2,64,128]{2,1,0:T(8,128)}, u32[]{:S(2)}) copy-start(f32[2,64,128]{2,1,0:T(8,128)} %constant.24.clone.twist_ref) | copy-start | bytes 196612
  18.1 11.9 %copy-start.1 = (s32[1,3,4,4096]{3,2,1,0:T(4,128)S(1)}, s32[1,3,4,4096]{3,2,1,0:T(4,128)}, u32[]{:S(2)}) copy-start(s32[1,3,4,4096]{3,2,1,0:T(4,128)} %param.15) | copy-start | bytes 589828
  18.1 11.9 %copy-start.3 = (s32[4,4096]{1,0:T(4,128)S(1)}, s32[4,4096]{1,0:T(4,128)}, u32[]{:S(2)}) copy-start(s32[4,4096]{1,0:T(4,128)} %param.14) | copy-start | bytes 196612
  18.1 11.9 %copy-start.4 = (f32[1,6,4,4096]{3,2,1,0:T(4,128)S(1)}, f32[1,6,4,4096]{3,2,1,0:T(4,128)}, u32[]{:S(2)}) copy-start(f32[1,6,4,4096]{3,2,1,0:T(4,128)} %param.16) | copy-start | bytes 1179652
  18.1 11.9 %copy-start.5 = (bf16[4,256,256]{2,1,0:T(8,128)(2,1)S(1)}, bf16[4,256,256]{2,1,0:T(8,128)(2,1)}, u32[]{:S(2)}) copy-start(bf16[4,256,256]{2,1,0:T(8,128)(2,1)} %constant.18.clone.depth_hbm.depth) | copy-start | bytes 1572868
  18.2 11.9 %copy-start.6 = (bf16[256,256]{1,0:T(8,128)(2,1)S(1)}, bf16[256,256]{1,0:T(8,128)(2,1)}, u32[]{:S(2)}) copy-start(bf16[256,256]{1,0:T(8,128)(2,1)} %constant.20.clone.rows_hbm.rows) | copy-start | bytes 393220
  19.2 10.8 %copy-start = (bf16[4,256,256]{2,1,0:T(8,128)(2,1)S(1)}, bf16[4,256,256]{2,1,0:T(8,128)(2,1)}, u32[]{:S(2)}) copy-start(bf16[4,256,256]{2,1,0:T(8,128)(2,1)} %constant.19.clone.back_depth) | copy-start | bytes 1572868
  19.3 10.8 %copy-start.2 = (bf16[256,256]{1,0:T(8,128)(2,1)S(1)}, bf16[256,256]{1,0:T(8,128)(2,1)}, u32[]{:S(2)}) copy-start(bf16[256,256]{1,0:T(8,128)(2,1)} %constant.21.clone.back_rows) | copy-start | bytes 393220

commit v9 on v8

--- a/solution.py
+++ b/solution.py
@@ -226,7 +226,7 @@
     return wave_y, jnp.concatenate([depth] * 16, axis=0)
 
 
-def forward_planes(stresses, depth, rows, out_ref):
+def forward_planes(stresses, depth, rows, out_ref, turn=0):
     tiles = gather_chunks(from_right(stresses, depth))
     tiles = [roll_chunks(tile, -s) for s, tile in enumerate(tiles)]
     pairs = [
@@ -238,7 +238,10 @@
     wave_y, wave_z = plane_waves()
     fields = (xx, xy, xz, wave_y * yy + wave_z * yz, wave_y * yz + wave_z * zz)
     for c, field in enumerate(fields):
-        out_ref[:, c * 8 : (c + 1) * 8, :] = field.reshape(16, 8, 128)
+        block = field.reshape(16, 8, 128)
+        out_ref[: 16 - turn, c * 8 : (c + 1) * 8, :] = block[turn:]
+        if turn:
+            out_ref[16 - turn :, c * 8 : (c + 1) * 8, :] = block[:turn]
 
 
 def backward_planes(in_ref, depth, rows):
@@ -326,7 +329,7 @@
     high, low = split(jnp.transpose(basis))
     turned_ref[0] = high
     turned_ref[1] = low
-    forward_planes(stresses, depth, rows, out_ref)
+    forward_planes(stresses, depth, rows, out_ref, FAR)
 
 
 def middle_kernel(
@@ -406,8 +409,13 @@
     out_ref[...] = line.reshape(SLABS, 1, 128)
 
 
-def column_kernel(in_ref, columns, back_columns, twist_ref, four, back_four, out_ref):
-    pairs = [split(in_ref[:, c * 8 : (c + 1) * 8, :].reshape(128, 128)) for c in range(FIELDS)]
+def column_kernel(turn, in_ref, columns, back_columns, twist_ref, four, back_four, out_ref):
+    pairs = []
+    for c in range(FIELDS):
+        block = in_ref[:, c * 8 : (c + 1) * 8, :]
+        if turn:
+            block = jnp.concatenate([block[16 - turn :], block[: 16 - turn]], axis=0)
+        pairs.append(split(block.reshape(128, 128)))
     mixed = from_left_values(columns, pairs)
     cosine, sine = twist_ref[0], twist_ref[1]
 
@@ -605,11 +613,13 @@
         ],
         compiler_params=params(), cost_estimate=cost(400_000_000, 2_000_000), name="first",
     )
-    columns = pl.pallas_call(
-        column_kernel, out_shape=block,
-        in_specs=[VMEM] * 6, out_specs=VMEM,
-        compiler_params=params(), cost_estimate=cost(400_000_000, 2_000_000), name="columns",
-    )
+    def columns(turn):
+        return pl.pallas_call(
+            functools.partial(column_kernel, turn), out_shape=block,
+            in_specs=[VMEM] * 6, out_specs=VMEM, compiler_params=params(),
+            cost_estimate=cost(400_000_000, 2_000_000), name="columns",
+        )
+
     middle = pl.pallas_call(
         middle_kernel, out_shape=(block, jax.ShapeDtypeStruct((768, 128), F32)),
         in_specs=[VMEM] * 9, out_specs=(VMEM, VMEM),
@@ -637,20 +647,20 @@
         cost_estimate=cost(10_000_000, 200_000), name="assembly",
     )
 
-    def apply_columns(array):
+    def apply_columns(array, turn):
         return exchange(
-            columns(exchange(array), column, back_column, twist, four, back_four)
+            columns(turn)(exchange(array, turn), column, back_column, twist, four, back_four)
         )
 
     operands = (connectivity, displacements.T, phases, flags, plastic, depth, line)
     spectrum, macro, basis, turned_basis = first(
         *(pltpu.with_memory_space_constraint(operand, pltpu.HBM) for operand in operands)
     )
-    planes = apply_columns(spectrum)
+    planes = apply_columns(spectrum, FAR)
     spectrum, elastic = middle(
         macro, phases, flags, plastic, planes, back_depth, back_line, depth, line
     )
-    planes = apply_columns(spectrum)
+    planes = apply_columns(spectrum, 0)
     partial = last(phases, flags, elastic, planes, back_depth, back_line)
     everyone = totals(exchange(partial, FAR))
     turned = [(g + first_of(points)) % points for g in range(points)]

time: 92 us -> 91.2 us (level)
  no operation moved by 1% of the time
where the time goes in v9:
time: 91.2 us; the launch traced here: 90.8 us
  blocking collectives  82.6 us (91%)
  Pallas kernels  7.29 us (8%)
    all_to_all x5, blocking collectives, exchange(): lax.all_to_all(array, 'slab', split_axis=0, concat_axis=0, tiled=True, ax...  54.4 us
    all_to_all x1, blocking collectives, on_device(): lax.all_to_all(everyone, 'rve', 0, 0, tiled=True, axis_index_groups=[turn...  28.2 us
    pallas_call x2, Pallas kernels, apply_columns(): columns(turn)  2.14 us
    pallas_call x1, Pallas kernels, on_device(): first(*(pltpu.with_memory_space_constraint(operand, pltpu.HBM) for operan...  1.91 us

profile of v9, /device:TPU:1, one launch (start us, length us, event | category | flops | bytes accessed | tf_op | source)
XLA Modules:
  0.0 90.8 jit_solution(4740509586438761551)
XLA Ops:
  0.6 1.9 %first.1 = (f32[16,40,128]{2,1,0:T(8,128)S(1)}, f32[8,128]{1,0:T(8,128)S(1)}, f32[192,128]{1,0:T(8,128)S(1)}, bf16[2,128,192]{2,1,0:T(8,128)(2,1)S(1)}) custom-call(s32[4,8]{1,0:T(4,128)} %conn_hbm.1, f32[3,20]{1,0:T(4,128)} %bitcast.27, s32[128,128]{1,0:T(8,128)} %bitcast.21, s32[384,128]{1,0:T(8,128)} %bitcast.18, f32[768,128]{1,0:T(8,128)} %bitcast.24, ...), custom_call_target="tpu_custom_call" | custom-call | flops 400000000 | bytes 2000000 | tf_op jit(solution)/shard_map/first/pallas_call | solution.py:656
  2.5 0.0 copy-start.7
  2.6 0.0 copy-start.8
  2.6 0.0 copy-start.9
  2.6 0.0 copy-start.10
  2.6 0.0 copy-start.11
  2.6 12.2 %all_to_all.30.in_ref = f32[16,40,128]{2,1,0:T(8,128)S(1)} all-to-all(f32[16,40,128]{2,1,0:T(8,128)S(1)} %get-tuple-element.17), channel_id=1, replica_groups={{10,11,12,13,14,15,0,1,2,3,4,5,6,7,8,9},{26,27,28,29,30,31,16,17,18,19,..., dimensions={0} | all-to-all | bytes 655360 | tf_op jit(solution)/shard_map/all_to_all | solution.py:567
  14.8 0.0 copy-done.7
  14.9 0.0 copy-done.8
  14.9 0.0 copy-done.9
  14.9 0.0 copy-done.10
  14.9 0.0 copy-done.11
  14.9 0.0 copy-start.1
  14.9 0.0 copy-start.3
  14.9 0.0 copy-start.4
  14.9 0.0 copy-start.5
  14.9 0.0 copy-start.6
  14.9 1.1 %columns.4 = f32[16,40,128]{2,1,0:T(8,128)S(1)} custom-call(f32[16,40,128]{2,1,0:T(8,128)S(1)} %all_to_all.30.in_ref, bf16[256,256]{1,0:T(8,128)(2,1)S(1)} %copy-done.10, bf16[256,256]{1,0:T(8,128)(2,1)S(1)} %copy-done.9, f32[2,64,128]{2,1,0:T(8,128)S(1)} %copy-done.11, bf16[256,256]{1,0:T(8,128)(2,1)S(1)} %copy-done.8, bf16[256,256]{1,0:T(8,128)(2,1)S(1)} %copy-done.7), custom_call_target="tpu_custom_call" | custom-call | flops 400000000 | bytes 2000000 | tf_op jit(solution)/shard_map/columns/pallas_call | solution.py:652
  16.0 0.0 copy-start
  16.0 0.0 copy-start.2
  16.0 13.0 %all_to_all.31.in_ref = f32[16,40,128]{2,1,0:T(8,128)S(1)} all-to-all(f32[16,40,128]{2,1,0:T(8,128)S(1)} %columns.4), channel_id=1, replica_groups=mesh['rve'=32,'slab'=16] {'slab'}, dimensions={0} | all-to-all | bytes 655360 | tf_op jit(solution)/shard_map/all_to_all | solution.py:567
  29.0 0.0 copy-done.1
  29.0 0.0 copy-done.3
  29.0 0.0 copy-done.4
  29.0 0.0 copy-done.5
  29.0 0.0 copy-done.6
  29.1 0.0 copy-done
  29.1 0.0 copy-done.2
  29.1 1.2 %middle.1 = (f32[16,40,128]{2,1,0:T(8,128)S(1)}, f32[768,128]{1,0:T(8,128)S(1)}) custom-call(f32[8,128]{1,0:T(8,128)S(1)} %get-tuple-element.16.macro_ref, s32[128,128]{1,0:T(8,128)S(1)} %bitcast.22, s32[384,128]{1,0:T(8,128)S(1)} %bitcast.19, f32[768,128]{1,0:T(8,128)S(1)} %bitcast.25, f32[16,40,128]{2,1,0:T(8,128)S(1)} %all_to_all.31.in_ref, ...), custom_call_target="tpu_custom_call" | custom-call | flops 800000000 | bytes 4000000 | tf_op jit(solution)/shard_map/middle/pallas_call | solution.py:660
  30.3 10.5 %all_to_all.32.in_ref = f32[16,40,128]{2,1,0:T(8,128)S(1)} all-to-all(f32[16,40,128]{2,1,0:T(8,128)S(1)} %get-tuple-element.19), channel_id=1, replica_groups=mesh['rve'=32,'slab'=16] {'slab'}, dimensions={0} | all-to-all | bytes 655360 | tf_op jit(solution)/shard_map/all_to_all | solution.py:567
  40.8 1.1 %columns.5 = f32[16,40,128]{2,1,0:T(8,128)S(1)} custom-call(f32[16,40,128]{2,1,0:T(8,128)S(1)} %all_to_all.32.in_ref, bf16[256,256]{1,0:T(8,128)(2,1)S(1)} %copy-done.10, bf16[256,256]{1,0:T(8,128)(2,1)S(1)} %copy-done.9, f32[2,64,128]{2,1,0:T(8,128)S(1)} %copy-done.11, bf16[256,256]{1,0:T(8,128)(2,1)S(1)} %copy-done.8, bf16[256,256]{1,0:T(8,128)(2,1)S(1)} %copy-done.7), custom_call_target="tpu_custom_call" | custom-call | flops 400000000 | bytes 2000000 | tf_op jit(solution)/shard_map/columns/pallas_call | solution.py:652
  41.8 10.5 %all_to_all.33.in_ref = f32[16,40,128]{2,1,0:T(8,128)S(1)} all-to-all(f32[16,40,128]{2,1,0:T(8,128)S(1)} %columns.5), channel_id=1, replica_groups=mesh['rve'=32,'slab'=16] {'slab'}, dimensions={0} | all-to-all | bytes 655360 | tf_op jit(solution)/shard_map/all_to_all | solution.py:567
  52.3 1.0 %last.1 = f32[16,1,128]{2,1,0:T(1,128)S(1)} custom-call(s32[128,128]{1,0:T(8,128)S(1)} %bitcast.23, s32[384,128]{1,0:T(8,128)S(1)} %bitcast.20, f32[768,128]{1,0:T(8,128)S(1)} %get-tuple-element.18.elastic_ref, f32[16,40,128]{2,1,0:T(8,128)S(1)} %all_to_all.33.in_ref, bf16[4,256,256]{2,1,0:T(8,128)(2,1)S(1)} %copy-done, bf16[256,256]{1,0:T(8,128)(2,1)S(1)} %copy-done.2), custom_call_target="tpu_custom_call" | custom-call | flops 400000000 | bytes 2000000 | tf_op jit(solution)/shard_map/last/pallas_call | solution.py:664
  53.3 8.2 %all_to_all.34.in_ref = f32[16,1,128]{2,1,0:T(1,128)S(1)} all-to-all(f32[16,1,128]{2,1,0:T(1,128)S(1)} %last.1), channel_id=1, replica_groups={{10,11,12,13,14,15,0,1,2,3,4,5,6,7,8,9},{26,27,28,29,30,31,16,17,18,19,..., dimensions={0} | all-to-all | bytes 16384 | tf_op jit(solution)/shard_map/all_to_all | solution.py:567
  61.6 28.2 %all_to_all.35.in_ref = f32[32,1,128]{2,1,0:T(1,128)S(1)} all-to-all(f32[32,1,128]{2,1,0:T(1,128)S(1)} %totals.1), channel_id=1, replica_groups={{272,288,304,320,336,352,368,384,400,416,432,448,464,480,496,0,16,32,48..., dimensions={0} | all-to-all | bytes 32768 | tf_op jit(solution)/shard_map/all_to_all | solution.py:667
  89.8 1.1 %assembly.1 = (f32[1,6]{1,0:T(1,128)}, f32[6,1,6]{2,1,0:T(1,128)}, f32[60,60]{1,0:T(8,128)}, f32[3,20]{1,0:T(4,128)}) custom-call(f32[192,128]{1,0:T(8,128)S(1)} %get-tuple-element.14.basis_ref, bf16[2,128,192]{2,1,0:T(8,128)(2,1)S(1)} %get-tuple-element.15.turned_ref, f32[32,1,128]{2,1,0:T(1,128)S(1)} %all_to_all.35.in_ref), custom_call_target="tpu_custom_call" | custom-call | flops 10000000 | bytes 200000 | tf_op jit(solution)/shard_map/assembly/pallas_call | solution.py:670
  (1 shorter events, 0.0 us)
Async XLA Ops:
  2.5 12.3 %copy-start.7 = (bf16[256,256]{1,0:T(8,128)(2,1)S(1)}, bf16[256,256]{1,0:T(8,128)(2,1)}, u32[]{:S(2)}) copy-start(bf16[256,256]{1,0:T(8,128)(2,1)} %constant.26.clone.back_four) | copy-start | bytes 393220
  2.6 12.3 %copy-start.8 = (bf16[256,256]{1,0:T(8,128)(2,1)S(1)}, bf16[256,256]{1,0:T(8,128)(2,1)}, u32[]{:S(2)}) copy-start(bf16[256,256]{1,0:T(8,128)(2,1)} %constant.25.clone.four) | copy-start | bytes 393220
  2.6 12.3 %copy-start.9 = (bf16[256,256]{1,0:T(8,128)(2,1)S(1)}, bf16[256,256]{1,0:T(8,128)(2,1)}, u32[]{:S(2)}) copy-start(bf16[256,256]{1,0:T(8,128)(2,1)} %constant.23.clone.back_columns) | copy-start | bytes 393220
  2.6 12.3 %copy-start.10 = (bf16[256,256]{1,0:T(8,128)(2,1)S(1)}, bf16[256,256]{1,0:T(8,128)(2,1)}, u32[]{:S(2)}) copy-start(bf16[256,256]{1,0:T(8,128)(2,1)} %constant.22.clone.columns) | copy-start | bytes 393220
  2.6 12.3 %copy-start.11 = (f32[2,64,128]{2,1,0:T(8,128)S(1)}, f32[2,64,128]{2,1,0:T(8,128)}, u32[]{:S(2)}) copy-start(f32[2,64,128]{2,1,0:T(8,128)} %constant.24.clone.twist_ref) | copy-start | bytes 196612
  14.9 14.1 %copy-start.1 = (s32[1,3,4,4096]{3,2,1,0:T(4,128)S(1)}, s32[1,3,4,4096]{3,2,1,0:T(4,128)}, u32[]{:S(2)}) copy-start(s32[1,3,4,4096]{3,2,1,0:T(4,128)} %param.15) | copy-start | bytes 589828
  14.9 14.1 %copy-start.3 = (s32[4,4096]{1,0:T(4,128)S(1)}, s32[4,4096]{1,0:T(4,128)}, u32[]{:S(2)}) copy-start(s32[4,4096]{1,0:T(4,128)} %param.14) | copy-start | bytes 196612
  14.9 14.1 %copy-start.4 = (f32[1,6,4,4096]{3,2,1,0:T(4,128)S(1)}, f32[1,6,4,4096]{3,2,1,0:T(4,128)}, u32[]{:S(2)}) copy-start(f32[1,6,4,4096]{3,2,1,0:T(4,128)} %param.16) | copy-start | bytes 1179652
  14.9 14.1 %copy-start.5 = (bf16[4,256,256]{2,1,0:T(8,128)(2,1)S(1)}, bf16[4,256,256]{2,1,0:T(8,128)(2,1)}, u32[]{:S(2)}) copy-start(bf16[4,256,256]{2,1,0:T(8,128)(2,1)} %constant.18.clone.depth_hbm.depth) | copy-start | bytes 1572868
  14.9 14.1 %copy-start.6 = (bf16[256,256]{1,0:T(8,128)(2,1)S(1)}, bf16[256,256]{1,0:T(8,128)(2,1)}, u32[]{:S(2)}) copy-start(bf16[256,256]{1,0:T(8,128)(2,1)} %constant.20.clone.rows_hbm.rows) | copy-start | bytes 393220
  16.0 13.0 %copy-start = (bf16[4,256,256]{2,1,0:T(8,128)(2,1)S(1)}, bf16[4,256,256]{2,1,0:T(8,128)(2,1)}, u32[]{:S(2)}) copy-start(bf16[4,256,256]{2,1,0:T(8,128)(2,1)} %constant.19.clone.back_depth) | copy-start | bytes 1572868
  16.0 13.0 %copy-start.2 = (bf16[256,256]{1,0:T(8,128)(2,1)S(1)}, bf16[256,256]{1,0:T(8,128)(2,1)}, u32[]{:S(2)}) copy-start(bf16[256,256]{1,0:T(8,128)(2,1)} %constant.21.clone.back_rows) | copy-start | bytes 393220

commit v10 on v9

--- a/solution.py
+++ b/solution.py
@@ -351,7 +351,7 @@
         flags = every_fourth(flag_ref, 128, plane)
         stress = material(elastic, phases, flags)[0]
         stresses.append(jnp.concatenate(stress, axis=0))
-    forward_planes(stresses, depth, rows, out_ref)
+    forward_planes(stresses, depth, rows, out_ref, FAR)
 
 
 def last_kernel(
@@ -660,7 +660,7 @@
     spectrum, elastic = middle(
         macro, phases, flags, plastic, planes, back_depth, back_line, depth, line
     )
-    planes = apply_columns(spectrum, 0)
+    planes = apply_columns(spectrum, FAR)
     partial = last(phases, flags, elastic, planes, back_depth, back_line)
     everyone = totals(exchange(partial, FAR))
     turned = [(g + first_of(points)) % points for g in range(points)]

time: 91.2 us -> 92.7 us (1.016)
  blocking collectives: 82.6 us -> 84.2 us
    all_to_all x5, blocking collectives: 54.4 us -> 56 us  [exchange(): lax.all_to_all(array, 'slab', split_axis=0, concat_axis=0, tiled=True, ax...]
where the time goes in v10:
time: 92.7 us; the launch traced here: 92.4 us
  blocking collectives  84.2 us (91%)
  Pallas kernels  7.29 us (8%)
    all_to_all x5, blocking collectives, exchange(): lax.all_to_all(array, 'slab', split_axis=0, concat_axis=0, tiled=True, ax...  56 us
    all_to_all x1, blocking collectives, on_device(): lax.all_to_all(everyone, 'rve', 0, 0, tiled=True, axis_index_groups=[turn...  28.2 us
    pallas_call x2, Pallas kernels, apply_columns(): columns(turn)  2.13 us
    pallas_call x1, Pallas kernels, on_device(): first(*(pltpu.with_memory_space_constraint(operand, pltpu.HBM) for operan...  1.91 us

profile of v10, /device:TPU:1, one launch (start us, length us, event | category | flops | bytes accessed | tf_op | source)
XLA Modules:
  0.0 92.4 jit_solution(3578905267541423201)
XLA Ops:
  0.6 1.9 %first.1 = (f32[16,40,128]{2,1,0:T(8,128)S(1)}, f32[8,128]{1,0:T(8,128)S(1)}, f32[192,128]{1,0:T(8,128)S(1)}, bf16[2,128,192]{2,1,0:T(8,128)(2,1)S(1)}) custom-call(s32[4,8]{1,0:T(4,128)} %conn_hbm.1, f32[3,20]{1,0:T(4,128)} %bitcast.27, s32[128,128]{1,0:T(8,128)} %bitcast.21, s32[384,128]{1,0:T(8,128)} %bitcast.18, f32[768,128]{1,0:T(8,128)} %bitcast.24, ...), custom_call_target="tpu_custom_call" | custom-call | flops 400000000 | bytes 2000000 | tf_op jit(solution)/shard_map/first/pallas_call | solution.py:656
  2.5 0.0 copy-start.7
  2.6 0.0 copy-start.8
  2.6 0.0 copy-start.9
  2.6 0.0 copy-start.10
  2.6 0.0 copy-start.11
  2.6 12.2 %all_to_all.30.in_ref = f32[16,40,128]{2,1,0:T(8,128)S(1)} all-to-all(f32[16,40,128]{2,1,0:T(8,128)S(1)} %get-tuple-element.17), channel_id=1, replica_groups={{10,11,12,13,14,15,0,1,2,3,4,5,6,7,8,9},{26,27,28,29,30,31,16,17,18,19,..., dimensions={0} | all-to-all | bytes 655360 | tf_op jit(solution)/shard_map/all_to_all | solution.py:567
  14.8 0.0 copy-done.7
  14.9 0.0 copy-done.8
  14.9 0.0 copy-done.9
  14.9 0.0 copy-done.10
  14.9 0.0 copy-done.11
  14.9 0.0 copy-start.1
  14.9 0.0 copy-start.3
  14.9 0.0 copy-start.4
  14.9 0.0 copy-start.5
  14.9 0.0 copy-start.6
  14.9 1.1 %columns.4 = f32[16,40,128]{2,1,0:T(8,128)S(1)} custom-call(f32[16,40,128]{2,1,0:T(8,128)S(1)} %all_to_all.30.in_ref, bf16[256,256]{1,0:T(8,128)(2,1)S(1)} %copy-done.10, bf16[256,256]{1,0:T(8,128)(2,1)S(1)} %copy-done.9, f32[2,64,128]{2,1,0:T(8,128)S(1)} %copy-done.11, bf16[256,256]{1,0:T(8,128)(2,1)S(1)} %copy-done.8, bf16[256,256]{1,0:T(8,128)(2,1)S(1)} %copy-done.7), custom_call_target="tpu_custom_call" | custom-call | flops 400000000 | bytes 2000000 | tf_op jit(solution)/shard_map/columns/pallas_call | solution.py:652
  16.0 0.0 copy-start
  16.0 0.0 copy-start.2
  16.0 13.0 %all_to_all.31.in_ref = f32[16,40,128]{2,1,0:T(8,128)S(1)} all-to-all(f32[16,40,128]{2,1,0:T(8,128)S(1)} %columns.4), channel_id=1, replica_groups=mesh['rve'=32,'slab'=16] {'slab'}, dimensions={0} | all-to-all | bytes 655360 | tf_op jit(solution)/shard_map/all_to_all | solution.py:567
  29.0 0.0 copy-done.1
  29.0 0.0 copy-done.3
  29.0 0.0 copy-done.4
  29.0 0.0 copy-done.5
  29.0 0.0 copy-done.6
  29.1 0.0 copy-done
  29.1 0.0 copy-done.2
  29.1 1.2 %middle.1 = (f32[16,40,128]{2,1,0:T(8,128)S(1)}, f32[768,128]{1,0:T(8,128)S(1)}) custom-call(f32[8,128]{1,0:T(8,128)S(1)} %get-tuple-element.16.macro_ref, s32[128,128]{1,0:T(8,128)S(1)} %bitcast.22, s32[384,128]{1,0:T(8,128)S(1)} %bitcast.19, f32[768,128]{1,0:T(8,128)S(1)} %bitcast.25, f32[16,40,128]{2,1,0:T(8,128)S(1)} %all_to_all.31.in_ref, ...), custom_call_target="tpu_custom_call" | custom-call | flops 800000000 | bytes 4000000 | tf_op jit(solution)/shard_map/middle/pallas_call | solution.py:660
  30.3 9.7 %all_to_all.32.in_ref = f32[16,40,128]{2,1,0:T(8,128)S(1)} all-to-all(f32[16,40,128]{2,1,0:T(8,128)S(1)} %get-tuple-element.19), channel_id=1, replica_groups={{10,11,12,13,14,15,0,1,2,3,4,5,6,7,8,9},{26,27,28,29,30,31,16,17,18,19,..., dimensions={0} | all-to-all | bytes 655360 | tf_op jit(solution)/shard_map/all_to_all | solution.py:567
  39.9 1.1 %columns.5 = f32[16,40,128]{2,1,0:T(8,128)S(1)} custom-call(f32[16,40,128]{2,1,0:T(8,128)S(1)} %all_to_all.32.in_ref, bf16[256,256]{1,0:T(8,128)(2,1)S(1)} %copy-done.10, bf16[256,256]{1,0:T(8,128)(2,1)S(1)} %copy-done.9, f32[2,64,128]{2,1,0:T(8,128)S(1)} %copy-done.11, bf16[256,256]{1,0:T(8,128)(2,1)S(1)} %copy-done.8, bf16[256,256]{1,0:T(8,128)(2,1)S(1)} %copy-done.7), custom_call_target="tpu_custom_call" | custom-call | flops 400000000 | bytes 2000000 | tf_op jit(solution)/shard_map/columns/pallas_call | solution.py:652
  41.0 12.8 %all_to_all.33.in_ref = f32[16,40,128]{2,1,0:T(8,128)S(1)} all-to-all(f32[16,40,128]{2,1,0:T(8,128)S(1)} %columns.5), channel_id=1, replica_groups=mesh['rve'=32,'slab'=16] {'slab'}, dimensions={0} | all-to-all | bytes 655360 | tf_op jit(solution)/shard_map/all_to_all | solution.py:567
  53.8 1.0 %last.1 = f32[16,1,128]{2,1,0:T(1,128)S(1)} custom-call(s32[128,128]{1,0:T(8,128)S(1)} %bitcast.23, s32[384,128]{1,0:T(8,128)S(1)} %bitcast.20, f32[768,128]{1,0:T(8,128)S(1)} %get-tuple-element.18.elastic_ref, f32[16,40,128]{2,1,0:T(8,128)S(1)} %all_to_all.33.in_ref, bf16[4,256,256]{2,1,0:T(8,128)(2,1)S(1)} %copy-done, bf16[256,256]{1,0:T(8,128)(2,1)S(1)} %copy-done.2), custom_call_target="tpu_custom_call" | custom-call | flops 400000000 | bytes 2000000 | tf_op jit(solution)/shard_map/last/pallas_call | solution.py:664
  54.8 8.2 %all_to_all.34.in_ref = f32[16,1,128]{2,1,0:T(1,128)S(1)} all-to-all(f32[16,1,128]{2,1,0:T(1,128)S(1)} %last.1), channel_id=1, replica_groups={{10,11,12,13,14,15,0,1,2,3,4,5,6,7,8,9},{26,27,28,29,30,31,16,17,18,19,..., dimensions={0} | all-to-all | bytes 16384 | tf_op jit(solution)/shard_map/all_to_all | solution.py:567
  63.1 28.2 %all_to_all.35.in_ref = f32[32,1,128]{2,1,0:T(1,128)S(1)} all-to-all(f32[32,1,128]{2,1,0:T(1,128)S(1)} %totals.1), channel_id=1, replica_groups={{272,288,304,320,336,352,368,384,400,416,432,448,464,480,496,0,16,32,48..., dimensions={0} | all-to-all | bytes 32768 | tf_op jit(solution)/shard_map/all_to_all | solution.py:667
  91.3 1.1 %assembly.1 = (f32[1,6]{1,0:T(1,128)}, f32[6,1,6]{2,1,0:T(1,128)}, f32[60,60]{1,0:T(8,128)}, f32[3,20]{1,0:T(4,128)}) custom-call(f32[192,128]{1,0:T(8,128)S(1)} %get-tuple-element.14.basis_ref, bf16[2,128,192]{2,1,0:T(8,128)(2,1)S(1)} %get-tuple-element.15.turned_ref, f32[32,1,128]{2,1,0:T(1,128)S(1)} %all_to_all.35.in_ref), custom_call_target="tpu_custom_call" | custom-call | flops 10000000 | bytes 200000 | tf_op jit(solution)/shard_map/assembly/pallas_call | solution.py:670
  (1 shorter events, 0.0 us)
Async XLA Ops:
  2.5 12.3 %copy-start.7 = (bf16[256,256]{1,0:T(8,128)(2,1)S(1)}, bf16[256,256]{1,0:T(8,128)(2,1)}, u32[]{:S(2)}) copy-start(bf16[256,256]{1,0:T(8,128)(2,1)} %constant.26.clone.back_four) | copy-start | bytes 393220
  2.6 12.3 %copy-start.8 = (bf16[256,256]{1,0:T(8,128)(2,1)S(1)}, bf16[256,256]{1,0:T(8,128)(2,1)}, u32[]{:S(2)}) copy-start(bf16[256,256]{1,0:T(8,128)(2,1)} %constant.25.clone.four) | copy-start | bytes 393220
  2.6 12.3 %copy-start.9 = (bf16[256,256]{1,0:T(8,128)(2,1)S(1)}, bf16[256,256]{1,0:T(8,128)(2,1)}, u32[]{:S(2)}) copy-start(bf16[256,256]{1,0:T(8,128)(2,1)} %constant.23.clone.back_columns) | copy-start | bytes 393220
  2.6 12.3 %copy-start.10 = (bf16[256,256]{1,0:T(8,128)(2,1)S(1)}, bf16[256,256]{1,0:T(8,128)(2,1)}, u32[]{:S(2)}) copy-start(bf16[256,256]{1,0:T(8,128)(2,1)} %constant.22.clone.columns) | copy-start | bytes 393220
  2.6 12.3 %copy-start.11 = (f32[2,64,128]{2,1,0:T(8,128)S(1)}, f32[2,64,128]{2,1,0:T(8,128)}, u32[]{:S(2)}) copy-start(f32[2,64,128]{2,1,0:T(8,128)} %constant.24.clone.twist_ref) | copy-start | bytes 196612
  14.9 14.1 %copy-start.1 = (s32[1,3,4,4096]{3,2,1,0:T(4,128)S(1)}, s32[1,3,4,4096]{3,2,1,0:T(4,128)}, u32[]{:S(2)}) copy-start(s32[1,3,4,4096]{3,2,1,0:T(4,128)} %param.15) | copy-start | bytes 589828
  14.9 14.1 %copy-start.3 = (s32[4,4096]{1,0:T(4,128)S(1)}, s32[4,4096]{1,0:T(4,128)}, u32[]{:S(2)}) copy-start(s32[4,4096]{1,0:T(4,128)} %param.14) | copy-start | bytes 196612
  14.9 14.1 %copy-start.4 = (f32[1,6,4,4096]{3,2,1,0:T(4,128)S(1)}, f32[1,6,4,4096]{3,2,1,0:T(4,128)}, u32[]{:S(2)}) copy-start(f32[1,6,4,4096]{3,2,1,0:T(4,128)} %param.16) | copy-start | bytes 1179652
  14.9 14.1 %copy-start.5 = (bf16[4,256,256]{2,1,0:T(8,128)(2,1)S(1)}, bf16[4,256,256]{2,1,0:T(8,128)(2,1)}, u32[]{:S(2)}) copy-start(bf16[4,256,256]{2,1,0:T(8,128)(2,1)} %constant.18.clone.depth_hbm.depth) | copy-start | bytes 1572868
  14.9 14.1 %copy-start.6 = (bf16[256,256]{1,0:T(8,128)(2,1)S(1)}, bf16[256,256]{1,0:T(8,128)(2,1)}, u32[]{:S(2)}) copy-start(bf16[256,256]{1,0:T(8,128)(2,1)} %constant.20.clone.rows_hbm.rows) | copy-start | bytes 393220
  16.0 13.0 %copy-start = (bf16[4,256,256]{2,1,0:T(8,128)(2,1)S(1)}, bf16[4,256,256]{2,1,0:T(8,128)(2,1)}, u32[]{:S(2)}) copy-start(bf16[4,256,256]{2,1,0:T(8,128)(2,1)} %constant.19.clone.back_depth) | copy-start | bytes 1572868
  16.0 13.0 %copy-start.2 = (bf16[256,256]{1,0:T(8,128)(2,1)S(1)}, bf16[256,256]{1,0:T(8,128)(2,1)}, u32[]{:S(2)}) copy-start(bf16[256,256]{1,0:T(8,128)(2,1)} %constant.21.clone.back_rows) | copy-start | bytes 393220

commit v11 on v9

--- a/solution.py
+++ b/solution.py
@@ -559,7 +559,7 @@
 
 
 def first_of(points):
-    return points // 2 + 1 if points > 1 else 0
+    return points // 2 + 3 if points > 4 else 0
 
 
 def exchange(array, turn=0):

time: 91.2 us -> 91.1 us (level)
  no operation moved by 1% of the time
where the time goes in v11:
time: 91.1 us; the launch traced here: 90.8 us
  blocking collectives  82.6 us (91%)
  Pallas kernels  7.29 us (8%)
    all_to_all x5, blocking collectives, exchange(): lax.all_to_all(array, 'slab', split_axis=0, concat_axis=0, tiled=True, ax...  54.4 us
    all_to_all x1, blocking collectives, on_device(): lax.all_to_all(everyone, 'rve', 0, 0, tiled=True, axis_index_groups=[turn...  28.1 us
    pallas_call x2, Pallas kernels, apply_columns(): columns(turn)  2.14 us
    pallas_call x1, Pallas kernels, on_device(): first(*(pltpu.with_memory_space_constraint(operand, pltpu.HBM) for operan...  1.91 us

profile of v11, /device:TPU:1, one launch (start us, length us, event | category | flops | bytes accessed | tf_op | source)
XLA Modules:
  0.0 90.8 jit_solution(5413363173305866187)
XLA Ops:
  0.6 1.9 %first.1 = (f32[16,40,128]{2,1,0:T(8,128)S(1)}, f32[8,128]{1,0:T(8,128)S(1)}, f32[192,128]{1,0:T(8,128)S(1)}, bf16[2,128,192]{2,1,0:T(8,128)(2,1)S(1)}) custom-call(s32[4,8]{1,0:T(4,128)} %conn_hbm.1, f32[3,20]{1,0:T(4,128)} %bitcast.27, s32[128,128]{1,0:T(8,128)} %bitcast.21, s32[384,128]{1,0:T(8,128)} %bitcast.18, f32[768,128]{1,0:T(8,128)} %bitcast.24, ...), custom_call_target="tpu_custom_call" | custom-call | flops 400000000 | bytes 2000000 | tf_op jit(solution)/shard_map/first/pallas_call | solution.py:656
  2.5 0.0 copy-start.7
  2.6 0.0 copy-start.8
  2.6 0.0 copy-start.9
  2.6 0.0 copy-start.10
  2.6 0.0 copy-start.11
  2.6 12.2 %all_to_all.30.in_ref = f32[16,40,128]{2,1,0:T(8,128)S(1)} all-to-all(f32[16,40,128]{2,1,0:T(8,128)S(1)} %get-tuple-element.17), channel_id=1, replica_groups={{10,11,12,13,14,15,0,1,2,3,4,5,6,7,8,9},{26,27,28,29,30,31,16,17,18,19,..., dimensions={0} | all-to-all | bytes 655360 | tf_op jit(solution)/shard_map/all_to_all | solution.py:567
  14.8 0.0 copy-done.7
  14.9 0.0 copy-done.8
  14.9 0.0 copy-done.9
  14.9 0.0 copy-done.10
  14.9 0.0 copy-done.11
  14.9 0.0 copy-start.1
  14.9 0.0 copy-start.3
  14.9 0.0 copy-start.4
  14.9 0.0 copy-start.5
  14.9 0.0 copy-start.6
  14.9 1.1 %columns.4 = f32[16,40,128]{2,1,0:T(8,128)S(1)} custom-call(f32[16,40,128]{2,1,0:T(8,128)S(1)} %all_to_all.30.in_ref, bf16[256,256]{1,0:T(8,128)(2,1)S(1)} %copy-done.10, bf16[256,256]{1,0:T(8,128)(2,1)S(1)} %copy-done.9, f32[2,64,128]{2,1,0:T(8,128)S(1)} %copy-done.11, bf16[256,256]{1,0:T(8,128)(2,1)S(1)} %copy-done.8, bf16[256,256]{1,0:T(8,128)(2,1)S(1)} %copy-done.7), custom_call_target="tpu_custom_call" | custom-call | flops 400000000 | bytes 2000000 | tf_op jit(solution)/shard_map/columns/pallas_call | solution.py:652
  16.0 0.0 copy-start
  16.0 0.0 copy-start.2
  16.0 13.0 %all_to_all.31.in_ref = f32[16,40,128]{2,1,0:T(8,128)S(1)} all-to-all(f32[16,40,128]{2,1,0:T(8,128)S(1)} %columns.4), channel_id=1, replica_groups=mesh['rve'=32,'slab'=16] {'slab'}, dimensions={0} | all-to-all | bytes 655360 | tf_op jit(solution)/shard_map/all_to_all | solution.py:567
  29.0 0.0 copy-done.1
  29.0 0.0 copy-done.3
  29.0 0.0 copy-done.4
  29.0 0.0 copy-done.5
  29.0 0.0 copy-done.6
  29.1 0.0 copy-done
  29.1 0.0 copy-done.2
  29.1 1.2 %middle.1 = (f32[16,40,128]{2,1,0:T(8,128)S(1)}, f32[768,128]{1,0:T(8,128)S(1)}) custom-call(f32[8,128]{1,0:T(8,128)S(1)} %get-tuple-element.16.macro_ref, s32[128,128]{1,0:T(8,128)S(1)} %bitcast.22, s32[384,128]{1,0:T(8,128)S(1)} %bitcast.19, f32[768,128]{1,0:T(8,128)S(1)} %bitcast.25, f32[16,40,128]{2,1,0:T(8,128)S(1)} %all_to_all.31.in_ref, ...), custom_call_target="tpu_custom_call" | custom-call | flops 800000000 | bytes 4000000 | tf_op jit(solution)/shard_map/middle/pallas_call | solution.py:660
  30.3 10.5 %all_to_all.32.in_ref = f32[16,40,128]{2,1,0:T(8,128)S(1)} all-to-all(f32[16,40,128]{2,1,0:T(8,128)S(1)} %get-tuple-element.19), channel_id=1, replica_groups=mesh['rve'=32,'slab'=16] {'slab'}, dimensions={0} | all-to-all | bytes 655360 | tf_op jit(solution)/shard_map/all_to_all | solution.py:567
  40.8 1.1 %columns.5 = f32[16,40,128]{2,1,0:T(8,128)S(1)} custom-call(f32[16,40,128]{2,1,0:T(8,128)S(1)} %all_to_all.32.in_ref, bf16[256,256]{1,0:T(8,128)(2,1)S(1)} %copy-done.10, bf16[256,256]{1,0:T(8,128)(2,1)S(1)} %copy-done.9, f32[2,64,128]{2,1,0:T(8,128)S(1)} %copy-done.11, bf16[256,256]{1,0:T(8,128)(2,1)S(1)} %copy-done.8, bf16[256,256]{1,0:T(8,128)(2,1)S(1)} %copy-done.7), custom_call_target="tpu_custom_call" | custom-call | flops 400000000 | bytes 2000000 | tf_op jit(solution)/shard_map/columns/pallas_call | solution.py:652
  41.8 10.5 %all_to_all.33.in_ref = f32[16,40,128]{2,1,0:T(8,128)S(1)} all-to-all(f32[16,40,128]{2,1,0:T(8,128)S(1)} %columns.5), channel_id=1, replica_groups=mesh['rve'=32,'slab'=16] {'slab'}, dimensions={0} | all-to-all | bytes 655360 | tf_op jit(solution)/shard_map/all_to_all | solution.py:567
  52.3 1.0 %last.1 = f32[16,1,128]{2,1,0:T(1,128)S(1)} custom-call(s32[128,128]{1,0:T(8,128)S(1)} %bitcast.23, s32[384,128]{1,0:T(8,128)S(1)} %bitcast.20, f32[768,128]{1,0:T(8,128)S(1)} %get-tuple-element.18.elastic_ref, f32[16,40,128]{2,1,0:T(8,128)S(1)} %all_to_all.33.in_ref, bf16[4,256,256]{2,1,0:T(8,128)(2,1)S(1)} %copy-done, bf16[256,256]{1,0:T(8,128)(2,1)S(1)} %copy-done.2), custom_call_target="tpu_custom_call" | custom-call | flops 400000000 | bytes 2000000 | tf_op jit(solution)/shard_map/last/pallas_call | solution.py:664
  53.3 8.2 %all_to_all.34.in_ref = f32[16,1,128]{2,1,0:T(1,128)S(1)} all-to-all(f32[16,1,128]{2,1,0:T(1,128)S(1)} %last.1), channel_id=1, replica_groups={{10,11,12,13,14,15,0,1,2,3,4,5,6,7,8,9},{26,27,28,29,30,31,16,17,18,19,..., dimensions={0} | all-to-all | bytes 16384 | tf_op jit(solution)/shard_map/all_to_all | solution.py:567
  61.6 28.1 %all_to_all.35.in_ref = f32[32,1,128]{2,1,0:T(1,128)S(1)} all-to-all(f32[32,1,128]{2,1,0:T(1,128)S(1)} %totals.1), channel_id=1, replica_groups={{304,320,336,352,368,384,400,416,432,448,464,480,496,0,16,32,48,64,80,9..., dimensions={0} | all-to-all | bytes 32768 | tf_op jit(solution)/shard_map/all_to_all | solution.py:667
  89.7 1.1 %assembly.1 = (f32[1,6]{1,0:T(1,128)}, f32[6,1,6]{2,1,0:T(1,128)}, f32[60,60]{1,0:T(8,128)}, f32[3,20]{1,0:T(4,128)}) custom-call(f32[192,128]{1,0:T(8,128)S(1)} %get-tuple-element.14.basis_ref, bf16[2,128,192]{2,1,0:T(8,128)(2,1)S(1)} %get-tuple-element.15.turned_ref, f32[32,1,128]{2,1,0:T(1,128)S(1)} %all_to_all.35.in_ref), custom_call_target="tpu_custom_call" | custom-call | flops 10000000 | bytes 200000 | tf_op jit(solution)/shard_map/assembly/pallas_call | solution.py:670
  (1 shorter events, 0.0 us)
Async XLA Ops:
  2.5 12.3 %copy-start.7 = (bf16[256,256]{1,0:T(8,128)(2,1)S(1)}, bf16[256,256]{1,0:T(8,128)(2,1)}, u32[]{:S(2)}) copy-start(bf16[256,256]{1,0:T(8,128)(2,1)} %constant.26.clone.back_four) | copy-start | bytes 393220
  2.6 12.3 %copy-start.8 = (bf16[256,256]{1,0:T(8,128)(2,1)S(1)}, bf16[256,256]{1,0:T(8,128)(2,1)}, u32[]{:S(2)}) copy-start(bf16[256,256]{1,0:T(8,128)(2,1)} %constant.25.clone.four) | copy-start | bytes 393220
  2.6 12.3 %copy-start.9 = (bf16[256,256]{1,0:T(8,128)(2,1)S(1)}, bf16[256,256]{1,0:T(8,128)(2,1)}, u32[]{:S(2)}) copy-start(bf16[256,256]{1,0:T(8,128)(2,1)} %constant.23.clone.back_columns) | copy-start | bytes 393220
  2.6 12.3 %copy-start.10 = (bf16[256,256]{1,0:T(8,128)(2,1)S(1)}, bf16[256,256]{1,0:T(8,128)(2,1)}, u32[]{:S(2)}) copy-start(bf16[256,256]{1,0:T(8,128)(2,1)} %constant.22.clone.columns) | copy-start | bytes 393220
  2.6 12.3 %copy-start.11 = (f32[2,64,128]{2,1,0:T(8,128)S(1)}, f32[2,64,128]{2,1,0:T(8,128)}, u32[]{:S(2)}) copy-start(f32[2,64,128]{2,1,0:T(8,128)} %constant.24.clone.twist_ref) | copy-start | bytes 196612
  14.9 14.1 %copy-start.1 = (s32[1,3,4,4096]{3,2,1,0:T(4,128)S(1)}, s32[1,3,4,4096]{3,2,1,0:T(4,128)}, u32[]{:S(2)}) copy-start(s32[1,3,4,4096]{3,2,1,0:T(4,128)} %param.15) | copy-start | bytes 589828
  14.9 14.1 %copy-start.3 = (s32[4,4096]{1,0:T(4,128)S(1)}, s32[4,4096]{1,0:T(4,128)}, u32[]{:S(2)}) copy-start(s32[4,4096]{1,0:T(4,128)} %param.14) | copy-start | bytes 196612
  14.9 14.1 %copy-start.4 = (f32[1,6,4,4096]{3,2,1,0:T(4,128)S(1)}, f32[1,6,4,4096]{3,2,1,0:T(4,128)}, u32[]{:S(2)}) copy-start(f32[1,6,4,4096]{3,2,1,0:T(4,128)} %param.16) | copy-start | bytes 1179652
  14.9 14.1 %copy-start.5 = (bf16[4,256,256]{2,1,0:T(8,128)(2,1)S(1)}, bf16[4,256,256]{2,1,0:T(8,128)(2,1)}, u32[]{:S(2)}) copy-start(bf16[4,256,256]{2,1,0:T(8,128)(2,1)} %constant.18.clone.depth_hbm.depth) | copy-start | bytes 1572868
  14.9 14.1 %copy-start.6 = (bf16[256,256]{1,0:T(8,128)(2,1)S(1)}, bf16[256,256]{1,0:T(8,128)(2,1)}, u32[]{:S(2)}) copy-start(bf16[256,256]{1,0:T(8,128)(2,1)} %constant.20.clone.rows_hbm.rows) | copy-start | bytes 393220
  16.0 13.0 %copy-start = (bf16[4,256,256]{2,1,0:T(8,128)(2,1)S(1)}, bf16[4,256,256]{2,1,0:T(8,128)(2,1)}, u32[]{:S(2)}) copy-start(bf16[4,256,256]{2,1,0:T(8,128)(2,1)} %constant.19.clone.back_depth) | copy-start | bytes 1572868
  16.0 13.0 %copy-start.2 = (bf16[256,256]{1,0:T(8,128)(2,1)S(1)}, bf16[256,256]{1,0:T(8,128)(2,1)}, u32[]{:S(2)}) copy-start(bf16[256,256]{1,0:T(8,128)(2,1)} %constant.21.clone.back_rows) | copy-start | bytes 393220
